TPU v7x, 256 devices: a whole 4x4x8 slice. The times are simulated.
256 devices in a mesh: freq: 2 (over y_hi), row: 4 (over y_lo, core), blk: 32 (over x, z).
Axes of the slice: x: 4, y: 4 (y_hi: 2, y_lo: 2; y = y_hi * 2 + y_lo), z: 8, core: 2. Of those that a mesh axis runs over, the one named last changes fastest.
Arguments:
- counts: int32 [65536, 8, 128], P(('freq', 'row', 'blk')), parts along dimension 0, may hold values from 0 to 28, as said below
- subspace: bfloat16 [65536, 32], P(('freq', 'row', 'blk')), parts along dimension 0, may hold values from -6 to 6
Outputs:
- modes: float32 [65536, 32], P(('freq', 'row', 'blk')), parts along dimension 0
There are 2 independent parts, one for each index of `freq`. A program takes and returns all parts, laid end to end along the dimension named above; each array names one. Nothing has to cross between parts.
Inputs may be any that keep to these rules, and one draw needn't show every extreme that they name: Integer spike counts.
All inputs are finite; a program needn't handle non-finite values.
Results may differ from a plain program's by a relative error of at most 0.008.
Values may be sent and summed in bfloat16 or wider, within the bound.
No kernel may reach another device: no remote copies, remote signals or barrier semaphores. Data moves between devices by JAX's collectives and lax.ppermute only.
A program may use at most 64 MiB of HBM per device.

v0:
```python
import functools

import jax
import jax.numpy as jnp
import numpy as np
from jax import lax
from jax.experimental import pallas as pl
from jax.experimental.pallas import tpu as pltpu
from jax.sharding import Mesh
from jax.sharding import PartitionSpec as P

SEGS = 8
TAPERS = 8
EPOCH_STEPS = 128
SPECTRAL_SLOT = 9
MODES = 32
DEGREES = float(SEGS * TAPERS)
COLS = SEGS * 2 * TAPERS
HALF = COLS // 2

SMALL = pltpu.CompilerParams(vmem_limit_bytes=8 << 20)
WHOLE = pltpu.CompilerParams(vmem_limit_bytes=60 * 1024 * 1024)
LARGE = pltpu.CompilerParams(vmem_limit_bytes=24 << 20)


def centred_tables():
    t = np.arange(EPOCH_STEPS, dtype=np.float64)
    k = np.arange(TAPERS, dtype=np.float64) + 1.0
    h = np.sqrt(2.0 / (EPOCH_STEPS + 1.0)) * np.sin(np.pi * (t[:, None] + 1.0) * k[None, :] / (EPOCH_STEPS + 1.0))
    turn = 2.0 * np.pi * SPECTRAL_SLOT * t / EPOCH_STEPS
    re = h * np.cos(turn)[:, None]
    im = -h * np.sin(turn)[:, None]
    re = re - re.mean(axis=0, keepdims=True)
    im = im - im.mean(axis=0, keepdims=True)
    full = np.concatenate([np.tile(re, (1, SEGS)), np.tile(im, (1, SEGS))], axis=1)
    parts = []
    rest = full
    for _ in range(3):
        part = rest.astype(jnp.bfloat16)
        parts.append(part)
        rest = rest - part.astype(np.float64)
    return np.stack(parts, axis=0)


def dot(a, b, ca, cb, precision=None):
    return lax.dot_general(
        a, b, (((ca,), (cb,)), ((), ())), precision=precision, preferred_element_type=jnp.float32
    )


CHUNKS = 4


def spectra_kernel(counts_hbm, subspace_hbm, tables_hbm, u_ref, w_ref, counts, subspace, tables, sems):
    rows = counts.shape[0]
    part = rows // CHUNKS
    copies = [pltpu.make_async_copy(tables_hbm, tables, sems.at[CHUNKS])]
    for i in range(CHUNKS):
        span = pl.ds(i * part, part)
        copies.append(pltpu.make_async_copy(counts_hbm.at[span], counts.at[span], sems.at[i]))
    copies.append(pltpu.make_async_copy(subspace_hbm, subspace, sems.at[CHUNKS + 1]))
    for copy in copies:
        copy.start()
    segment = lax.broadcasted_iota(jnp.int32, (EPOCH_STEPS, COLS), 1) % HALF // TAPERS
    copies[0].wait()
    table = [
        [jnp.where(segment == s, tables[p].astype(jnp.float32), 0.0).astype(jnp.bfloat16) for p in range(3)]
        for s in range(SEGS)
    ]
    for i in range(CHUNKS):
        copies[1 + i].wait()
        span = slice(i * part, (i + 1) * part)
        total = jnp.zeros((part, COLS), jnp.float32)
        for s in range(SEGS):
            x = counts[span, s, :].astype(jnp.float32).astype(jnp.bfloat16)
            for p in range(3):
                total = total + dot(x, table[s][p], 1, 0)
        spectra = total.astype(jnp.bfloat16).astype(jnp.float32)
        power = jnp.sum(spectra * spectra, axis=1, keepdims=True) + 1e-05
        scale = jnp.sqrt(np.float32(np.sqrt(DEGREES / (DEGREES - 1.0))) / power)
        u = (spectra * scale).astype(jnp.bfloat16)
        u_ref[span, :] = u
        w_ref[span, :] = u
    copies[-1].wait()
    for j in range(rows // 128):
        w_ref[rows + MODES * j : rows + MODES * (j + 1), :] = subspace[:, 128 * j : 128 * (j + 1)]


def twist(u):
    turned = pltpu.roll(u.astype(jnp.float32), HALF, 1)
    lane = lax.broadcasted_iota(jnp.int32, turned.shape, 1)
    return jnp.where(lane < HALF, turned, -turned).astype(jnp.bfloat16)


def image_kernel(shard, step, pieces, has_start, *refs):
    rows_ref = refs[0]
    panels = refs[1 : 1 + pieces]
    start = refs[1 + pieces] if has_start else None
    out = refs[-1]
    packed = shard + shard // 128 * MODES
    total = rows_ref.shape[0]
    for i in range(total // step):
        u = rows_ref[i * step : (i + 1) * step, :]
        t = twist(u)
        acc = start[:, i * step : (i + 1) * step] if has_start else jnp.zeros((MODES, step), jnp.float32)
        for panel in panels:
            for k in range(panel.shape[0] // packed):
                base = k * packed
                w = panel[base : base + shard, :]
                re = dot(u, w, 1, 1)
                im = dot(t, w, 1, 1)
                c = jnp.maximum(re * re + im * im - np.float32(1.0 / (DEGREES - 1.0)), 0.0).astype(jnp.bfloat16)
                st = jnp.concatenate(
                    [
                        panel[base + shard + MODES * j : base + shard + MODES * (j + 1), :]
                        for j in range(shard // 128)
                    ],
                    axis=1,
                )
                acc = acc + dot(st, c, 1, 1)
        out[:, i * step : (i + 1) * step] = acc


def image(rows, panels, shard, start=None):
    n = rows.shape[0]
    operands = (rows, *panels) + (() if start is None else (start,))
    cols = sum(p.shape[0] for p in panels) * 4 // 5
    return image_call(n, operands, cols, panels, shard, start)


def image_call(n, operands, cols, panels, shard, start):
    return pl.pallas_call(
        functools.partial(image_kernel, shard, min(1024, n), len(panels), start is not None),
        out_shape=jax.ShapeDtypeStruct((MODES, n), jnp.float32),
        compiler_params=LARGE,
        cost_estimate=pl.CostEstimate(
            flops=2 * n * cols * (2 * COLS + 4 * MODES), bytes_accessed=n * 256 + cols * 320, transcendentals=0
        ),
    )(*operands)


def split_kernel(count, *refs):
    a, b = refs[0], refs[1]
    width = a.shape[1] // count
    for k in range(count):
        refs[2 + k][...] = a[:, k * width : (k + 1) * width] + b[:, k * width : (k + 1) * width]


def add_and_split(a, b, count):
    width = a.shape[1] // count
    return pl.pallas_call(
        functools.partial(split_kernel, count),
        out_shape=[jax.ShapeDtypeStruct((a.shape[0], width), jnp.float32)] * count,
        compiler_params=SMALL,
        name="add_and_split",
    )(a, b)


def pack(g):
    return jnp.concatenate([g[8 * q : 8 * q + 8, :] for q in range(4)], axis=1)


def unpack(g):
    return jnp.concatenate([g[:, 32 * q : 32 * q + 32] for q in range(4)], axis=0)


def gram_kernel(count, *refs):
    total = refs[0][...]
    for k in range(1, count):
        total = total + refs[k][...]
    refs[count][...] = total
    refs[count + 1][...] = pack(dot(total, total, 1, 1, lax.Precision.HIGHEST))


def gram_of(parts):
    return pl.pallas_call(
        functools.partial(gram_kernel, len(parts)),
        out_shape=[
            jax.ShapeDtypeStruct(parts[0].shape, jnp.float32),
            jax.ShapeDtypeStruct((8, 128), jnp.float32),
        ],
        compiler_params=SMALL,
        name="gram",
    )(*parts)


def sum_kernel(count, copies, *refs):
    total = (refs[0][...] + refs[1][...]) + (refs[2][...] + refs[3][...])
    for k in range(copies):
        refs[count][k] = total


def sum_copies(grams, copies):
    return pl.pallas_call(
        functools.partial(sum_kernel, len(grams), copies),
        out_shape=jax.ShapeDtypeStruct((copies, 8, 128), jnp.float32),
        compiler_params=SMALL,
        name="gram_sum",
    )(*grams)


def modes_kernel(scale, grams, image_ref, out):
    g = unpack(jnp.sum(grams[...], axis=0))
    y = image_ref[...]
    row = lax.broadcasted_iota(jnp.int32, (MODES, 1), 0)
    for k in range(MODES):
        pivot = g[k : k + 1, k : k + 1]
        inv = lax.rsqrt(pivot)
        inv = inv * (1.5 - 0.5 * pivot * inv * inv)
        pivot_g = g[k : k + 1, :] * inv
        pivot_y = y[k : k + 1, :] * inv
        below = jnp.where(row > k, g[:, k : k + 1] * inv, 0.0)
        g = g - below * pivot_g
        y = jnp.where(row == k, pivot_y, y - below * pivot_y)
    out[...] = y * scale


def modes_of(grams, img, scale):
    return pl.pallas_call(
        functools.partial(modes_kernel, scale),
        out_shape=jax.ShapeDtypeStruct((MODES, img.shape[1]), jnp.float32),
        compiler_params=SMALL,
        name="modes",
    )(grams, img)


def local(sizes, counts, subspace):
    ny, nc, nx, nz = sizes
    shard = counts.shape[0]
    neurons = shard * ny * nc * nx * nz
    u, w = pl.pallas_call(
        spectra_kernel,
        out_shape=[
            jax.ShapeDtypeStruct((shard, COLS), jnp.bfloat16),
            jax.ShapeDtypeStruct((shard + shard // 128 * MODES, COLS), jnp.bfloat16),
        ],
        in_specs=[pl.BlockSpec(memory_space=pltpu.HBM)] * 3,
        scratch_shapes=[
            pltpu.VMEM(counts.shape, jnp.int32),
            pltpu.VMEM((MODES, shard), jnp.bfloat16),
            pltpu.VMEM((3, EPOCH_STEPS, COLS), jnp.bfloat16),
            pltpu.SemaphoreType.DMA((CHUNKS + 2,)),
        ],
        compiler_params=WHOLE,
        name="spectra",
    )(counts, subspace.T, jnp.asarray(centred_tables()))

    def from_x(v, k):
        return lax.ppermute(v, "x", [((i + k) % nx, i) for i in range(nx)])

    def to_x(v, k):
        return lax.ppermute(v, "x", [(i, (i + k) % nx) for i in range(nx)])

    def swap(v, axis):
        return lax.ppermute(v, axis, [(0, 1), (1, 0)])

    def both_ways(v, k):
        pairs = [(z, (z + k) % nz) for z in range(nz)] + [(nz + z, nz + (z - k) % nz) for z in range(nz)]
        return lax.ppermute(v, ("c", "z"), pairs)

    pair = jnp.concatenate([w, swap(w, "c")], axis=0)
    rows_own = jnp.concatenate([u] + [from_x(u, k) for k in range(1, nx)], axis=0)
    rows_other = swap(rows_own, "y")
    one = both_ways(pair, 1)
    three = both_ways(pair, 3)
    one_c = swap(one, "c")
    two = both_ways(one, 1)
    three_c = swap(three, "c")
    four = both_ways(three, 1)
    two_c = swap(two, "c")
    mine = image(rows_own, [pair], shard)
    mine = image(rows_own, [one, one_c], shard, start=mine)
    other = image(rows_other, [pair, one, one_c, three, three_c], shard)
    other = image(rows_other, [two, two_c, four], shard, start=other)
    mine = image(rows_own, [three, three_c, two, two_c, four], shard, start=mine)
    sums = add_and_split(mine, swap(other, "y"), nx)
    parts = [sums[0]] + [to_x(sums[k], k) for k in range(1, nx)]
    img, gram = gram_of(parts)
    quad = ("y", "c")
    four = [gram] + [lax.ppermute(gram, quad, [(i, i ^ k) for i in range(4)]) for k in (1, 2, 3)]
    grams = sum_copies(four, nx * nz)
    grams = lax.all_to_all(grams, ("x", "z"), 0, 0)
    return modes_of(grams, img, float(np.sqrt(neurons))).T


def solution(mesh):
    fine = Mesh(mesh.devices.reshape(2, 2, 2, 4, 8), ("freq", "y", "c", "x", "z"))
    every = ("freq", "y", "c", "x", "z")

    def body(counts, subspace):
        return local((2, 2, 4, 8), counts, subspace)

    return jax.shard_map(
        body,
        mesh=fine,
        in_specs=(P(every, None, None), P(every, None)),
        out_specs=P(every, None),
        check_vma=False,
    )
```

profile of v0, /device:TPU:16, one launch (start us, length us, event | category | flops | bytes accessed | tf_op | source)
XLA Modules:
  0.0 77.9 jit_solution(10615847641086614961)
XLA Ops:
  0.0 4.3 %spectra.1 = (bf16[256,128]{1,0:T(8,128)(2,1)}, bf16[320,128]{1,0:T(8,128)(2,1)}) custom-call(s32[256,8,128]{2,1,0:T(8,128)} %counts_hbm.1, bf16[32,256]{1,0:T(8,128)(2,1)} %bitcast.2, bf16[3,128,128]{2,1,0:T(8,128)(2,1)} %constant.2.clone.tables_hbm), custom_call_target="tpu_custom_call" | custom-call | tf_op jit(solution)/shard_map/spectra/pallas_call | solution.py:231
  4.3 2.8 %collective-permute-start = (bf16[256,128]{1,0:T(8,128)(2,1)}, bf16[256,128]{1,0:T(8,128)(2,1)S(1)}, u32[]{:S(2)}, u32[]{:S(2)}) collective-permute-start(bf16[256,128]{1,0:T(8,128)(2,1)} %get-tuple-element.13), channel_id=1, source_target_pairs={{8,0},{16,8},{24,16},{0,24},{9,1},{17,9},{25,17},{1,25},{10,2},{18... | collective-permute-start | bytes 196616 | tf_op jit(solution)/shard_map/ppermute | solution.py:249
  8.8 0.9 %constant_dynamic-update-slice_fusion.5 = bf16[640,128]{1,0:T(8,128)(2,1)S(1)} fusion(bf16[320,128]{1,0:T(8,128)(2,1)} %get-tuple-element.14), kind=kLoop, calls=%fused_computation.5 | loop fusion | bytes 163840
  10.3 2.0 %collective-permute-start.6 = (bf16[640,128]{1,0:T(8,128)(2,1)S(1)}, bf16[640,128]{1,0:T(8,128)(2,1)S(1)}, u32[]{:S(2)}, u32[]{:S(2)}) collective-permute-start(bf16[640,128]{1,0:T(8,128)(2,1)S(1)} %constant_dynamic-update-slice_fusion.4.refs_1_), channel_id=1, source_target_pairs={{0,1},{1,2},{2,3},{3,4},{4,5},{5,6},{6,7},{7,0},{32,39},{33,32},{3... | collective-permute-start | bytes 491528 | tf_op jit(solution)/shard_map/ppermute | solution.py:259
  13.1 5.1 %collective-permute-start.4 = (bf16[640,128]{1,0:T(8,128)(2,1)S(1)}, bf16[640,128]{1,0:T(8,128)(2,1)S(1)}, u32[]{:S(2)}, u32[]{:S(2)}) collective-permute-start(bf16[640,128]{1,0:T(8,128)(2,1)S(1)} %constant_dynamic-update-slice_fusion.4.refs_1_), channel_id=1, source_target_pairs={{0,3},{1,4},{2,5},{3,6},{4,7},{5,0},{6,1},{7,2},{32,37},{33,38},{3... | collective-permute-start | bytes 491528 | tf_op jit(solution)/shard_map/ppermute | solution.py:259
  18.3 1.4 %collective-permute-start.11 = (bf16[1024,128]{1,0:T(8,128)(2,1)S(1)}, bf16[1024,128]{1,0:T(8,128)(2,1)S(1)}, u32[]{:S(2)}, u32[]{:S(2)}) collective-permute-start(bf16[1024,128]{1,0:T(8,128)(2,1)S(1)} %constant_dynamic-update-slice_fusion.refs_0_), channel_id=1, source_target_pairs={{0,64},{64,0},{1,65},{65,1},{2,66},{66,2},{3,67},{67,3},{4,68},{68... | collective-permute-start | bytes 786440 | tf_op jit(solution)/shard_map/ppermute | solution.py:255
  19.6 2.7 %collective-permute-start.7 = (bf16[640,128]{1,0:T(8,128)(2,1)S(1)}, bf16[640,128]{1,0:T(8,128)(2,1)S(1)}, u32[]{:S(2)}, u32[]{:S(2)}) collective-permute-start(bf16[640,128]{1,0:T(8,128)(2,1)S(1)} %collective-permute-done.6.refs_1_.refs_2_), channel_id=1, source_target_pairs={{0,1},{1,2},{2,3},{3,4},{4,5},{5,6},{6,7},{7,0},{32,39},{33,32},{3... | collective-permute-start | bytes 491528 | tf_op jit(solution)/shard_map/ppermute | solution.py:259
  22.3 1.1 %collective-permute-done.4.refs_1_.refs_4_ = bf16[640,128]{1,0:T(8,128)(2,1)S(1)} collective-permute-done((bf16[640,128]{1,0:T(8,128)(2,1)S(1)}, bf16[640,128]{1,0:T(8,128)(2,1)S(1)}, u32[]{:S(2)}, u32[]{:S(2)}) %collective-permute-start.4) | collective-permute-done | bytes 163872 | tf_op jit(solution)/shard_map/ppermute | solution.py:259
  23.4 1.0 %collective-permute-start.5 = (bf16[640,128]{1,0:T(8,128)(2,1)S(1)}, bf16[640,128]{1,0:T(8,128)(2,1)S(1)}, u32[]{:S(2)}, u32[]{:S(2)}) collective-permute-start(bf16[640,128]{1,0:T(8,128)(2,1)S(1)} %collective-permute-done.4.refs_1_.refs_4_), channel_id=1, source_target_pairs={{0,32},{32,0},{1,33},{33,1},{2,34},{34,2},{3,35},{35,3},{4,36},{36... | collective-permute-start | bytes 491528 | tf_op jit(solution)/shard_map/ppermute | solution.py:255
  24.4 1.0 %shard_map.37.refs_3_ = f32[32,1024]{1,0:T(8,128)S(1)} custom-call(bf16[1024,128]{1,0:T(8,128)(2,1)S(1)} %constant_dynamic-update-slice_fusion.refs_0_, bf16[640,128]{1,0:T(8,128)(2,1)S(1)} %constant_dynamic-update-slice_fusion.4.refs_1_), custom_call_target="tpu_custom_call" | custom-call | flops 402653184 | bytes 425984 | tf_op jit(solution)/shard_map/pallas_call | solution.py:132
  25.4 3.4 %collective-permute-start.9 = (bf16[640,128]{1,0:T(8,128)(2,1)S(1)}, bf16[640,128]{1,0:T(8,128)(2,1)S(1)}, u32[]{:S(2)}, u32[]{:S(2)}) collective-permute-start(bf16[640,128]{1,0:T(8,128)(2,1)S(1)} %collective-permute-done.4.refs_1_.refs_4_), channel_id=1, source_target_pairs={{0,1},{1,2},{2,3},{3,4},{4,5},{5,6},{6,7},{7,0},{32,39},{33,32},{3... | collective-permute-start | bytes 491528 | tf_op jit(solution)/shard_map/ppermute | solution.py:259
  29.1 1.9 %shard_map.38.refs_6_ = f32[32,1024]{1,0:T(8,128)S(1)} custom-call(bf16[1024,128]{1,0:T(8,128)(2,1)S(1)} %constant_dynamic-update-slice_fusion.refs_0_, bf16[640,128]{1,0:T(8,128)(2,1)S(1)} %collective-permute-done.6.refs_1_.refs_2_, bf16[640,128]{1,0:T(8,128)(2,1)S(1)} %collective-permute-done.10.refs_2_.refs_3_, f32[32,1024]{1,0:T(8,128)S(1)} %shard_map.37.refs_3_), custom_call_target="tpu_custom_call" | custom-call | flops 805306368 | bytes 589824 | tf_op jit(solution)/shard_map/pallas_call | solution.py:132
  31.0 4.5 %shard_map.40.refs_4_ = f32[32,1024]{1,0:T(8,128)S(1)} custom-call(bf16[1024,128]{1,0:T(8,128)(2,1)S(1)} %collective-permute-done.11.refs_0_, bf16[640,128]{1,0:T(8,128)(2,1)S(1)} %constant_dynamic-update-slice_fusion.4.refs_1_, bf16[640,128]{1,0:T(8,128)(2,1)S(1)} %collective-permute-done.6.refs_1_.refs_2_, ...), custom_call_target="tpu_custom_call" | custom-call | flops 2013265920 | bytes 1081344 | tf_op jit(solution)/shard_map/pallas_call | solution.py:132
  35.4 2.7 %shard_map.41 = f32[32,1024]{1,0:T(8,128)S(1)} custom-call(bf16[1024,128]{1,0:T(8,128)(2,1)S(1)} %collective-permute-done.11.refs_0_, bf16[640,128]{1,0:T(8,128)(2,1)S(1)} %collective-permute-done.7.refs_3_.refs_1_, bf16[640,128]{1,0:T(8,128)(2,1)S(1)} %collective-permute-done.8.refs_4_.refs_2_, bf16[640,128]{1,0:T(8,128)(2,1)S(1)} %collective-permute-done.9.refs_5_.refs_3_, ...), custom_call_target="tpu_custom_call" | custom-call | flops 1207959552 | bytes 753664 | tf_op jit(solution)/shard_map/pallas_call | solution.py:132
  38.2 1.5 %collective-permute-start.12 = (f32[32,1024]{1,0:T(8,128)S(1)}, f32[32,1024]{1,0:T(8,128)S(1)}, u32[]{:S(2)}, u32[]{:S(2)}) collective-permute-start(f32[32,1024]{1,0:T(8,128)S(1)} %shard_map.41), channel_id=1, source_target_pairs={{0,64},{64,0},{1,65},{65,1},{2,66},{66,2},{3,67},{67,3},{4,68},{68... | collective-permute-start | bytes 393224 | tf_op jit(solution)/shard_map/ppermute | solution.py:255
  39.7 4.5 %shard_map.39.refs_0_ = f32[32,1024]{1,0:T(8,128)S(1)} custom-call(bf16[1024,128]{1,0:T(8,128)(2,1)S(1)} %constant_dynamic-update-slice_fusion.refs_0_, bf16[640,128]{1,0:T(8,128)(2,1)S(1)} %collective-permute-done.4.refs_1_.refs_4_, bf16[640,128]{1,0:T(8,128)(2,1)S(1)} %collective-permute-done.5.refs_2_.refs_5_, ...), custom_call_target="tpu_custom_call" | custom-call | flops 2013265920 | bytes 1081344 | tf_op jit(solution)/shard_map/pallas_call | solution.py:132
  44.2 2.0 %collective-permute-start.13 = (f32[32,256]{1,0:T(8,128)S(1)}, f32[32,256]{1,0:T(8,128)S(1)}, u32[]{:S(2)}, u32[]{:S(2)}) collective-permute-start(f32[32,256]{1,0:T(8,128)S(1)} %get-tuple-element.16), channel_id=1, source_target_pairs={{0,8},{8,16},{16,24},{24,0},{1,9},{9,17},{17,25},{25,1},{2,10},{10... | collective-permute-start | bytes 98312 | tf_op jit(solution)/shard_map/ppermute | solution.py:252
  46.2 2.6 %collective-permute-start.14 = (f32[32,256]{1,0:T(8,128)S(1)}, f32[32,256]{1,0:T(8,128)S(1)}, u32[]{:S(2)}, u32[]{:S(2)}) collective-permute-start(f32[32,256]{1,0:T(8,128)S(1)} %get-tuple-element.17), channel_id=1, source_target_pairs={{0,16},{8,24},{16,0},{24,8},{1,17},{9,25},{17,1},{25,9},{2,18},{10... | collective-permute-start | bytes 98312 | tf_op jit(solution)/shard_map/ppermute | solution.py:252
  49.4 2.2 %collective-permute-done.14.refs_2_ = f32[32,256]{1,0:T(8,128)S(1)} collective-permute-done((f32[32,256]{1,0:T(8,128)S(1)}, f32[32,256]{1,0:T(8,128)S(1)}, u32[]{:S(2)}, u32[]{:S(2)}) %collective-permute-start.14) | collective-permute-done | bytes 32800 | tf_op jit(solution)/shard_map/ppermute | solution.py:252
  51.6 1.1 %collective-permute-done.15.refs_3_ = f32[32,256]{1,0:T(8,128)S(1)} collective-permute-done((f32[32,256]{1,0:T(8,128)S(1)}, f32[32,256]{1,0:T(8,128)S(1)}, u32[]{:S(2)}, u32[]{:S(2)}) %collective-permute-start.15) | collective-permute-done | bytes 32800 | tf_op jit(solution)/shard_map/ppermute | solution.py:252
  53.0 1.4 %collective-permute-start.17 = (f32[8,128]{1,0:T(8,128)S(1)}, f32[8,128]{1,0:T(8,128)S(1)}, u32[]{:S(2)}, u32[]{:S(2)}) collective-permute-start(f32[8,128]{1,0:T(8,128)S(1)} %get-tuple-element.19.refs_0_), channel_id=1, source_target_pairs={{0,64},{32,96},{64,0},{96,32},{1,65},{33,97},{65,1},{97,33},{2,66}... | collective-permute-start | bytes 12296 | tf_op jit(solution)/shard_map/ppermute | solution.py:280
  54.8 1.8 %collective-permute-done.17.refs_2_ = f32[8,128]{1,0:T(8,128)S(1)} collective-permute-done((f32[8,128]{1,0:T(8,128)S(1)}, f32[8,128]{1,0:T(8,128)S(1)}, u32[]{:S(2)}, u32[]{:S(2)}) %collective-permute-start.17) | collective-permute-done | bytes 4128 | tf_op jit(solution)/shard_map/ppermute | solution.py:280
  57.4 17.1 %all_to_all.5.grams = f32[32,8,128]{2,1,0:T(8,128)S(1)} all-to-all(f32[32,8,128]{2,1,0:T(8,128)S(1)} %gram_sum.1), channel_id=1, replica_groups=mesh['freq'=2,'y'=2,'c'=2,'x'=4,'z'=8] {'x','z'}, dimensions={0} | all-to-all | bytes 262144 | tf_op jit(solution)/shard_map/all_to_all | solution.py:282
  74.5 3.4 %modes.1 = f32[32,256]{1,0:T(8,128)} custom-call(f32[32,8,128]{2,1,0:T(8,128)S(1)} %all_to_all.5.grams, f32[32,256]{1,0:T(8,128)S(1)} %get-tuple-element.20.image_ref), custom_call_target="tpu_custom_call" | custom-call | tf_op jit(solution)/shard_map/modes/pallas_call | solution.py:219
  (33 shorter events, 5.4 us)
Async XLA Ops:
  4.3 5.5 %collective-permute-start = (bf16[256,128]{1,0:T(8,128)(2,1)}, bf16[256,128]{1,0:T(8,128)(2,1)S(1)}, u32[]{:S(2)}, u32[]{:S(2)}) collective-permute-start(bf16[256,128]{1,0:T(8,128)(2,1)} %get-tuple-element.13), channel_id=1, source_target_pairs={{8,0},{16,8},{24,16},{0,24},{9,1},{17,9},{25,17},{1,25},{10,2},{18... | collective-permute-start | bytes 196616 | tf_op jit(solution)/shard_map/ppermute | solution.py:249
  7.1 6.0 %collective-permute-start.1 = (bf16[256,128]{1,0:T(8,128)(2,1)}, bf16[256,128]{1,0:T(8,128)(2,1)S(1)}, u32[]{:S(2)}, u32[]{:S(2)}) collective-permute-start(bf16[256,128]{1,0:T(8,128)(2,1)} %get-tuple-element.13), channel_id=1, source_target_pairs={{16,0},{24,8},{0,16},{8,24},{17,1},{25,9},{1,17},{9,25},{18,2},{26... | collective-permute-start | bytes 196616 | tf_op jit(solution)/shard_map/ppermute | solution.py:249
  7.9 10.3 %collective-permute-start.2 = (bf16[256,128]{1,0:T(8,128)(2,1)}, bf16[256,128]{1,0:T(8,128)(2,1)S(1)}, u32[]{:S(2)}, u32[]{:S(2)}) collective-permute-start(bf16[256,128]{1,0:T(8,128)(2,1)} %get-tuple-element.13), channel_id=1, source_target_pairs={{24,0},{0,8},{8,16},{16,24},{25,1},{1,9},{9,17},{17,25},{26,2},{2,... | collective-permute-start | bytes 196616 | tf_op jit(solution)/shard_map/ppermute | solution.py:249
  8.8 0.9 %copy-start = (bf16[256,128]{1,0:T(8,128)(2,1)S(1)}, bf16[256,128]{1,0:T(8,128)(2,1)}, u32[]{:S(2)}) copy-start(bf16[256,128]{1,0:T(8,128)(2,1)} %get-tuple-element.13) | copy-start | bytes 196612
  8.8 1.5 %collective-permute-start.3 = (bf16[320,128]{1,0:T(8,128)(2,1)}, bf16[320,128]{1,0:T(8,128)(2,1)S(1)}, u32[]{:S(2)}, u32[]{:S(2)}) collective-permute-start(bf16[320,128]{1,0:T(8,128)(2,1)} %get-tuple-element.14), channel_id=1, source_target_pairs={{0,32},{32,0},{1,33},{33,1},{2,34},{34,2},{3,35},{35,3},{4,36},{36... | collective-permute-start | bytes 245768 | tf_op jit(solution)/shard_map/ppermute | solution.py:255
  10.3 9.3 %collective-permute-start.6 = (bf16[640,128]{1,0:T(8,128)(2,1)S(1)}, bf16[640,128]{1,0:T(8,128)(2,1)S(1)}, u32[]{:S(2)}, u32[]{:S(2)}) collective-permute-start(bf16[640,128]{1,0:T(8,128)(2,1)S(1)} %constant_dynamic-update-slice_fusion.4.refs_1_), channel_id=1, source_target_pairs={{0,1},{1,2},{2,3},{3,4},{4,5},{5,6},{6,7},{7,0},{32,39},{33,32},{3... | collective-permute-start | bytes 491528 | tf_op jit(solution)/shard_map/ppermute | solution.py:259
  13.1 10.3 %collective-permute-start.4 = (bf16[640,128]{1,0:T(8,128)(2,1)S(1)}, bf16[640,128]{1,0:T(8,128)(2,1)S(1)}, u32[]{:S(2)}, u32[]{:S(2)}) collective-permute-start(bf16[640,128]{1,0:T(8,128)(2,1)S(1)} %constant_dynamic-update-slice_fusion.4.refs_1_), channel_id=1, source_target_pairs={{0,3},{1,4},{2,5},{3,6},{4,7},{5,0},{6,1},{7,2},{32,37},{33,38},{3... | collective-permute-start | bytes 491528 | tf_op jit(solution)/shard_map/ppermute | solution.py:259
  18.3 12.7 %collective-permute-start.11 = (bf16[1024,128]{1,0:T(8,128)(2,1)S(1)}, bf16[1024,128]{1,0:T(8,128)(2,1)S(1)}, u32[]{:S(2)}, u32[]{:S(2)}) collective-permute-start(bf16[1024,128]{1,0:T(8,128)(2,1)S(1)} %constant_dynamic-update-slice_fusion.refs_0_), channel_id=1, source_target_pairs={{0,64},{64,0},{1,65},{65,1},{2,66},{66,2},{3,67},{67,3},{4,68},{68... | collective-permute-start | bytes 786440 | tf_op jit(solution)/shard_map/ppermute | solution.py:255
  19.6 9.2 %collective-permute-start.7 = (bf16[640,128]{1,0:T(8,128)(2,1)S(1)}, bf16[640,128]{1,0:T(8,128)(2,1)S(1)}, u32[]{:S(2)}, u32[]{:S(2)}) collective-permute-start(bf16[640,128]{1,0:T(8,128)(2,1)S(1)} %collective-permute-done.6.refs_1_.refs_2_), channel_id=1, source_target_pairs={{0,1},{1,2},{2,3},{3,4},{4,5},{5,6},{6,7},{7,0},{32,39},{33,32},{3... | collective-permute-start | bytes 491528 | tf_op jit(solution)/shard_map/ppermute | solution.py:259
  22.3 6.7 %collective-permute-start.10 = (bf16[640,128]{1,0:T(8,128)(2,1)S(1)}, bf16[640,128]{1,0:T(8,128)(2,1)S(1)}, u32[]{:S(2)}, u32[]{:S(2)}) collective-permute-start(bf16[640,128]{1,0:T(8,128)(2,1)S(1)} %collective-permute-done.6.refs_1_.refs_2_), channel_id=1, source_target_pairs={{0,32},{32,0},{1,33},{33,1},{2,34},{34,2},{3,35},{35,3},{4,36},{36... | collective-permute-start | bytes 491528 | tf_op jit(solution)/shard_map/ppermute | solution.py:255
  23.4 7.5 %collective-permute-start.5 = (bf16[640,128]{1,0:T(8,128)(2,1)S(1)}, bf16[640,128]{1,0:T(8,128)(2,1)S(1)}, u32[]{:S(2)}, u32[]{:S(2)}) collective-permute-start(bf16[640,128]{1,0:T(8,128)(2,1)S(1)} %collective-permute-done.4.refs_1_.refs_4_), channel_id=1, source_target_pairs={{0,32},{32,0},{1,33},{33,1},{2,34},{34,2},{3,35},{35,3},{4,36},{36... | collective-permute-start | bytes 491528 | tf_op jit(solution)/shard_map/ppermute | solution.py:255
  25.4 10.0 %collective-permute-start.9 = (bf16[640,128]{1,0:T(8,128)(2,1)S(1)}, bf16[640,128]{1,0:T(8,128)(2,1)S(1)}, u32[]{:S(2)}, u32[]{:S(2)}) collective-permute-start(bf16[640,128]{1,0:T(8,128)(2,1)S(1)} %collective-permute-done.4.refs_1_.refs_4_), channel_id=1, source_target_pairs={{0,1},{1,2},{2,3},{3,4},{4,5},{5,6},{6,7},{7,0},{32,39},{33,32},{3... | collective-permute-start | bytes 491528 | tf_op jit(solution)/shard_map/ppermute | solution.py:259
  28.8 6.6 %collective-permute-start.8 = (bf16[640,128]{1,0:T(8,128)(2,1)S(1)}, bf16[640,128]{1,0:T(8,128)(2,1)S(1)}, u32[]{:S(2)}, u32[]{:S(2)}) collective-permute-start(bf16[640,128]{1,0:T(8,128)(2,1)S(1)} %collective-permute-done.7.refs_3_.refs_1_), channel_id=1, source_target_pairs={{0,32},{32,0},{1,33},{33,1},{2,34},{34,2},{3,35},{35,3},{4,36},{36... | collective-permute-start | bytes 491528 | tf_op jit(solution)/shard_map/ppermute | solution.py:255
  38.2 6.0 %collective-permute-start.12 = (f32[32,1024]{1,0:T(8,128)S(1)}, f32[32,1024]{1,0:T(8,128)S(1)}, u32[]{:S(2)}, u32[]{:S(2)}) collective-permute-start(f32[32,1024]{1,0:T(8,128)S(1)} %shard_map.41), channel_id=1, source_target_pairs={{0,64},{64,0},{1,65},{65,1},{2,66},{66,2},{3,67},{67,3},{4,68},{68... | collective-permute-start | bytes 393224 | tf_op jit(solution)/shard_map/ppermute | solution.py:255
  44.2 5.2 %collective-permute-start.13 = (f32[32,256]{1,0:T(8,128)S(1)}, f32[32,256]{1,0:T(8,128)S(1)}, u32[]{:S(2)}, u32[]{:S(2)}) collective-permute-start(f32[32,256]{1,0:T(8,128)S(1)} %get-tuple-element.16), channel_id=1, source_target_pairs={{0,8},{8,16},{16,24},{24,0},{1,9},{9,17},{17,25},{25,1},{2,10},{10... | collective-permute-start | bytes 98312 | tf_op jit(solution)/shard_map/ppermute | solution.py:252
  46.2 5.4 %collective-permute-start.14 = (f32[32,256]{1,0:T(8,128)S(1)}, f32[32,256]{1,0:T(8,128)S(1)}, u32[]{:S(2)}, u32[]{:S(2)}) collective-permute-start(f32[32,256]{1,0:T(8,128)S(1)} %get-tuple-element.17), channel_id=1, source_target_pairs={{0,16},{8,24},{16,0},{24,8},{1,17},{9,25},{17,1},{25,9},{2,18},{10... | collective-permute-start | bytes 98312 | tf_op jit(solution)/shard_map/ppermute | solution.py:252
  48.8 3.9 %collective-permute-start.15 = (f32[32,256]{1,0:T(8,128)S(1)}, f32[32,256]{1,0:T(8,128)S(1)}, u32[]{:S(2)}, u32[]{:S(2)}) collective-permute-start(f32[32,256]{1,0:T(8,128)S(1)} %get-tuple-element.18), channel_id=1, source_target_pairs={{0,24},{8,0},{16,8},{24,16},{1,25},{9,1},{17,9},{25,17},{2,26},{10... | collective-permute-start | bytes 98312 | tf_op jit(solution)/shard_map/ppermute | solution.py:252
  52.9 1.9 %collective-permute-start.16 = (f32[8,128]{1,0:T(8,128)S(1)}, f32[8,128]{1,0:T(8,128)S(1)}, u32[]{:S(2)}, u32[]{:S(2)}) collective-permute-start(f32[8,128]{1,0:T(8,128)S(1)} %get-tuple-element.19.refs_0_), channel_id=1, source_target_pairs={{0,32},{32,0},{64,96},{96,64},{1,33},{33,1},{65,97},{97,65},{2,34}... | collective-permute-start | bytes 12296 | tf_op jit(solution)/shard_map/ppermute | solution.py:280
  53.0 3.7 %collective-permute-start.17 = (f32[8,128]{1,0:T(8,128)S(1)}, f32[8,128]{1,0:T(8,128)S(1)}, u32[]{:S(2)}, u32[]{:S(2)}) collective-permute-start(f32[8,128]{1,0:T(8,128)S(1)} %get-tuple-element.19.refs_0_), channel_id=1, source_target_pairs={{0,64},{32,96},{64,0},{96,32},{1,65},{33,97},{65,1},{97,33},{2,66}... | collective-permute-start | bytes 12296 | tf_op jit(solution)/shard_map/ppermute | solution.py:280
  54.4 3.0 %collective-permute-start.18 = (f32[8,128]{1,0:T(8,128)S(1)}, f32[8,128]{1,0:T(8,128)S(1)}, u32[]{:S(2)}, u32[]{:S(2)}) collective-permute-start(f32[8,128]{1,0:T(8,128)S(1)} %get-tuple-element.19.refs_0_), channel_id=1, source_target_pairs={{0,96},{32,64},{64,32},{96,0},{1,97},{33,65},{65,33},{97,1},{2,98}... | collective-permute-start | bytes 12296 | tf_op jit(solution)/shard_map/ppermute | solution.py:280
where the time goes:
time: 78.1 us; the launch traced here: 77.9 us
  starting transfers between devices  28.5 us (36%)
  Pallas kernels  22.5 us (29%)
  blocking collectives  17.1 us (22%)
  waiting for transfers between devices  8.75 us (11%)
  local copies, waits for them, and re-layouts  0.99 us (1%)
    all_to_all x1, blocking collectives, local(): grams = lax.all_to_all(grams, ('x', 'z'), 0, 0)  17.1 us
    pallas_call x5, Pallas kernels, image_call(): pl.pallas_call(functools.partial(image_kernel, shard, min(1024, n), len(p...  14.5 us
    ppermute x4, starting transfers between devices, both_ways(): return lax.ppermute(v, ('c', 'z'), pairs)  13.2 us
    ppermute x3, starting transfers between devices, to_x(): return lax.ppermute(v, 'x', [(i, (i + k) % nx) for i in range(nx)])  4.74 us
    ppermute x3, starting transfers between devices, from_x(): return lax.ppermute(v, 'x', [((i + k) % nx, i) for i in range(nx)])  4.52 us
    pallas_call x1, Pallas kernels, local(): pl.pallas_call(spectra_kernel, out_shape=[jax.ShapeDtypeStruct((shard, CO...  4.27 us
    ppermute x6, starting transfers between devices, swap(): return lax.ppermute(v, axis, [(0, 1), (1, 0)])  4.12 us
    ppermute x3, waiting for transfers between devices, to_x(): return lax.ppermute(v, 'x', [(i, (i + k) % nx) for i in range(nx)])  3.75 us
  transfers between devices with their start and end apart: 19, of which 8 were waited for; matrix products, arithmetic and copies ran while one was open for 1% of the time, Pallas kernels for 15%

commit v1 on v0

--- a/solution.py
+++ b/solution.py
@@ -19,7 +19,6 @@
 HALF = COLS // 2
 
 SMALL = pltpu.CompilerParams(vmem_limit_bytes=8 << 20)
-WHOLE = pltpu.CompilerParams(vmem_limit_bytes=60 * 1024 * 1024)
 LARGE = pltpu.CompilerParams(vmem_limit_bytes=24 << 20)
 
 
@@ -92,17 +91,16 @@
     return jnp.where(lane < HALF, turned, -turned).astype(jnp.bfloat16)
 
 
-def image_kernel(shard, step, pieces, has_start, *refs):
-    rows_ref = refs[0]
-    panels = refs[1 : 1 + pieces]
-    start = refs[1 + pieces] if has_start else None
-    out = refs[-1]
+def image_kernel(shard, halves, blocks, pieces, has_start, *refs):
+    rows = refs[:blocks]
+    panels = refs[blocks : blocks + pieces]
+    starts = refs[blocks + pieces : blocks + pieces + len(halves)] if has_start else ()
+    outs = refs[-len(halves) :]
     packed = shard + shard // 128 * MODES
-    total = rows_ref.shape[0]
-    for i in range(total // step):
-        u = rows_ref[i * step : (i + 1) * step, :]
+    for h, half in enumerate(halves):
+        u = jnp.concatenate([r[half * shard : (half + 1) * shard, :] for r in rows], axis=0)
         t = twist(u)
-        acc = start[:, i * step : (i + 1) * step] if has_start else jnp.zeros((MODES, step), jnp.float32)
+        acc = starts[h][...] if has_start else jnp.zeros((MODES, blocks * shard), jnp.float32)
         for panel in panels:
             for k in range(panel.shape[0] // packed):
                 base = k * packed
@@ -118,25 +116,22 @@
                     axis=1,
                 )
                 acc = acc + dot(st, c, 1, 1)
-        out[:, i * step : (i + 1) * step] = acc
-
-
-def image(rows, panels, shard, start=None):
-    n = rows.shape[0]
-    operands = (rows, *panels) + (() if start is None else (start,))
+        outs[h][...] = acc
+
+
+def image(rows, halves, panels, shard, starts=()):
+    n = len(rows) * shard
     cols = sum(p.shape[0] for p in panels) * 4 // 5
-    return image_call(n, operands, cols, panels, shard, start)
-
-
-def image_call(n, operands, cols, panels, shard, start):
-    return pl.pallas_call(
-        functools.partial(image_kernel, shard, min(1024, n), len(panels), start is not None),
-        out_shape=jax.ShapeDtypeStruct((MODES, n), jnp.float32),
+    return pl.pallas_call(
+        functools.partial(image_kernel, shard, halves, len(rows), len(panels), len(starts) > 0),
+        out_shape=[jax.ShapeDtypeStruct((MODES, n), jnp.float32)] * len(halves),
         compiler_params=LARGE,
         cost_estimate=pl.CostEstimate(
-            flops=2 * n * cols * (2 * COLS + 4 * MODES), bytes_accessed=n * 256 + cols * 320, transcendentals=0
+            flops=2 * n * len(halves) * cols * (2 * COLS + 4 * MODES),
+            bytes_accessed=n * 256 + cols * 320,
+            transcendentals=0,
         ),
-    )(*operands)
+    )(*rows, *panels, *starts)
 
 
 def split_kernel(count, *refs):
@@ -241,9 +236,9 @@
             pltpu.VMEM((3, EPOCH_STEPS, COLS), jnp.bfloat16),
             pltpu.SemaphoreType.DMA((CHUNKS + 2,)),
         ],
-        compiler_params=WHOLE,
+        compiler_params=LARGE,
         name="spectra",
-    )(counts, subspace.T, jnp.asarray(centred_tables()))
+    )(*(pltpu.with_memory_space_constraint(v, pltpu.HBM) for v in (counts, subspace.T, jnp.asarray(centred_tables()))))
 
     def from_x(v, k):
         return lax.ppermute(v, "x", [((i + k) % nx, i) for i in range(nx)])
@@ -258,22 +253,21 @@
         pairs = [(z, (z + k) % nz) for z in range(nz)] + [(nz + z, nz + (z - k) % nz) for z in range(nz)]
         return lax.ppermute(v, ("c", "z"), pairs)
 
+    first = jnp.concatenate([u, swap(u, "y")], axis=0)
     pair = jnp.concatenate([w, swap(w, "c")], axis=0)
-    rows_own = jnp.concatenate([u] + [from_x(u, k) for k in range(1, nx)], axis=0)
-    rows_other = swap(rows_own, "y")
     one = both_ways(pair, 1)
-    three = both_ways(pair, 3)
+    two = both_ways(pair, 2)
+    rows = [first] + [from_x(first, k) for k in range(1, nx)]
     one_c = swap(one, "c")
-    two = both_ways(one, 1)
-    three_c = swap(three, "c")
-    four = both_ways(three, 1)
     two_c = swap(two, "c")
-    mine = image(rows_own, [pair], shard)
-    mine = image(rows_own, [one, one_c], shard, start=mine)
-    other = image(rows_other, [pair, one, one_c, three, three_c], shard)
-    other = image(rows_other, [two, two_c, four], shard, start=other)
-    mine = image(rows_own, [three, three_c, two, two_c, four], shard, start=mine)
-    sums = add_and_split(mine, swap(other, "y"), nx)
+    far = both_ways(jnp.concatenate([one, two], axis=0), 2)
+    far_c = swap(far[: pair.shape[0]], "c")
+    own, other = image(rows, (0, 1), [pair, one, one_c], shard)
+    (other,) = image(rows, (1,), [two, two_c], shard, (other,))
+    (own,) = image(rows, (0,), [two, two_c], shard, (own,))
+    (other,) = image(rows, (1,), [far, far_c], shard, (other,))
+    (own,) = image(rows, (0,), [far, far_c], shard, (own,))
+    sums = add_and_split(own, swap(other, "y"), nx)
     parts = [sums[0]] + [to_x(sums[k], k) for k in range(1, nx)]
     img, gram = gram_of(parts)
     quad = ("y", "c")

time: 78.1 us -> 81.1 us (1.038)
  waiting for transfers between devices: 8.75 us -> 16.1 us
  starting transfers between devices: 28.5 us -> 24.4 us
  blocking collectives: 17.1 us -> 18.4 us
  local copies, waits for them, and re-layouts: 0.99 us -> 0.05 us
    ppermute x4 -> x3, waiting for transfers between devices: 1.11 us -> 10.5 us  [both_ways(): return lax.ppermute(v, ('c', 'z'), pairs)]
    ppermute x4 -> x3, starting transfers between devices: 13.2 us -> 6.46 us  [both_ways(): return lax.ppermute(v, ('c', 'z'), pairs)]
    all_to_all x1, blocking collectives: 17.1 us -> 18.4 us  [local(): grams = lax.all_to_all(grams, ('x', 'z'), 0, 0)]
    ppermute x3, waiting for transfers between devices: 3.75 us -> 2.48 us  [to_x(): return lax.ppermute(v, 'x', [(i, (i + k) % nx) for i in range(nx)])]
    ppermute x3, starting transfers between devices: 4.52 us -> 5.73 us  [from_x(): return lax.ppermute(v, 'x', [((i + k) % nx, i) for i in range(nx)])]
    ppermute x3, starting transfers between devices: 4.74 us -> 5.73 us  [to_x(): return lax.ppermute(v, 'x', [(i, (i + k) % nx) for i in range(nx)])]
    unnamed x6 -> x2, local copies, waits for them, and re-layouts: 0.96 us -> 0.01 us
  transfers between devices with their start and end apart: 19 -> 18, of which waited for: 8 -> 8; matrix products, arithmetic and copies ran while one was open for 1% -> 0% of each run, Pallas kernels for 15% -> 15%
where the time goes in v1:
time: 81.1 us; the launch traced here: 81 us
  starting transfers between devices  24.4 us (30%)
  Pallas kernels  21.9 us (27%)
  blocking collectives  18.4 us (23%)
  waiting for transfers between devices  16.1 us (20%)
    all_to_all x1, blocking collectives, local(): grams = lax.all_to_all(grams, ('x', 'z'), 0, 0)  18.4 us
    pallas_call x5, Pallas kernels, image(): pl.pallas_call(functools.partial(image_kernel, shard, halves, len(rows),...  14.6 us
    ppermute x3, waiting for transfers between devices, both_ways(): return lax.ppermute(v, ('c', 'z'), pairs)  10.5 us
    ppermute x3, starting transfers between devices, both_ways(): return lax.ppermute(v, ('c', 'z'), pairs)  6.46 us
    ppermute x3, starting transfers between devices, from_x(): return lax.ppermute(v, 'x', [((i + k) % nx, i) for i in range(nx)])  5.73 us
    ppermute x3, starting transfers between devices, to_x(): return lax.ppermute(v, 'x', [(i, (i + k) % nx) for i in range(nx)])  5.73 us
    ppermute x6, starting transfers between devices, swap(): return lax.ppermute(v, axis, [(0, 1), (1, 0)])  4.55 us
    pallas_call x1, Pallas kernels, local(): pl.pallas_call(spectra_kernel, out_shape=[jax.ShapeDtypeStruct((shard, CO...  3.62 us
  transfers between devices with their start and end apart: 18, of which 8 were waited for; matrix products, arithmetic and copies ran while one was open for 0% of the time, Pallas kernels for 15%

profile of v1, /device:TPU:16, one launch (start us, length us, event | category | flops | bytes accessed | tf_op | source)
XLA Modules:
  0.0 81.0 jit_solution(11901529316592397914)
XLA Ops:
  0.0 3.6 %spectra.1 = (bf16[256,128]{1,0:T(8,128)(2,1)S(1)}, bf16[320,128]{1,0:T(8,128)(2,1)S(1)}) custom-call(s32[256,8,128]{2,1,0:T(8,128)} %counts_hbm.1, bf16[32,256]{1,0:T(8,128)(2,1)} %bitcast.2, bf16[3,128,128]{2,1,0:T(8,128)(2,1)} %constant.2.clone.tables_hbm), custom_call_target="tpu_custom_call" | custom-call | tf_op jit(solution)/shard_map/spectra/pallas_call | solution.py:226
  3.7 1.2 %collective-permute-done.4 = bf16[320,128]{1,0:T(8,128)(2,1)S(1)} collective-permute-done((bf16[320,128]{1,0:T(8,128)(2,1)S(1)}, bf16[320,128]{1,0:T(8,128)(2,1)S(1)}, u32[]{:S(2)}, u32[]{:S(2)}) %collective-permute-start.4) | collective-permute-done | bytes 81952 | tf_op jit(solution)/shard_map/ppermute | solution.py:250
  5.0 3.3 %collective-permute-start.6 = (bf16[640,128]{1,0:T(8,128)(2,1)S(1)}, bf16[640,128]{1,0:T(8,128)(2,1)S(1)}, u32[]{:S(2)}, u32[]{:S(2)}) collective-permute-start(bf16[640,128]{1,0:T(8,128)(2,1)S(1)} %constant_dynamic-update-slice_fusion.2.refs_4_), channel_id=1, source_target_pairs={{0,2},{1,3},{2,4},{3,5},{4,6},{5,7},{6,0},{7,1},{32,38},{33,39},{3... | collective-permute-start | bytes 491528 | tf_op jit(solution)/shard_map/ppermute | solution.py:254
  8.4 1.9 %collective-permute-start.5 = (bf16[640,128]{1,0:T(8,128)(2,1)S(1)}, bf16[640,128]{1,0:T(8,128)(2,1)S(1)}, u32[]{:S(2)}, u32[]{:S(2)}) collective-permute-start(bf16[640,128]{1,0:T(8,128)(2,1)S(1)} %constant_dynamic-update-slice_fusion.2.refs_4_), channel_id=1, source_target_pairs={{0,1},{1,2},{2,3},{3,4},{4,5},{5,6},{6,7},{7,0},{32,39},{33,32},{3... | collective-permute-start | bytes 491528 | tf_op jit(solution)/shard_map/ppermute | solution.py:254
  10.3 1.3 %collective-permute-start = (bf16[256,128]{1,0:T(8,128)(2,1)S(1)}, bf16[256,128]{1,0:T(8,128)(2,1)S(1)}, u32[]{:S(2)}, u32[]{:S(2)}) collective-permute-start(bf16[256,128]{1,0:T(8,128)(2,1)S(1)} %get-tuple-element.15), channel_id=1, source_target_pairs={{0,64},{64,0},{1,65},{65,1},{2,66},{66,2},{3,67},{67,3},{4,68},{68... | collective-permute-start | bytes 196616 | tf_op jit(solution)/shard_map/ppermute | solution.py:250
  11.6 3.2 %collective-permute-done.6.refs_4_ = bf16[640,128]{1,0:T(8,128)(2,1)S(1)} collective-permute-done((bf16[640,128]{1,0:T(8,128)(2,1)S(1)}, bf16[640,128]{1,0:T(8,128)(2,1)S(1)}, u32[]{:S(2)}, u32[]{:S(2)}) %collective-permute-start.6) | collective-permute-done | bytes 163872 | tf_op jit(solution)/shard_map/ppermute | solution.py:254
  14.8 3.0 %collective-permute-done.5.refs_5_ = bf16[640,128]{1,0:T(8,128)(2,1)S(1)} collective-permute-done((bf16[640,128]{1,0:T(8,128)(2,1)S(1)}, bf16[640,128]{1,0:T(8,128)(2,1)S(1)}, u32[]{:S(2)}, u32[]{:S(2)}) %collective-permute-start.5) | collective-permute-done | bytes 163872 | tf_op jit(solution)/shard_map/ppermute | solution.py:254
  19.9 1.6 %collective-permute-start.3 = (bf16[512,128]{1,0:T(8,128)(2,1)S(1)}, bf16[512,128]{1,0:T(8,128)(2,1)S(1)}, u32[]{:S(2)}, u32[]{:S(2)}) collective-permute-start(bf16[512,128]{1,0:T(8,128)(2,1)S(1)} %constant_dynamic-update-slice_fusion.refs_0_), channel_id=1, source_target_pairs={{24,0},{0,8},{8,16},{16,24},{25,1},{1,9},{9,17},{17,25},{26,2},{2,... | collective-permute-start | bytes 393224 | tf_op jit(solution)/shard_map/ppermute | solution.py:244
  21.4 2.7 %collective-permute-start.2 = (bf16[512,128]{1,0:T(8,128)(2,1)S(1)}, bf16[512,128]{1,0:T(8,128)(2,1)S(1)}, u32[]{:S(2)}, u32[]{:S(2)}) collective-permute-start(bf16[512,128]{1,0:T(8,128)(2,1)S(1)} %constant_dynamic-update-slice_fusion.refs_0_), channel_id=1, source_target_pairs={{16,0},{24,8},{0,16},{8,24},{17,1},{25,9},{1,17},{9,25},{18,2},{26... | collective-permute-start | bytes 393224 | tf_op jit(solution)/shard_map/ppermute | solution.py:244
  24.2 1.4 %collective-permute-start.1 = (bf16[512,128]{1,0:T(8,128)(2,1)S(1)}, bf16[512,128]{1,0:T(8,128)(2,1)S(1)}, u32[]{:S(2)}, u32[]{:S(2)}) collective-permute-start(bf16[512,128]{1,0:T(8,128)(2,1)S(1)} %constant_dynamic-update-slice_fusion.refs_0_), channel_id=1, source_target_pairs={{8,0},{16,8},{24,16},{0,24},{9,1},{17,9},{25,17},{1,25},{10,2},{18... | collective-permute-start | bytes 393224 | tf_op jit(solution)/shard_map/ppermute | solution.py:244
  25.6 4.4 %collective-permute-done.7.refs_4_ = bf16[1280,128]{1,0:T(8,128)(2,1)S(1)} collective-permute-done((bf16[1280,128]{1,0:T(8,128)(2,1)S(1)}, bf16[1280,128]{1,0:T(8,128)(2,1)S(1)}, u32[]{:S(2)}, u32[]{:S(2)}) %collective-permute-start.7) | collective-permute-done | bytes 327712 | tf_op jit(solution)/shard_map/ppermute | solution.py:254
  30.8 5.3 %shard_map.37 = (f32[32,1024]{1,0:T(8,128)S(1)}, f32[32,1024]{1,0:T(8,128)S(1)}) custom-call(bf16[512,128]{1,0:T(8,128)(2,1)S(1)} %constant_dynamic-update-slice_fusion.refs_0_, bf16[512,128]{1,0:T(8,128)(2,1)S(1)} %collective-permute-done.1.refs_1_, bf16[512,128]{1,0:T(8,128)(2,1)S(1)} %collective-permute-done.2.refs_2_, ...), custom_call_target="tpu_custom_call" | custom-call | flops 2415919104 | bytes 753664 | tf_op jit(solution)/shard_map/pallas_call | solution.py:125
  36.1 1.9 %shard_map.40.refs_6_ = f32[32,1024]{1,0:T(8,128)S(1)} custom-call(bf16[512,128]{1,0:T(8,128)(2,1)S(1)} %constant_dynamic-update-slice_fusion.refs_0_, bf16[512,128]{1,0:T(8,128)(2,1)S(1)} %collective-permute-done.1.refs_1_, bf16[512,128]{1,0:T(8,128)(2,1)S(1)} %collective-permute-done.2.refs_2_, bf16[512,128]{1,0:T(8,128)(2,1)S(1)} %collective-permute-done.3.refs_3_, ...), custom_call_target="tpu_custom_call" | custom-call | flops 805306368 | bytes 589824 | tf_op jit(solution)/shard_map/pallas_call | solution.py:125
  38.0 2.7 %shard_map.41 = f32[32,1024]{1,0:T(8,128)S(1)} custom-call(bf16[512,128]{1,0:T(8,128)(2,1)S(1)} %constant_dynamic-update-slice_fusion.refs_0_, bf16[512,128]{1,0:T(8,128)(2,1)S(1)} %collective-permute-done.1.refs_1_, bf16[512,128]{1,0:T(8,128)(2,1)S(1)} %collective-permute-done.2.refs_2_, bf16[512,128]{1,0:T(8,128)(2,1)S(1)} %collective-permute-done.3.refs_3_, ...), custom_call_target="tpu_custom_call" | custom-call | flops 1207959552 | bytes 753664 | tf_op jit(solution)/shard_map/pallas_call | solution.py:125
  40.7 1.5 %collective-permute-start.11 = (f32[32,1024]{1,0:T(8,128)S(1)}, f32[32,1024]{1,0:T(8,128)S(1)}, u32[]{:S(2)}, u32[]{:S(2)}) collective-permute-start(f32[32,1024]{1,0:T(8,128)S(1)} %shard_map.41), channel_id=1, source_target_pairs={{0,64},{64,0},{1,65},{65,1},{2,66},{66,2},{3,67},{67,3},{4,68},{68... | collective-permute-start | bytes 393224 | tf_op jit(solution)/shard_map/ppermute | solution.py:250
  42.3 1.9 %shard_map.38.refs_6_ = f32[32,1024]{1,0:T(8,128)S(1)} custom-call(bf16[512,128]{1,0:T(8,128)(2,1)S(1)} %constant_dynamic-update-slice_fusion.refs_0_, bf16[512,128]{1,0:T(8,128)(2,1)S(1)} %collective-permute-done.1.refs_1_, bf16[512,128]{1,0:T(8,128)(2,1)S(1)} %collective-permute-done.2.refs_2_, bf16[512,128]{1,0:T(8,128)(2,1)S(1)} %collective-permute-done.3.refs_3_, ...), custom_call_target="tpu_custom_call" | custom-call | flops 805306368 | bytes 589824 | tf_op jit(solution)/shard_map/pallas_call | solution.py:125
  44.1 2.8 %shard_map.39.refs_0_ = f32[32,1024]{1,0:T(8,128)S(1)} custom-call(bf16[512,128]{1,0:T(8,128)(2,1)S(1)} %constant_dynamic-update-slice_fusion.refs_0_, bf16[512,128]{1,0:T(8,128)(2,1)S(1)} %collective-permute-done.1.refs_1_, bf16[512,128]{1,0:T(8,128)(2,1)S(1)} %collective-permute-done.2.refs_2_, bf16[512,128]{1,0:T(8,128)(2,1)S(1)} %collective-permute-done.3.refs_3_, ...), custom_call_target="tpu_custom_call" | custom-call | flops 1207959552 | bytes 753664 | tf_op jit(solution)/shard_map/pallas_call | solution.py:125
  46.9 1.6 %collective-permute-start.12 = (f32[32,256]{1,0:T(8,128)S(1)}, f32[32,256]{1,0:T(8,128)S(1)}, u32[]{:S(2)}, u32[]{:S(2)}) collective-permute-start(f32[32,256]{1,0:T(8,128)S(1)} %get-tuple-element.20), channel_id=1, source_target_pairs={{0,8},{8,16},{16,24},{24,0},{1,9},{9,17},{17,25},{25,1},{2,10},{10... | collective-permute-start | bytes 98312 | tf_op jit(solution)/shard_map/ppermute | solution.py:247
  48.5 2.7 %collective-permute-start.13 = (f32[32,256]{1,0:T(8,128)S(1)}, f32[32,256]{1,0:T(8,128)S(1)}, u32[]{:S(2)}, u32[]{:S(2)}) collective-permute-start(f32[32,256]{1,0:T(8,128)S(1)} %get-tuple-element.21), channel_id=1, source_target_pairs={{0,16},{8,24},{16,0},{24,8},{1,17},{9,25},{17,1},{25,9},{2,18},{10... | collective-permute-start | bytes 98312 | tf_op jit(solution)/shard_map/ppermute | solution.py:247
  51.2 1.4 %collective-permute-start.14 = (f32[32,256]{1,0:T(8,128)S(1)}, f32[32,256]{1,0:T(8,128)S(1)}, u32[]{:S(2)}, u32[]{:S(2)}) collective-permute-start(f32[32,256]{1,0:T(8,128)S(1)} %get-tuple-element.22), channel_id=1, source_target_pairs={{0,24},{8,0},{16,8},{24,16},{1,25},{9,1},{17,9},{25,17},{2,26},{10... | collective-permute-start | bytes 98312 | tf_op jit(solution)/shard_map/ppermute | solution.py:247
  52.7 1.3 %collective-permute-done.13.refs_2_ = f32[32,256]{1,0:T(8,128)S(1)} collective-permute-done((f32[32,256]{1,0:T(8,128)S(1)}, f32[32,256]{1,0:T(8,128)S(1)}, u32[]{:S(2)}, u32[]{:S(2)}) %collective-permute-start.13) | collective-permute-done | bytes 32800 | tf_op jit(solution)/shard_map/ppermute | solution.py:247
  53.9 1.2 %collective-permute-done.14.refs_3_ = f32[32,256]{1,0:T(8,128)S(1)} collective-permute-done((f32[32,256]{1,0:T(8,128)S(1)}, f32[32,256]{1,0:T(8,128)S(1)}, u32[]{:S(2)}, u32[]{:S(2)}) %collective-permute-start.14) | collective-permute-done | bytes 32800 | tf_op jit(solution)/shard_map/ppermute | solution.py:247
  59.1 18.4 %all_to_all.5.grams = f32[32,8,128]{2,1,0:T(8,128)S(1)} all-to-all(f32[32,8,128]{2,1,0:T(8,128)S(1)} %gram_sum.1), channel_id=1, replica_groups=mesh['freq'=2,'y'=2,'c'=2,'x'=4,'z'=8] {'x','z'}, dimensions={0} | all-to-all | bytes 262144 | tf_op jit(solution)/shard_map/all_to_all | solution.py:276
  77.5 3.4 %modes.1 = f32[32,256]{1,0:T(8,128)} custom-call(f32[32,8,128]{2,1,0:T(8,128)S(1)} %all_to_all.5.grams, f32[32,256]{1,0:T(8,128)S(1)} %get-tuple-element.24.image_ref), custom_call_target="tpu_custom_call" | custom-call | tf_op jit(solution)/shard_map/modes/pallas_call | solution.py:214
  (29 shorter events, 7.0 us)
Async XLA Ops:
  3.6 1.4 %collective-permute-start.4 = (bf16[320,128]{1,0:T(8,128)(2,1)S(1)}, bf16[320,128]{1,0:T(8,128)(2,1)S(1)}, u32[]{:S(2)}, u32[]{:S(2)}) collective-permute-start(bf16[320,128]{1,0:T(8,128)(2,1)S(1)} %get-tuple-element.16), channel_id=1, source_target_pairs={{0,32},{32,0},{1,33},{33,1},{2,34},{34,2},{3,35},{35,3},{4,36},{36... | collective-permute-start | bytes 245768 | tf_op jit(solution)/shard_map/ppermute | solution.py:250
  5.0 9.8 %collective-permute-start.6 = (bf16[640,128]{1,0:T(8,128)(2,1)S(1)}, bf16[640,128]{1,0:T(8,128)(2,1)S(1)}, u32[]{:S(2)}, u32[]{:S(2)}) collective-permute-start(bf16[640,128]{1,0:T(8,128)(2,1)S(1)} %constant_dynamic-update-slice_fusion.2.refs_4_), channel_id=1, source_target_pairs={{0,2},{1,3},{2,4},{3,5},{4,6},{5,7},{6,0},{7,1},{32,38},{33,39},{3... | collective-permute-start | bytes 491528 | tf_op jit(solution)/shard_map/ppermute | solution.py:254
  8.4 9.4 %collective-permute-start.5 = (bf16[640,128]{1,0:T(8,128)(2,1)S(1)}, bf16[640,128]{1,0:T(8,128)(2,1)S(1)}, u32[]{:S(2)}, u32[]{:S(2)}) collective-permute-start(bf16[640,128]{1,0:T(8,128)(2,1)S(1)} %constant_dynamic-update-slice_fusion.2.refs_4_), channel_id=1, source_target_pairs={{0,1},{1,2},{2,3},{3,4},{4,5},{5,6},{6,7},{7,0},{32,39},{33,32},{3... | collective-permute-start | bytes 491528 | tf_op jit(solution)/shard_map/ppermute | solution.py:254
  10.3 9.6 %collective-permute-start = (bf16[256,128]{1,0:T(8,128)(2,1)S(1)}, bf16[256,128]{1,0:T(8,128)(2,1)S(1)}, u32[]{:S(2)}, u32[]{:S(2)}) collective-permute-start(bf16[256,128]{1,0:T(8,128)(2,1)S(1)} %get-tuple-element.15), channel_id=1, source_target_pairs={{0,64},{64,0},{1,65},{65,1},{2,66},{66,2},{3,67},{67,3},{4,68},{68... | collective-permute-start | bytes 196616 | tf_op jit(solution)/shard_map/ppermute | solution.py:250
  17.8 12.2 %collective-permute-start.7 = (bf16[1280,128]{1,0:T(8,128)(2,1)S(1)}, bf16[1280,128]{1,0:T(8,128)(2,1)S(1)}, u32[]{:S(2)}, u32[]{:S(2)}) collective-permute-start(bf16[1280,128]{1,0:T(8,128)(2,1)S(1)} %pad_maximum_fusion), channel_id=1, source_target_pairs={{0,2},{1,3},{2,4},{3,5},{4,6},{5,7},{6,0},{7,1},{32,38},{33,39},{3... | collective-permute-start | bytes 983048 | tf_op jit(solution)/shard_map/ppermute | solution.py:254
  19.0 11.8 %collective-permute-start.10 = (bf16[640,128]{1,0:T(8,128)(2,1)S(1)}, bf16[640,128]{1,0:T(8,128)(2,1)S(1)}, u32[]{:S(2)}, u32[]{:S(2)}) collective-permute-start(bf16[640,128]{1,0:T(8,128)(2,1)S(1)} %collective-permute-done.5.refs_5_), channel_id=1, source_target_pairs={{0,32},{32,0},{1,33},{33,1},{2,34},{34,2},{3,35},{35,3},{4,36},{36... | collective-permute-start | bytes 491528 | tf_op jit(solution)/shard_map/ppermute | solution.py:250
  19.9 10.1 %collective-permute-start.3 = (bf16[512,128]{1,0:T(8,128)(2,1)S(1)}, bf16[512,128]{1,0:T(8,128)(2,1)S(1)}, u32[]{:S(2)}, u32[]{:S(2)}) collective-permute-start(bf16[512,128]{1,0:T(8,128)(2,1)S(1)} %constant_dynamic-update-slice_fusion.refs_0_), channel_id=1, source_target_pairs={{24,0},{0,8},{8,16},{16,24},{25,1},{1,9},{9,17},{17,25},{26,2},{2,... | collective-permute-start | bytes 393224 | tf_op jit(solution)/shard_map/ppermute | solution.py:244
  21.4 9.3 %collective-permute-start.2 = (bf16[512,128]{1,0:T(8,128)(2,1)S(1)}, bf16[512,128]{1,0:T(8,128)(2,1)S(1)}, u32[]{:S(2)}, u32[]{:S(2)}) collective-permute-start(bf16[512,128]{1,0:T(8,128)(2,1)S(1)} %constant_dynamic-update-slice_fusion.refs_0_), channel_id=1, source_target_pairs={{16,0},{24,8},{0,16},{8,24},{17,1},{25,9},{1,17},{9,25},{18,2},{26... | collective-permute-start | bytes 393224 | tf_op jit(solution)/shard_map/ppermute | solution.py:244
  24.2 6.6 %collective-permute-start.1 = (bf16[512,128]{1,0:T(8,128)(2,1)S(1)}, bf16[512,128]{1,0:T(8,128)(2,1)S(1)}, u32[]{:S(2)}, u32[]{:S(2)}) collective-permute-start(bf16[512,128]{1,0:T(8,128)(2,1)S(1)} %constant_dynamic-update-slice_fusion.refs_0_), channel_id=1, source_target_pairs={{8,0},{16,8},{24,16},{0,24},{9,1},{17,9},{25,17},{1,25},{10,2},{18... | collective-permute-start | bytes 393224 | tf_op jit(solution)/shard_map/ppermute | solution.py:244
  29.9 6.1 %collective-permute-start.9 = (bf16[640,128]{1,0:T(8,128)(2,1)S(1)}, bf16[640,128]{1,0:T(8,128)(2,1)S(1)}, u32[]{:S(2)}, u32[]{:S(2)}) collective-permute-start(bf16[640,128]{1,0:T(8,128)(2,1)S(1)} %collective-permute-done.6.refs_4_), channel_id=1, source_target_pairs={{0,32},{32,0},{1,33},{33,1},{2,34},{34,2},{3,35},{35,3},{4,36},{36... | collective-permute-start | bytes 491528 | tf_op jit(solution)/shard_map/ppermute | solution.py:250
  30.0 8.0 %collective-permute-start.8 = (bf16[640,128]{1,0:T(8,128)(2,1)S(1)}, bf16[640,128]{1,0:T(8,128)(2,1)S(1)}, u32[]{:S(2)}, u32[]{:S(2)}) collective-permute-start(bf16[640,128]{1,0:T(8,128)(2,1)S(1)} %slice.4), channel_id=1, source_target_pairs={{0,32},{32,0},{1,33},{33,1},{2,34},{34,2},{3,35},{35,3},{4,36},{36... | collective-permute-start | bytes 491528 | tf_op jit(solution)/shard_map/ppermute | solution.py:250
  40.7 6.2 %collective-permute-start.11 = (f32[32,1024]{1,0:T(8,128)S(1)}, f32[32,1024]{1,0:T(8,128)S(1)}, u32[]{:S(2)}, u32[]{:S(2)}) collective-permute-start(f32[32,1024]{1,0:T(8,128)S(1)} %shard_map.41), channel_id=1, source_target_pairs={{0,64},{64,0},{1,65},{65,1},{2,66},{66,2},{3,67},{67,3},{4,68},{68... | collective-permute-start | bytes 393224 | tf_op jit(solution)/shard_map/ppermute | solution.py:250
  46.9 5.7 %collective-permute-start.12 = (f32[32,256]{1,0:T(8,128)S(1)}, f32[32,256]{1,0:T(8,128)S(1)}, u32[]{:S(2)}, u32[]{:S(2)}) collective-permute-start(f32[32,256]{1,0:T(8,128)S(1)} %get-tuple-element.20), channel_id=1, source_target_pairs={{0,8},{8,16},{16,24},{24,0},{1,9},{9,17},{17,25},{25,1},{2,10},{10... | collective-permute-start | bytes 98312 | tf_op jit(solution)/shard_map/ppermute | solution.py:247
  48.5 5.4 %collective-permute-start.13 = (f32[32,256]{1,0:T(8,128)S(1)}, f32[32,256]{1,0:T(8,128)S(1)}, u32[]{:S(2)}, u32[]{:S(2)}) collective-permute-start(f32[32,256]{1,0:T(8,128)S(1)} %get-tuple-element.21), channel_id=1, source_target_pairs={{0,16},{8,24},{16,0},{24,8},{1,17},{9,25},{17,1},{25,9},{2,18},{10... | collective-permute-start | bytes 98312 | tf_op jit(solution)/shard_map/ppermute | solution.py:247
  51.2 3.9 %collective-permute-start.14 = (f32[32,256]{1,0:T(8,128)S(1)}, f32[32,256]{1,0:T(8,128)S(1)}, u32[]{:S(2)}, u32[]{:S(2)}) collective-permute-start(f32[32,256]{1,0:T(8,128)S(1)} %get-tuple-element.22), channel_id=1, source_target_pairs={{0,24},{8,0},{16,8},{24,16},{1,25},{9,1},{17,9},{25,17},{2,26},{10... | collective-permute-start | bytes 98312 | tf_op jit(solution)/shard_map/ppermute | solution.py:247
  55.4 3.1 %collective-permute-start.17 = (f32[8,128]{1,0:T(8,128)S(1)}, f32[8,128]{1,0:T(8,128)S(1)}, u32[]{:S(2)}, u32[]{:S(2)}) collective-permute-start(f32[8,128]{1,0:T(8,128)S(1)} %get-tuple-element.23.refs_0_), channel_id=1, source_target_pairs={{0,96},{32,64},{64,32},{96,0},{1,97},{33,65},{65,33},{97,1},{2,98}... | collective-permute-start | bytes 12296 | tf_op jit(solution)/shard_map/ppermute | solution.py:274
  55.4 3.7 %collective-permute-start.16 = (f32[8,128]{1,0:T(8,128)S(1)}, f32[8,128]{1,0:T(8,128)S(1)}, u32[]{:S(2)}, u32[]{:S(2)}) collective-permute-start(f32[8,128]{1,0:T(8,128)S(1)} %get-tuple-element.23.refs_0_), channel_id=1, source_target_pairs={{0,64},{32,96},{64,0},{96,32},{1,65},{33,97},{65,1},{97,33},{2,66}... | collective-permute-start | bytes 12296 | tf_op jit(solution)/shard_map/ppermute | solution.py:274
  56.3 2.8 %collective-permute-start.15 = (f32[8,128]{1,0:T(8,128)S(1)}, f32[8,128]{1,0:T(8,128)S(1)}, u32[]{:S(2)}, u32[]{:S(2)}) collective-permute-start(f32[8,128]{1,0:T(8,128)S(1)} %get-tuple-element.23.refs_0_), channel_id=1, source_target_pairs={{0,32},{32,0},{64,96},{96,64},{1,33},{33,1},{65,97},{97,65},{2,34}... | collective-permute-start | bytes 12296 | tf_op jit(solution)/shard_map/ppermute | solution.py:274

commit v2 on v1

--- a/solution.py
+++ b/solution.py
@@ -91,64 +91,62 @@
     return jnp.where(lane < HALF, turned, -turned).astype(jnp.bfloat16)
 
 
-def image_kernel(shard, halves, blocks, pieces, has_start, *refs):
+def image_kernel(shard, blocks, pieces, has_start, *refs):
     rows = refs[:blocks]
     panels = refs[blocks : blocks + pieces]
-    starts = refs[blocks + pieces : blocks + pieces + len(halves)] if has_start else ()
-    outs = refs[-len(halves) :]
+    starts = refs[blocks + pieces : 2 * blocks + pieces] if has_start else ()
+    outs = refs[-blocks:]
     packed = shard + shard // 128 * MODES
-    for h, half in enumerate(halves):
-        u = jnp.concatenate([r[half * shard : (half + 1) * shard, :] for r in rows], axis=0)
-        t = twist(u)
-        acc = starts[h][...] if has_start else jnp.zeros((MODES, blocks * shard), jnp.float32)
-        for panel in panels:
-            for k in range(panel.shape[0] // packed):
-                base = k * packed
-                w = panel[base : base + shard, :]
-                re = dot(u, w, 1, 1)
-                im = dot(t, w, 1, 1)
-                c = jnp.maximum(re * re + im * im - np.float32(1.0 / (DEGREES - 1.0)), 0.0).astype(jnp.bfloat16)
-                st = jnp.concatenate(
-                    [
-                        panel[base + shard + MODES * j : base + shard + MODES * (j + 1), :]
-                        for j in range(shard // 128)
-                    ],
-                    axis=1,
-                )
-                acc = acc + dot(st, c, 1, 1)
-        outs[h][...] = acc
-
-
-def image(rows, halves, panels, shard, starts=()):
-    n = len(rows) * shard
+    u = jnp.concatenate([r[...] for r in rows], axis=0)
+    t = twist(u)
+    if has_start:
+        acc = jnp.concatenate([r[...] for r in starts], axis=1)
+    else:
+        acc = jnp.zeros((MODES, u.shape[0]), jnp.float32)
+    for panel in panels:
+        for k in range(panel.shape[0] // packed):
+            base = k * packed
+            w = panel[base : base + shard, :]
+            re = dot(u, w, 1, 1)
+            im = dot(t, w, 1, 1)
+            c = jnp.maximum(re * re + im * im - np.float32(1.0 / (DEGREES - 1.0)), 0.0).astype(jnp.bfloat16)
+            st = jnp.concatenate(
+                [panel[base + shard + MODES * j : base + shard + MODES * (j + 1), :] for j in range(shard // 128)],
+                axis=1,
+            )
+            acc = acc + dot(st, c, 1, 1)
+    width = rows[0].shape[0]
+    for i in range(blocks):
+        outs[i][...] = acc[:, i * width : (i + 1) * width]
+
+
+def image(rows, panels, shard, starts=()):
+    n = sum(r.shape[0] for r in rows)
     cols = sum(p.shape[0] for p in panels) * 4 // 5
     return pl.pallas_call(
-        functools.partial(image_kernel, shard, halves, len(rows), len(panels), len(starts) > 0),
-        out_shape=[jax.ShapeDtypeStruct((MODES, n), jnp.float32)] * len(halves),
+        functools.partial(image_kernel, shard, len(rows), len(panels), len(starts) > 0),
+        out_shape=[jax.ShapeDtypeStruct((MODES, r.shape[0]), jnp.float32) for r in rows],
         compiler_params=LARGE,
         cost_estimate=pl.CostEstimate(
-            flops=2 * n * len(halves) * cols * (2 * COLS + 4 * MODES),
-            bytes_accessed=n * 256 + cols * 320,
-            transcendentals=0,
+            flops=2 * n * cols * (2 * COLS + 4 * MODES), bytes_accessed=n * 256 + cols * 320, transcendentals=0
         ),
     )(*rows, *panels, *starts)
 
 
-def split_kernel(count, *refs):
-    a, b = refs[0], refs[1]
-    width = a.shape[1] // count
-    for k in range(count):
-        refs[2 + k][...] = a[:, k * width : (k + 1) * width] + b[:, k * width : (k + 1) * width]
-
-
-def add_and_split(a, b, count):
-    width = a.shape[1] // count
-    return pl.pallas_call(
-        functools.partial(split_kernel, count),
-        out_shape=[jax.ShapeDtypeStruct((a.shape[0], width), jnp.float32)] * count,
+def add_kernel(*refs):
+    total = refs[0][...]
+    for r in refs[1:-1]:
+        total = total + r[...]
+    refs[-1][...] = total
+
+
+def add(parts):
+    return pl.pallas_call(
+        add_kernel,
+        out_shape=jax.ShapeDtypeStruct(parts[0].shape, jnp.float32),
         compiler_params=SMALL,
-        name="add_and_split",
-    )(a, b)
+        name="add",
+    )(*parts)
 
 
 def pack(g):
@@ -159,55 +157,85 @@
     return jnp.concatenate([g[:, 32 * q : 32 * q + 32] for q in range(4)], axis=0)
 
 
-def gram_kernel(count, *refs):
-    total = refs[0][...]
-    for k in range(1, count):
-        total = total + refs[k][...]
-    refs[count][...] = total
-    refs[count + 1][...] = pack(dot(total, total, 1, 1, lax.Precision.HIGHEST))
-
-
-def gram_of(parts):
-    return pl.pallas_call(
-        functools.partial(gram_kernel, len(parts)),
+def gram_kernel(mine, theirs, image_ref, gram_ref):
+    half = mine.shape[1] // 2
+    own = mine[:, :half] + theirs[:, half:]
+    other = mine[:, half:] + theirs[:, :half]
+    image_ref[...] = own
+    g = dot(own, own, 1, 1, lax.Precision.HIGHEST) + dot(other, other, 1, 1, lax.Precision.HIGHEST)
+    gram_ref[...] = pack(g)
+
+
+def gram_of(mine, theirs):
+    return pl.pallas_call(
+        gram_kernel,
         out_shape=[
-            jax.ShapeDtypeStruct(parts[0].shape, jnp.float32),
+            jax.ShapeDtypeStruct((MODES, mine.shape[1] // 2), jnp.float32),
             jax.ShapeDtypeStruct((8, 128), jnp.float32),
         ],
         compiler_params=SMALL,
         name="gram",
-    )(*parts)
-
-
-def sum_kernel(count, copies, *refs):
-    total = (refs[0][...] + refs[1][...]) + (refs[2][...] + refs[3][...])
+    )(mine, theirs)
+
+
+def copies_kernel(copies, a, b, out):
+    total = a[...] + b[...]
     for k in range(copies):
-        refs[count][k] = total
-
-
-def sum_copies(grams, copies):
-    return pl.pallas_call(
-        functools.partial(sum_kernel, len(grams), copies),
+        out[k] = total
+
+
+def add_and_copy(a, b, copies):
+    return pl.pallas_call(
+        functools.partial(copies_kernel, copies),
         out_shape=jax.ShapeDtypeStruct((copies, 8, 128), jnp.float32),
         compiler_params=SMALL,
-        name="gram_sum",
-    )(*grams)
+        name="gram_copies",
+    )(a, b)
+
+
+BLOCK = 4
 
 
 def modes_kernel(scale, grams, image_ref, out):
     g = unpack(jnp.sum(grams[...], axis=0))
+    g = jnp.concatenate([g, jnp.zeros((MODES, 128 - MODES), jnp.float32)], axis=1)
     y = image_ref[...]
-    row = lax.broadcasted_iota(jnp.int32, (MODES, 1), 0)
-    for k in range(MODES):
-        pivot = g[k : k + 1, k : k + 1]
-        inv = lax.rsqrt(pivot)
-        inv = inv * (1.5 - 0.5 * pivot * inv * inv)
-        pivot_g = g[k : k + 1, :] * inv
-        pivot_y = y[k : k + 1, :] * inv
-        below = jnp.where(row > k, g[:, k : k + 1] * inv, 0.0)
-        g = g - below * pivot_g
-        y = jnp.where(row == k, pivot_y, y - below * pivot_y)
-    out[...] = y * scale
+    n = y.shape[1]
+    for k in range(0, MODES, BLOCK):
+        block = [
+            [jnp.broadcast_to(g[k + i : k + i + 1, k + j : k + j + 1], (8, 128)) for j in range(i + 1)]
+            for i in range(BLOCK)
+        ]
+        gr = [jnp.broadcast_to(g[k + i : k + i + 1, :], (8, 128)) for i in range(BLOCK)]
+        yr = [jnp.broadcast_to(y[k + i : k + i + 1, :], (8, n)) for i in range(BLOCK)]
+        gc = [jnp.broadcast_to(g[:, k + i : k + i + 1], (MODES, 128)) for i in range(BLOCK)]
+        wide = lambda v: jnp.concatenate([v] * (n // 128), axis=1)
+        tall = lambda v: jnp.concatenate([v] * (MODES // 8), axis=0)
+        for i in range(BLOCK):
+            for j in range(i):
+                low = block[i][j]
+                for r in range(i, BLOCK):
+                    if r == i:
+                        block[i][i] = block[i][i] - low * low
+                    else:
+                        block[r][i] = block[r][i] - block[r][j] * low
+                gr[i] = gr[i] - low * gr[j]
+                yr[i] = yr[i] - wide(low) * yr[j]
+                gc[i] = gc[i] - tall(low) * gc[j]
+            pivot = block[i][i]
+            inv = lax.rsqrt(pivot)
+            inv = inv * (1.5 - 0.5 * pivot * inv * inv)
+            for r in range(i + 1, BLOCK):
+                block[r][i] = block[r][i] * inv
+            gr[i] = gr[i] * inv
+            yr[i] = yr[i] * wide(inv)
+            gc[i] = gc[i] * tall(inv)
+        if k + BLOCK < MODES:
+            for i in range(BLOCK):
+                g = g - gc[i] * tall(gr[i])
+                y = y - wide(gc[i]) * tall(yr[i])
+        for i in range(BLOCK):
+            out[k + i : k + i + 1, :] = yr[i][0:1, :] * scale
 
 
 def modes_of(grams, img, scale):
@@ -260,19 +288,20 @@
     rows = [first] + [from_x(first, k) for k in range(1, nx)]
     one_c = swap(one, "c")
     two_c = swap(two, "c")
-    far = both_ways(jnp.concatenate([one, two], axis=0), 2)
-    far_c = swap(far[: pair.shape[0]], "c")
-    own, other = image(rows, (0, 1), [pair, one, one_c], shard)
-    (other,) = image(rows, (1,), [two, two_c], shard, (other,))
-    (own,) = image(rows, (0,), [two, two_c], shard, (own,))
-    (other,) = image(rows, (1,), [far, far_c], shard, (other,))
-    (own,) = image(rows, (0,), [far, far_c], shard, (own,))
-    sums = add_and_split(own, swap(other, "y"), nx)
-    parts = [sums[0]] + [to_x(sums[k], k) for k in range(1, nx)]
-    img, gram = gram_of(parts)
-    quad = ("y", "c")
-    four = [gram] + [lax.ppermute(gram, quad, [(i, i ^ k) for i in range(4)]) for k in (1, 2, 3)]
-    grams = sum_copies(four, nx * nz)
+    far = both_ways(jnp.concatenate([one, two[: w.shape[0]]], axis=0), 2)
+    far_c = swap(far, "c")
+    home, rest = rows[:1], rows[1:]
+    near = image(home, [pair], shard)
+    near = image(home, [one, one_c, two, two_c], shard, near)
+    away = image(rest, [pair, one, one_c], shard)
+    away = image(rest, [two, two_c], shard, away)
+    away = image(rest, [far], shard, away)
+    away = image(rest, [far_c], shard, away)
+    back = [to_x(away[k - 1], k) for k in (2, 1, 3)]
+    near = image(home, [far, far_c], shard, near)
+    mine = add([*near, *back])
+    img, gram = gram_of(mine, swap(mine, "y"))
+    grams = add_and_copy(gram, swap(gram, "c"), nx * nz)
     grams = lax.all_to_all(grams, ("x", "z"), 0, 0)
     return modes_of(grams, img, float(np.sqrt(neurons))).T
 

time: 81.1 us -> 75.7 us (0.933)
  starting transfers between devices: 24.4 us -> 21.8 us
  blocking collectives: 18.4 us -> 16.6 us
    ppermute x6 -> x7, waiting for transfers between devices: 1.27 us -> 5.4 us  [swap(): return lax.ppermute(v, axis, [(0, 1), (1, 0)])]
    ppermute x3, waiting for transfers between devices: 10.5 us -> 7.77 us  [both_ways(): return lax.ppermute(v, ('c', 'z'), pairs)]
    ppermute x3, waiting for transfers between devices: 0.01 us -> 2.54 us  [from_x(): return lax.ppermute(v, 'x', [((i + k) % nx, i) for i in range(nx)])]
    ppermute x3, waiting for transfers between devices: 2.48 us -> 0.01 us  [to_x(): return lax.ppermute(v, 'x', [(i, (i + k) % nx) for i in range(nx)])]
    ppermute x3 -> x0, starting transfers between devices: 1.89 us -> none  [local(): lax.ppermute(gram, quad, [(i, i ^ k) for i in range(4)])]
    ppermute x3 -> x0, waiting for transfers between devices: 1.85 us -> none  [local(): lax.ppermute(gram, quad, [(i, i ^ k) for i in range(4)])]
    all_to_all x1, blocking collectives: 18.4 us -> 16.6 us  [local(): grams = lax.all_to_all(grams, ('x', 'z'), 0, 0)]
    pallas_call x1, Pallas kernels: 3.44 us -> 2.08 us  [modes_of(): pl.pallas_call(functools.partial(modes_kernel, scale), out_shape=jax.Shap...]
  transfers between devices with their start and end apart: 18 -> 16, of which waited for: 8 -> 8; matrix products, arithmetic and copies ran while one was open for 0% -> 0% of each run, Pallas kernels for 15% -> 18%
where the time goes in v2:
time: 75.7 us; the launch traced here: 75.5 us
  starting transfers between devices  21.8 us (29%)
  Pallas kernels  21.2 us (28%)
  blocking collectives  16.6 us (22%)
  waiting for transfers between devices  15.7 us (21%)
    all_to_all x1, blocking collectives, local(): grams = lax.all_to_all(grams, ('x', 'z'), 0, 0)  16.6 us
    pallas_call x7, Pallas kernels, image(): pl.pallas_call(functools.partial(image_kernel, shard, len(rows), len(pane...  15.2 us
    ppermute x3, waiting for transfers between devices, both_ways(): return lax.ppermute(v, ('c', 'z'), pairs)  7.77 us
    ppermute x3, starting transfers between devices, both_ways(): return lax.ppermute(v, ('c', 'z'), pairs)  6.46 us
    ppermute x3, starting transfers between devices, to_x(): return lax.ppermute(v, 'x', [(i, (i + k) % nx) for i in range(nx)])  5.96 us
    ppermute x3, starting transfers between devices, from_x(): return lax.ppermute(v, 'x', [((i + k) % nx, i) for i in range(nx)])  5.73 us
    ppermute x7, waiting for transfers between devices, swap(): return lax.ppermute(v, axis, [(0, 1), (1, 0)])  5.4 us
    ppermute x7, starting transfers between devices, swap(): return lax.ppermute(v, axis, [(0, 1), (1, 0)])  3.65 us
  transfers between devices with their start and end apart: 16, of which 8 were waited for; matrix products, arithmetic and copies ran while one was open for 0% of the time, Pallas kernels for 18%

profile of v2, /device:TPU:16, one launch (start us, length us, event | category | flops | bytes accessed | tf_op | source)
XLA Modules:
  0.0 75.5 jit_solution(16603370913267353358)
XLA Ops:
  0.0 3.6 %spectra.1 = (bf16[256,128]{1,0:T(8,128)(2,1)S(1)}, bf16[320,128]{1,0:T(8,128)(2,1)S(1)}) custom-call(s32[256,8,128]{2,1,0:T(8,128)} %counts_hbm.1, bf16[32,256]{1,0:T(8,128)(2,1)} %bitcast.2, bf16[3,128,128]{2,1,0:T(8,128)(2,1)} %constant.2.clone.tables_hbm), custom_call_target="tpu_custom_call" | custom-call | tf_op jit(solution)/shard_map/spectra/pallas_call | solution.py:254
  3.7 1.2 %collective-permute-done.1 = bf16[320,128]{1,0:T(8,128)(2,1)S(1)} collective-permute-done((bf16[320,128]{1,0:T(8,128)(2,1)S(1)}, bf16[320,128]{1,0:T(8,128)(2,1)S(1)}, u32[]{:S(2)}, u32[]{:S(2)}) %collective-permute-start.1) | collective-permute-done | bytes 81952 | tf_op jit(solution)/shard_map/ppermute | solution.py:278
  5.0 3.3 %collective-permute-start.3 = (bf16[640,128]{1,0:T(8,128)(2,1)S(1)}, bf16[640,128]{1,0:T(8,128)(2,1)S(1)}, u32[]{:S(2)}, u32[]{:S(2)}) collective-permute-start(bf16[640,128]{1,0:T(8,128)(2,1)S(1)} %constant_dynamic-update-slice_fusion.2.refs_1_.refs_3_), channel_id=1, source_target_pairs={{0,2},{1,3},{2,4},{3,5},{4,6},{5,7},{6,0},{7,1},{32,38},{33,39},{3... | collective-permute-start | bytes 491528 | tf_op jit(solution)/shard_map/ppermute | solution.py:282
  8.4 1.9 %collective-permute-start.2 = (bf16[640,128]{1,0:T(8,128)(2,1)S(1)}, bf16[640,128]{1,0:T(8,128)(2,1)S(1)}, u32[]{:S(2)}, u32[]{:S(2)}) collective-permute-start(bf16[640,128]{1,0:T(8,128)(2,1)S(1)} %constant_dynamic-update-slice_fusion.2.refs_1_.refs_3_), channel_id=1, source_target_pairs={{0,1},{1,2},{2,3},{3,4},{4,5},{5,6},{6,7},{7,0},{32,39},{33,32},{3... | collective-permute-start | bytes 491528 | tf_op jit(solution)/shard_map/ppermute | solution.py:282
  10.3 1.3 %collective-permute-start = (bf16[256,128]{1,0:T(8,128)(2,1)S(1)}, bf16[256,128]{1,0:T(8,128)(2,1)S(1)}, u32[]{:S(2)}, u32[]{:S(2)}) collective-permute-start(bf16[256,128]{1,0:T(8,128)(2,1)S(1)} %get-tuple-element.21), channel_id=1, source_target_pairs={{0,64},{64,0},{1,65},{65,1},{2,66},{66,2},{3,67},{67,3},{4,68},{68... | collective-permute-start | bytes 196616 | tf_op jit(solution)/shard_map/ppermute | solution.py:278
  11.6 3.2 %collective-permute-done.3.refs_3_ = bf16[640,128]{1,0:T(8,128)(2,1)S(1)} collective-permute-done((bf16[640,128]{1,0:T(8,128)(2,1)S(1)}, bf16[640,128]{1,0:T(8,128)(2,1)S(1)}, u32[]{:S(2)}, u32[]{:S(2)}) %collective-permute-start.3) | collective-permute-done | bytes 163872 | tf_op jit(solution)/shard_map/ppermute | solution.py:282
  14.8 3.0 %collective-permute-done.2.refs_1_.refs_4_ = bf16[640,128]{1,0:T(8,128)(2,1)S(1)} collective-permute-done((bf16[640,128]{1,0:T(8,128)(2,1)S(1)}, bf16[640,128]{1,0:T(8,128)(2,1)S(1)}, u32[]{:S(2)}, u32[]{:S(2)}) %collective-permute-start.2) | collective-permute-done | bytes 163872 | tf_op jit(solution)/shard_map/ppermute | solution.py:282
  19.8 1.6 %collective-permute-start.10 = (bf16[512,128]{1,0:T(8,128)(2,1)S(1)}, bf16[512,128]{1,0:T(8,128)(2,1)S(1)}, u32[]{:S(2)}, u32[]{:S(2)}) collective-permute-start(bf16[512,128]{1,0:T(8,128)(2,1)S(1)} %constant_dynamic-update-slice_fusion.refs_0_), channel_id=1, source_target_pairs={{24,0},{0,8},{8,16},{16,24},{25,1},{1,9},{9,17},{17,25},{26,2},{2,... | collective-permute-start | bytes 393224 | tf_op jit(solution)/shard_map/ppermute | solution.py:272
  21.4 2.7 %collective-permute-start.9 = (bf16[512,128]{1,0:T(8,128)(2,1)S(1)}, bf16[512,128]{1,0:T(8,128)(2,1)S(1)}, u32[]{:S(2)}, u32[]{:S(2)}) collective-permute-start(bf16[512,128]{1,0:T(8,128)(2,1)S(1)} %constant_dynamic-update-slice_fusion.refs_0_), channel_id=1, source_target_pairs={{16,0},{24,8},{0,16},{8,24},{17,1},{25,9},{1,17},{9,25},{18,2},{26... | collective-permute-start | bytes 393224 | tf_op jit(solution)/shard_map/ppermute | solution.py:272
  24.1 1.4 %collective-permute-start.8 = (bf16[512,128]{1,0:T(8,128)(2,1)S(1)}, bf16[512,128]{1,0:T(8,128)(2,1)S(1)}, u32[]{:S(2)}, u32[]{:S(2)}) collective-permute-start(bf16[512,128]{1,0:T(8,128)(2,1)S(1)} %constant_dynamic-update-slice_fusion.refs_0_), channel_id=1, source_target_pairs={{8,0},{16,8},{24,16},{0,24},{9,1},{17,9},{25,17},{1,25},{10,2},{18... | collective-permute-start | bytes 393224 | tf_op jit(solution)/shard_map/ppermute | solution.py:272
  26.6 1.6 %collective-permute-done.4.refs_1_.refs_3_ = bf16[960,128]{1,0:T(8,128)(2,1)S(1)} collective-permute-done((bf16[960,128]{1,0:T(8,128)(2,1)S(1)}, bf16[960,128]{1,0:T(8,128)(2,1)S(1)}, u32[]{:S(2)}, u32[]{:S(2)}) %collective-permute-start.4) | collective-permute-done | bytes 245792 | tf_op jit(solution)/shard_map/ppermute | solution.py:282
  28.2 2.2 %collective-permute-done.9.refs_1_ = bf16[512,128]{1,0:T(8,128)(2,1)S(1)} collective-permute-done((bf16[512,128]{1,0:T(8,128)(2,1)S(1)}, bf16[512,128]{1,0:T(8,128)(2,1)S(1)}, u32[]{:S(2)}, u32[]{:S(2)}) %collective-permute-start.9) | collective-permute-done | bytes 131104 | tf_op jit(solution)/shard_map/ppermute | solution.py:272
  30.4 3.7 %shard_map.40 = (f32[32,512]{1,0:T(8,128)S(1)}, f32[32,512]{1,0:T(8,128)S(1)}, f32[32,512]{1,0:T(8,128)S(1)}) custom-call(bf16[512,128]{1,0:T(8,128)(2,1)S(1)} %collective-permute-done.8.refs_0_, bf16[512,128]{1,0:T(8,128)(2,1)S(1)} %collective-permute-done.9.refs_1_, bf16[512,128]{1,0:T(8,128)(2,1)S(1)} %collective-permute-done.10.refs_2_, ...), custom_call_target="tpu_custom_call" | custom-call | flops 1811939328 | bytes 884736 | tf_op jit(solution)/shard_map/pallas_call | solution.py:126
  34.1 2.5 %shard_map.41 = (f32[32,512]{1,0:T(8,128)S(1)}, f32[32,512]{1,0:T(8,128)S(1)}, f32[32,512]{1,0:T(8,128)S(1)}) custom-call(bf16[512,128]{1,0:T(8,128)(2,1)S(1)} %collective-permute-done.8.refs_0_, bf16[512,128]{1,0:T(8,128)(2,1)S(1)} %collective-permute-done.9.refs_1_, bf16[512,128]{1,0:T(8,128)(2,1)S(1)} %collective-permute-done.10.refs_2_, ...), custom_call_target="tpu_custom_call" | custom-call | flops 1207959552 | bytes 720896 | tf_op jit(solution)/shard_map/pallas_call | solution.py:126
  36.6 1.9 %shard_map.42 = (f32[32,512]{1,0:T(8,128)S(1)}, f32[32,512]{1,0:T(8,128)S(1)}, f32[32,512]{1,0:T(8,128)S(1)}) custom-call(bf16[512,128]{1,0:T(8,128)(2,1)S(1)} %collective-permute-done.8.refs_0_, bf16[512,128]{1,0:T(8,128)(2,1)S(1)} %collective-permute-done.9.refs_1_, bf16[512,128]{1,0:T(8,128)(2,1)S(1)} %collective-permute-done.10.refs_2_, ...), custom_call_target="tpu_custom_call" | custom-call | flops 905969664 | bytes 638976 | tf_op jit(solution)/shard_map/pallas_call | solution.py:126
  38.6 1.9 %shard_map.43 = (f32[32,512]{1,0:T(8,128)S(1)}, f32[32,512]{1,0:T(8,128)S(1)}, f32[32,512]{1,0:T(8,128)S(1)}) custom-call(bf16[512,128]{1,0:T(8,128)(2,1)S(1)} %collective-permute-done.8.refs_0_, bf16[512,128]{1,0:T(8,128)(2,1)S(1)} %collective-permute-done.9.refs_1_, bf16[512,128]{1,0:T(8,128)(2,1)S(1)} %collective-permute-done.10.refs_2_, ...), custom_call_target="tpu_custom_call" | custom-call | flops 905969664 | bytes 638976 | tf_op jit(solution)/shard_map/pallas_call | solution.py:126
  40.5 2.7 %collective-permute-start.11 = (f32[32,512]{1,0:T(8,128)S(1)}, f32[32,512]{1,0:T(8,128)S(1)}, u32[]{:S(2)}, u32[]{:S(2)}) collective-permute-start(f32[32,512]{1,0:T(8,128)S(1)} %get-tuple-element.32), channel_id=1, source_target_pairs={{0,16},{8,24},{16,0},{24,8},{1,17},{9,25},{17,1},{25,9},{2,18},{10... | collective-permute-start | bytes 196616 | tf_op jit(solution)/shard_map/ppermute | solution.py:275
  43.7 2.8 %collective-permute-start.13 = (f32[32,512]{1,0:T(8,128)S(1)}, f32[32,512]{1,0:T(8,128)S(1)}, u32[]{:S(2)}, u32[]{:S(2)}) collective-permute-start(f32[32,512]{1,0:T(8,128)S(1)} %get-tuple-element.34), channel_id=1, source_target_pairs={{0,24},{8,0},{16,8},{24,16},{1,25},{9,1},{17,9},{25,17},{2,26},{10... | collective-permute-start | bytes 196616 | tf_op jit(solution)/shard_map/ppermute | solution.py:275
  46.5 2.5 %shard_map.38.refs_3_ = f32[32,512]{1,0:T(8,128)S(1)} custom-call(bf16[512,128]{1,0:T(8,128)(2,1)S(1)} %constant_dynamic-update-slice_fusion.refs_0_, bf16[640,128]{1,0:T(8,128)(2,1)S(1)} %collective-permute-done.2.refs_1_.refs_4_, bf16[640,128]{1,0:T(8,128)(2,1)S(1)} %collective-permute-done.6.refs_2_.refs_5_, ...), custom_call_target="tpu_custom_call" | custom-call | flops 805306368 | bytes 786432 | tf_op jit(solution)/shard_map/pallas_call | solution.py:126
  49.0 1.9 %shard_map.39.refs_0_ = f32[32,512]{1,0:T(8,128)S(1)} custom-call(bf16[512,128]{1,0:T(8,128)(2,1)S(1)} %constant_dynamic-update-slice_fusion.refs_0_, bf16[960,128]{1,0:T(8,128)(2,1)S(1)} %collective-permute-done.4.refs_1_.refs_3_, bf16[960,128]{1,0:T(8,128)(2,1)S(1)} %collective-permute-done.5.refs_2_.refs_3_, f32[32,512]{1,0:T(8,128)S(1)} %shard_map.38.refs_3_), custom_call_target="tpu_custom_call" | custom-call | flops 603979776 | bytes 622592 | tf_op jit(solution)/shard_map/pallas_call | solution.py:126
  51.0 1.4 %collective-permute-start.14 = (f32[32,512]{1,0:T(8,128)S(1)}, f32[32,512]{1,0:T(8,128)S(1)}, u32[]{:S(2)}, u32[]{:S(2)}) collective-permute-start(f32[32,512]{1,0:T(8,128)S(1)} %add.1.mine), channel_id=1, source_target_pairs={{0,64},{64,0},{1,65},{65,1},{2,66},{66,2},{3,67},{67,3},{4,68},{68... | collective-permute-start | bytes 196616 | tf_op jit(solution)/shard_map/ppermute | solution.py:278
  52.4 3.0 %collective-permute-done.14.theirs = f32[32,512]{1,0:T(8,128)S(1)} collective-permute-done((f32[32,512]{1,0:T(8,128)S(1)}, f32[32,512]{1,0:T(8,128)S(1)}, u32[]{:S(2)}, u32[]{:S(2)}) %collective-permute-start.14) | collective-permute-done | bytes 65568 | tf_op jit(solution)/shard_map/ppermute | solution.py:278
  56.8 16.6 %all_to_all.5.grams = f32[32,8,128]{2,1,0:T(8,128)S(1)} all-to-all(f32[32,8,128]{2,1,0:T(8,128)S(1)} %gram_copies.1), channel_id=1, replica_groups=mesh['freq'=2,'y'=2,'c'=2,'x'=4,'z'=8] {'x','z'}, dimensions={0} | all-to-all | bytes 262144 | tf_op jit(solution)/shard_map/all_to_all | solution.py:305
  73.4 2.1 %modes.1 = f32[32,256]{1,0:T(8,128)} custom-call(f32[32,8,128]{2,1,0:T(8,128)S(1)} %all_to_all.5.grams, f32[32,256]{1,0:T(8,128)S(1)} %get-tuple-element.36.image_ref), custom_call_target="tpu_custom_call" | custom-call | tf_op jit(solution)/shard_map/modes/pallas_call | solution.py:242
  (27 shorter events, 5.2 us)
Async XLA Ops:
  3.6 1.4 %collective-permute-start.1 = (bf16[320,128]{1,0:T(8,128)(2,1)S(1)}, bf16[320,128]{1,0:T(8,128)(2,1)S(1)}, u32[]{:S(2)}, u32[]{:S(2)}) collective-permute-start(bf16[320,128]{1,0:T(8,128)(2,1)S(1)} %get-tuple-element.22), channel_id=1, source_target_pairs={{0,32},{32,0},{1,33},{33,1},{2,34},{34,2},{3,35},{35,3},{4,36},{36... | collective-permute-start | bytes 245768 | tf_op jit(solution)/shard_map/ppermute | solution.py:278
  5.0 9.8 %collective-permute-start.3 = (bf16[640,128]{1,0:T(8,128)(2,1)S(1)}, bf16[640,128]{1,0:T(8,128)(2,1)S(1)}, u32[]{:S(2)}, u32[]{:S(2)}) collective-permute-start(bf16[640,128]{1,0:T(8,128)(2,1)S(1)} %constant_dynamic-update-slice_fusion.2.refs_1_.refs_3_), channel_id=1, source_target_pairs={{0,2},{1,3},{2,4},{3,5},{4,6},{5,7},{6,0},{7,1},{32,38},{33,39},{3... | collective-permute-start | bytes 491528 | tf_op jit(solution)/shard_map/ppermute | solution.py:282
  8.4 9.4 %collective-permute-start.2 = (bf16[640,128]{1,0:T(8,128)(2,1)S(1)}, bf16[640,128]{1,0:T(8,128)(2,1)S(1)}, u32[]{:S(2)}, u32[]{:S(2)}) collective-permute-start(bf16[640,128]{1,0:T(8,128)(2,1)S(1)} %constant_dynamic-update-slice_fusion.2.refs_1_.refs_3_), channel_id=1, source_target_pairs={{0,1},{1,2},{2,3},{3,4},{4,5},{5,6},{6,7},{7,0},{32,39},{33,32},{3... | collective-permute-start | bytes 491528 | tf_op jit(solution)/shard_map/ppermute | solution.py:282
  10.3 9.6 %collective-permute-start = (bf16[256,128]{1,0:T(8,128)(2,1)S(1)}, bf16[256,128]{1,0:T(8,128)(2,1)S(1)}, u32[]{:S(2)}, u32[]{:S(2)}) collective-permute-start(bf16[256,128]{1,0:T(8,128)(2,1)S(1)} %get-tuple-element.21), channel_id=1, source_target_pairs={{0,64},{64,0},{1,65},{65,1},{2,66},{66,2},{3,67},{67,3},{4,68},{68... | collective-permute-start | bytes 196616 | tf_op jit(solution)/shard_map/ppermute | solution.py:278
  17.8 10.4 %collective-permute-start.4 = (bf16[960,128]{1,0:T(8,128)(2,1)S(1)}, bf16[960,128]{1,0:T(8,128)(2,1)S(1)}, u32[]{:S(2)}, u32[]{:S(2)}) collective-permute-start(bf16[960,128]{1,0:T(8,128)(2,1)S(1)} %pad_maximum_fusion), channel_id=1, source_target_pairs={{0,2},{1,3},{2,4},{3,5},{4,6},{5,7},{6,0},{7,1},{32,38},{33,39},{3... | collective-permute-start | bytes 737288 | tf_op jit(solution)/shard_map/ppermute | solution.py:282
  19.0 11.4 %collective-permute-start.6 = (bf16[640,128]{1,0:T(8,128)(2,1)S(1)}, bf16[640,128]{1,0:T(8,128)(2,1)S(1)}, u32[]{:S(2)}, u32[]{:S(2)}) collective-permute-start(bf16[640,128]{1,0:T(8,128)(2,1)S(1)} %collective-permute-done.2.refs_1_.refs_4_), channel_id=1, source_target_pairs={{0,32},{32,0},{1,33},{33,1},{2,34},{34,2},{3,35},{35,3},{4,36},{36... | collective-permute-start | bytes 491528 | tf_op jit(solution)/shard_map/ppermute | solution.py:278
  19.8 6.7 %collective-permute-start.10 = (bf16[512,128]{1,0:T(8,128)(2,1)S(1)}, bf16[512,128]{1,0:T(8,128)(2,1)S(1)}, u32[]{:S(2)}, u32[]{:S(2)}) collective-permute-start(bf16[512,128]{1,0:T(8,128)(2,1)S(1)} %constant_dynamic-update-slice_fusion.refs_0_), channel_id=1, source_target_pairs={{24,0},{0,8},{8,16},{16,24},{25,1},{1,9},{9,17},{17,25},{26,2},{2,... | collective-permute-start | bytes 393224 | tf_op jit(solution)/shard_map/ppermute | solution.py:272
  21.4 8.9 %collective-permute-start.9 = (bf16[512,128]{1,0:T(8,128)(2,1)S(1)}, bf16[512,128]{1,0:T(8,128)(2,1)S(1)}, u32[]{:S(2)}, u32[]{:S(2)}) collective-permute-start(bf16[512,128]{1,0:T(8,128)(2,1)S(1)} %constant_dynamic-update-slice_fusion.refs_0_), channel_id=1, source_target_pairs={{16,0},{24,8},{0,16},{8,24},{17,1},{25,9},{1,17},{9,25},{18,2},{26... | collective-permute-start | bytes 393224 | tf_op jit(solution)/shard_map/ppermute | solution.py:272
  24.1 6.2 %collective-permute-start.8 = (bf16[512,128]{1,0:T(8,128)(2,1)S(1)}, bf16[512,128]{1,0:T(8,128)(2,1)S(1)}, u32[]{:S(2)}, u32[]{:S(2)}) collective-permute-start(bf16[512,128]{1,0:T(8,128)(2,1)S(1)} %constant_dynamic-update-slice_fusion.refs_0_), channel_id=1, source_target_pairs={{8,0},{16,8},{24,16},{0,24},{9,1},{17,9},{25,17},{1,25},{10,2},{18... | collective-permute-start | bytes 393224 | tf_op jit(solution)/shard_map/ppermute | solution.py:272
  26.6 7.5 %collective-permute-start.7 = (bf16[640,128]{1,0:T(8,128)(2,1)S(1)}, bf16[640,128]{1,0:T(8,128)(2,1)S(1)}, u32[]{:S(2)}, u32[]{:S(2)}) collective-permute-start(bf16[640,128]{1,0:T(8,128)(2,1)S(1)} %collective-permute-done.3.refs_3_), channel_id=1, source_target_pairs={{0,32},{32,0},{1,33},{33,1},{2,34},{34,2},{3,35},{35,3},{4,36},{36... | collective-permute-start | bytes 491528 | tf_op jit(solution)/shard_map/ppermute | solution.py:278
  28.1 10.4 %collective-permute-start.5 = (bf16[960,128]{1,0:T(8,128)(2,1)S(1)}, bf16[960,128]{1,0:T(8,128)(2,1)S(1)}, u32[]{:S(2)}, u32[]{:S(2)}) collective-permute-start(bf16[960,128]{1,0:T(8,128)(2,1)S(1)} %collective-permute-done.4.refs_1_.refs_3_), channel_id=1, source_target_pairs={{0,32},{32,0},{1,33},{33,1},{2,34},{34,2},{3,35},{35,3},{4,36},{36... | collective-permute-start | bytes 737288 | tf_op jit(solution)/shard_map/ppermute | solution.py:278
  40.5 10.4 %collective-permute-start.11 = (f32[32,512]{1,0:T(8,128)S(1)}, f32[32,512]{1,0:T(8,128)S(1)}, u32[]{:S(2)}, u32[]{:S(2)}) collective-permute-start(f32[32,512]{1,0:T(8,128)S(1)} %get-tuple-element.32), channel_id=1, source_target_pairs={{0,16},{8,24},{16,0},{24,8},{1,17},{9,25},{17,1},{25,9},{2,18},{10... | collective-permute-start | bytes 196616 | tf_op jit(solution)/shard_map/ppermute | solution.py:275
  43.2 7.7 %collective-permute-start.12 = (f32[32,512]{1,0:T(8,128)S(1)}, f32[32,512]{1,0:T(8,128)S(1)}, u32[]{:S(2)}, u32[]{:S(2)}) collective-permute-start(f32[32,512]{1,0:T(8,128)S(1)} %get-tuple-element.33), channel_id=1, source_target_pairs={{0,8},{8,16},{16,24},{24,0},{1,9},{9,17},{17,25},{25,1},{2,10},{10... | collective-permute-start | bytes 196616 | tf_op jit(solution)/shard_map/ppermute | solution.py:275
  43.7 7.2 %collective-permute-start.13 = (f32[32,512]{1,0:T(8,128)S(1)}, f32[32,512]{1,0:T(8,128)S(1)}, u32[]{:S(2)}, u32[]{:S(2)}) collective-permute-start(f32[32,512]{1,0:T(8,128)S(1)} %get-tuple-element.34), channel_id=1, source_target_pairs={{0,24},{8,0},{16,8},{24,16},{1,25},{9,1},{17,9},{25,17},{2,26},{10... | collective-permute-start | bytes 196616 | tf_op jit(solution)/shard_map/ppermute | solution.py:275
  51.0 4.4 %collective-permute-start.14 = (f32[32,512]{1,0:T(8,128)S(1)}, f32[32,512]{1,0:T(8,128)S(1)}, u32[]{:S(2)}, u32[]{:S(2)}) collective-permute-start(f32[32,512]{1,0:T(8,128)S(1)} %add.1.mine), channel_id=1, source_target_pairs={{0,64},{64,0},{1,65},{65,1},{2,66},{66,2},{3,67},{67,3},{4,68},{68... | collective-permute-start | bytes 196616 | tf_op jit(solution)/shard_map/ppermute | solution.py:278
  55.6 1.2 %collective-permute-start.15 = (f32[8,128]{1,0:T(8,128)S(1)}, f32[8,128]{1,0:T(8,128)S(1)}, u32[]{:S(2)}, u32[]{:S(2)}) collective-permute-start(f32[8,128]{1,0:T(8,128)S(1)} %get-tuple-element.35.a), channel_id=1, source_target_pairs={{0,32},{32,0},{1,33},{33,1},{2,34},{34,2},{3,35},{35,3},{4,36},{36... | collective-permute-start | bytes 12296 | tf_op jit(solution)/shard_map/ppermute | solution.py:278

commit v3 on v2

--- a/solution.py
+++ b/solution.py
@@ -47,7 +47,7 @@
     )
 
 
-CHUNKS = 4
+CHUNKS = 2
 
 
 def spectra_kernel(counts_hbm, subspace_hbm, tables_hbm, u_ref, w_ref, counts, subspace, tables, sems):
@@ -69,11 +69,15 @@
     for i in range(CHUNKS):
         copies[1 + i].wait()
         span = slice(i * part, (i + 1) * part)
-        total = jnp.zeros((part, COLS), jnp.float32)
-        for s in range(SEGS):
-            x = counts[span, s, :].astype(jnp.float32).astype(jnp.bfloat16)
-            for p in range(3):
-                total = total + dot(x, table[s][p], 1, 0)
+        upper = jnp.zeros((part, 2 * COLS), jnp.float32)
+        lower = jnp.zeros((part, COLS), jnp.float32)
+        for s in range(0, SEGS, 2):
+            x = [counts[span, s + j, :].astype(jnp.float32).astype(jnp.bfloat16) for j in range(2)]
+            x = jnp.concatenate(x, axis=1)
+            t = [jnp.concatenate([table[s][p], table[s + 1][p]], axis=0) for p in range(3)]
+            upper = upper + dot(x, jnp.concatenate(t[:2], axis=1), 1, 0)
+            lower = lower + dot(x, t[2], 1, 0)
+        total = upper[:, :COLS] + (upper[:, COLS:] + lower)
         spectra = total.astype(jnp.bfloat16).astype(jnp.float32)
         power = jnp.sum(spectra * spectra, axis=1, keepdims=True) + 1e-05
         scale = jnp.sqrt(np.float32(np.sqrt(DEGREES / (DEGREES - 1.0))) / power)
@@ -91,30 +95,41 @@
     return jnp.where(lane < HALF, turned, -turned).astype(jnp.bfloat16)
 
 
+def unpack_panels(panels, shard):
+    packed = shard + shard // 128 * MODES
+    w, st = [], []
+    for panel in panels:
+        for base in range(0, panel.shape[0], packed):
+            w.append(panel[base : base + shard, :])
+            st += [panel[base + shard + MODES * j : base + shard + MODES * (j + 1), :] for j in range(shard // 128)]
+    return w, st
+
+
+def coherence(re, im):
+    return jnp.maximum(re * re + im * im - np.float32(1.0 / (DEGREES - 1.0)), 0.0).astype(jnp.bfloat16)
+
+
 def image_kernel(shard, blocks, pieces, has_start, *refs):
     rows = refs[:blocks]
     panels = refs[blocks : blocks + pieces]
     starts = refs[blocks + pieces : 2 * blocks + pieces] if has_start else ()
     outs = refs[-blocks:]
-    packed = shard + shard // 128 * MODES
     u = jnp.concatenate([r[...] for r in rows], axis=0)
     t = twist(u)
     if has_start:
         acc = jnp.concatenate([r[...] for r in starts], axis=1)
     else:
         acc = jnp.zeros((MODES, u.shape[0]), jnp.float32)
-    for panel in panels:
-        for k in range(panel.shape[0] // packed):
-            base = k * packed
-            w = panel[base : base + shard, :]
-            re = dot(u, w, 1, 1)
-            im = dot(t, w, 1, 1)
-            c = jnp.maximum(re * re + im * im - np.float32(1.0 / (DEGREES - 1.0)), 0.0).astype(jnp.bfloat16)
-            st = jnp.concatenate(
-                [panel[base + shard + MODES * j : base + shard + MODES * (j + 1), :] for j in range(shard // 128)],
-                axis=1,
-            )
-            acc = acc + dot(st, c, 1, 1)
+    w, st = unpack_panels(panels, shard)
+    per = len(st) // len(w)
+    if u.shape[0] < 1024:
+        w = jnp.concatenate(w, axis=0)
+        c = coherence(dot(w, u, 1, 1), dot(w, t, 1, 1))
+        acc = acc + dot(jnp.concatenate(st, axis=1), c, 1, 0)
+    else:
+        for k in range(len(w)):
+            c = coherence(dot(u, w[k], 1, 1), dot(t, w[k], 1, 1))
+            acc = acc + dot(jnp.concatenate(st[k * per : (k + 1) * per], axis=1), c, 1, 1)
     width = rows[0].shape[0]
     for i in range(blocks):
         outs[i][...] = acc[:, i * width : (i + 1) * width]
@@ -157,40 +172,34 @@
     return jnp.concatenate([g[:, 32 * q : 32 * q + 32] for q in range(4)], axis=0)
 
 
-def gram_kernel(mine, theirs, image_ref, gram_ref):
+def gram_kernel(copies, mine, by_y, by_core, by_both, image_ref, gram_ref):
     half = mine.shape[1] // 2
-    own = mine[:, :half] + theirs[:, half:]
-    other = mine[:, half:] + theirs[:, :half]
+    own = mine[:, :half] + by_y[:, half:]
     image_ref[...] = own
-    g = dot(own, own, 1, 1, lax.Precision.HIGHEST) + dot(other, other, 1, 1, lax.Precision.HIGHEST)
-    gram_ref[...] = pack(g)
-
-
-def gram_of(mine, theirs):
+    sums = jnp.concatenate(
+        [
+            own,
+            mine[:, half:] + by_y[:, :half],
+            by_core[:, :half] + by_both[:, half:],
+            by_core[:, half:] + by_both[:, :half],
+        ],
+        axis=1,
+    )
+    g = pack(dot(sums, sums, 1, 1, lax.Precision.HIGHEST))
+    for k in range(copies):
+        gram_ref[k] = g
+
+
+def gram_of(parts, copies):
     return pl.pallas_call(
-        gram_kernel,
+        functools.partial(gram_kernel, copies),
         out_shape=[
-            jax.ShapeDtypeStruct((MODES, mine.shape[1] // 2), jnp.float32),
-            jax.ShapeDtypeStruct((8, 128), jnp.float32),
+            jax.ShapeDtypeStruct((MODES, parts[0].shape[1] // 2), jnp.float32),
+            jax.ShapeDtypeStruct((copies, 8, 128), jnp.float32),
         ],
         compiler_params=SMALL,
         name="gram",
-    )(mine, theirs)
-
-
-def copies_kernel(copies, a, b, out):
-    total = a[...] + b[...]
-    for k in range(copies):
-        out[k] = total
-
-
-def add_and_copy(a, b, copies):
-    return pl.pallas_call(
-        functools.partial(copies_kernel, copies),
-        out_shape=jax.ShapeDtypeStruct((copies, 8, 128), jnp.float32),
-        compiler_params=SMALL,
-        name="gram_copies",
-    )(a, b)
+    )(*parts)
 
 
 BLOCK = 4
@@ -300,8 +309,9 @@
     back = [to_x(away[k - 1], k) for k in (2, 1, 3)]
     near = image(home, [far, far_c], shard, near)
     mine = add([*near, *back])
-    img, gram = gram_of(mine, swap(mine, "y"))
-    grams = add_and_copy(gram, swap(gram, "c"), nx * nz)
+    quad = ("y", "c")
+    others = [lax.ppermute(mine, quad, [(i, i ^ k) for i in range(4)]) for k in (2, 1, 3)]
+    img, grams = gram_of([mine, *others], nx * nz)
     grams = lax.all_to_all(grams, ("x", "z"), 0, 0)
     return modes_of(grams, img, float(np.sqrt(neurons))).T
 

time: 75.7 us -> 75 us (level)
  Pallas kernels: 21.2 us -> 19.4 us
  blocking collectives: 16.6 us -> 17.5 us
  starting transfers between devices: 21.8 us -> 22.6 us
    ppermute x7 -> x5, waiting for transfers between devices: 5.4 us -> 1.27 us  [swap(): return lax.ppermute(v, axis, [(0, 1), (1, 0)])]
    ppermute x0 -> x3, waiting for transfers between devices: none -> 3.52 us  [local(): lax.ppermute(mine, quad, [(i, i ^ k) for i in range(4)])]
    ppermute x0 -> x3, starting transfers between devices: none -> 2.22 us  [local(): lax.ppermute(mine, quad, [(i, i ^ k) for i in range(4)])]
    ppermute x7 -> x5, starting transfers between devices: 3.65 us -> 2.24 us  [swap(): return lax.ppermute(v, axis, [(0, 1), (1, 0)])]
    pallas_call x7, Pallas kernels: 15.2 us -> 14.1 us  [image(): pl.pallas_call(functools.partial(image_kernel, shard, len(rows), len(pane...]
    all_to_all x1, blocking collectives: 16.6 us -> 17.5 us  [local(): grams = lax.all_to_all(grams, ('x', 'z'), 0, 0)]
  transfers between devices with their start and end apart: 16 -> 17, of which waited for: 8 -> 8; matrix products, arithmetic and copies ran while one was open for 0% -> 0% of each run, Pallas kernels for 18% -> 16%
where the time goes in v3:
time: 75 us; the launch traced here: 74.8 us
  starting transfers between devices  22.6 us (30%)
  Pallas kernels  19.4 us (26%)
  blocking collectives  17.5 us (23%)
  waiting for transfers between devices  15.1 us (20%)
    all_to_all x1, blocking collectives, local(): grams = lax.all_to_all(grams, ('x', 'z'), 0, 0)  17.5 us
    pallas_call x7, Pallas kernels, image(): pl.pallas_call(functools.partial(image_kernel, shard, len(rows), len(pane...  14.1 us
    ppermute x3, waiting for transfers between devices, both_ways(): return lax.ppermute(v, ('c', 'z'), pairs)  7.77 us
    ppermute x3, starting transfers between devices, both_ways(): return lax.ppermute(v, ('c', 'z'), pairs)  6.46 us
    ppermute x3, starting transfers between devices, to_x(): return lax.ppermute(v, 'x', [(i, (i + k) % nx) for i in range(nx)])  5.97 us
    ppermute x3, starting transfers between devices, from_x(): return lax.ppermute(v, 'x', [((i + k) % nx, i) for i in range(nx)])  5.73 us
    ppermute x3, waiting for transfers between devices, local(): lax.ppermute(mine, quad, [(i, i ^ k) for i in range(4)])  3.52 us
    pallas_call x1, Pallas kernels, local(): pl.pallas_call(spectra_kernel, out_shape=[jax.ShapeDtypeStruct((shard, CO...  2.89 us
  transfers between devices with their start and end apart: 17, of which 8 were waited for; matrix products, arithmetic and copies ran while one was open for 0% of the time, Pallas kernels for 16%

profile of v3, /device:TPU:16, one launch (start us, length us, event | category | flops | bytes accessed | tf_op | source)
XLA Modules:
  0.0 74.8 jit_solution(14602465187296227988)
XLA Ops:
  0.0 2.9 %spectra.1 = (bf16[256,128]{1,0:T(8,128)(2,1)S(1)}, bf16[320,128]{1,0:T(8,128)(2,1)S(1)}) custom-call(s32[256,8,128]{2,1,0:T(8,128)} %counts_hbm.1, bf16[32,256]{1,0:T(8,128)(2,1)} %bitcast.2, bf16[3,128,128]{2,1,0:T(8,128)(2,1)} %constant.2.clone.tables_hbm), custom_call_target="tpu_custom_call" | custom-call | tf_op jit(solution)/shard_map/spectra/pallas_call | solution.py:263
  4.3 3.3 %collective-permute-start.3 = (bf16[640,128]{1,0:T(8,128)(2,1)S(1)}, bf16[640,128]{1,0:T(8,128)(2,1)S(1)}, u32[]{:S(2)}, u32[]{:S(2)}) collective-permute-start(bf16[640,128]{1,0:T(8,128)(2,1)S(1)} %constant_dynamic-update-slice_fusion.2.refs_1_.refs_3_), channel_id=1, source_target_pairs={{0,2},{1,3},{2,4},{3,5},{4,6},{5,7},{6,0},{7,1},{32,38},{33,39},{3... | collective-permute-start | bytes 491528 | tf_op jit(solution)/shard_map/ppermute | solution.py:291
  7.6 1.9 %collective-permute-start.2 = (bf16[640,128]{1,0:T(8,128)(2,1)S(1)}, bf16[640,128]{1,0:T(8,128)(2,1)S(1)}, u32[]{:S(2)}, u32[]{:S(2)}) collective-permute-start(bf16[640,128]{1,0:T(8,128)(2,1)S(1)} %constant_dynamic-update-slice_fusion.2.refs_1_.refs_3_), channel_id=1, source_target_pairs={{0,1},{1,2},{2,3},{3,4},{4,5},{5,6},{6,7},{7,0},{32,39},{33,32},{3... | collective-permute-start | bytes 491528 | tf_op jit(solution)/shard_map/ppermute | solution.py:291
  9.5 1.3 %collective-permute-start = (bf16[256,128]{1,0:T(8,128)(2,1)S(1)}, bf16[256,128]{1,0:T(8,128)(2,1)S(1)}, u32[]{:S(2)}, u32[]{:S(2)}) collective-permute-start(bf16[256,128]{1,0:T(8,128)(2,1)S(1)} %get-tuple-element.21), channel_id=1, source_target_pairs={{0,64},{64,0},{1,65},{65,1},{2,66},{66,2},{3,67},{67,3},{4,68},{68... | collective-permute-start | bytes 196616 | tf_op jit(solution)/shard_map/ppermute | solution.py:287
  10.8 3.2 %collective-permute-done.3.refs_3_ = bf16[640,128]{1,0:T(8,128)(2,1)S(1)} collective-permute-done((bf16[640,128]{1,0:T(8,128)(2,1)S(1)}, bf16[640,128]{1,0:T(8,128)(2,1)S(1)}, u32[]{:S(2)}, u32[]{:S(2)}) %collective-permute-start.3) | collective-permute-done | bytes 163872 | tf_op jit(solution)/shard_map/ppermute | solution.py:291
  14.1 3.0 %collective-permute-done.2.refs_1_.refs_4_ = bf16[640,128]{1,0:T(8,128)(2,1)S(1)} collective-permute-done((bf16[640,128]{1,0:T(8,128)(2,1)S(1)}, bf16[640,128]{1,0:T(8,128)(2,1)S(1)}, u32[]{:S(2)}, u32[]{:S(2)}) %collective-permute-start.2) | collective-permute-done | bytes 163872 | tf_op jit(solution)/shard_map/ppermute | solution.py:291
  19.1 1.6 %collective-permute-start.10 = (bf16[512,128]{1,0:T(8,128)(2,1)S(1)}, bf16[512,128]{1,0:T(8,128)(2,1)S(1)}, u32[]{:S(2)}, u32[]{:S(2)}) collective-permute-start(bf16[512,128]{1,0:T(8,128)(2,1)S(1)} %constant_dynamic-update-slice_fusion.refs_0_), channel_id=1, source_target_pairs={{24,0},{0,8},{8,16},{16,24},{25,1},{1,9},{9,17},{17,25},{26,2},{2,... | collective-permute-start | bytes 393224 | tf_op jit(solution)/shard_map/ppermute | solution.py:281
  20.7 2.7 %collective-permute-start.9 = (bf16[512,128]{1,0:T(8,128)(2,1)S(1)}, bf16[512,128]{1,0:T(8,128)(2,1)S(1)}, u32[]{:S(2)}, u32[]{:S(2)}) collective-permute-start(bf16[512,128]{1,0:T(8,128)(2,1)S(1)} %constant_dynamic-update-slice_fusion.refs_0_), channel_id=1, source_target_pairs={{16,0},{24,8},{0,16},{8,24},{17,1},{25,9},{1,17},{9,25},{18,2},{26... | collective-permute-start | bytes 393224 | tf_op jit(solution)/shard_map/ppermute | solution.py:281
  23.4 1.4 %collective-permute-start.8 = (bf16[512,128]{1,0:T(8,128)(2,1)S(1)}, bf16[512,128]{1,0:T(8,128)(2,1)S(1)}, u32[]{:S(2)}, u32[]{:S(2)}) collective-permute-start(bf16[512,128]{1,0:T(8,128)(2,1)S(1)} %constant_dynamic-update-slice_fusion.refs_0_), channel_id=1, source_target_pairs={{8,0},{16,8},{24,16},{0,24},{9,1},{17,9},{25,17},{1,25},{10,2},{18... | collective-permute-start | bytes 393224 | tf_op jit(solution)/shard_map/ppermute | solution.py:281
  25.8 1.6 %collective-permute-done.4.refs_1_.refs_3_ = bf16[960,128]{1,0:T(8,128)(2,1)S(1)} collective-permute-done((bf16[960,128]{1,0:T(8,128)(2,1)S(1)}, bf16[960,128]{1,0:T(8,128)(2,1)S(1)}, u32[]{:S(2)}, u32[]{:S(2)}) %collective-permute-start.4) | collective-permute-done | bytes 245792 | tf_op jit(solution)/shard_map/ppermute | solution.py:291
  27.4 2.2 %collective-permute-done.9.refs_1_ = bf16[512,128]{1,0:T(8,128)(2,1)S(1)} collective-permute-done((bf16[512,128]{1,0:T(8,128)(2,1)S(1)}, bf16[512,128]{1,0:T(8,128)(2,1)S(1)}, u32[]{:S(2)}, u32[]{:S(2)}) %collective-permute-start.9) | collective-permute-done | bytes 131104 | tf_op jit(solution)/shard_map/ppermute | solution.py:281
  29.6 3.7 %shard_map.40 = (f32[32,512]{1,0:T(8,128)S(1)}, f32[32,512]{1,0:T(8,128)S(1)}, f32[32,512]{1,0:T(8,128)S(1)}) custom-call(bf16[512,128]{1,0:T(8,128)(2,1)S(1)} %collective-permute-done.8.refs_0_, bf16[512,128]{1,0:T(8,128)(2,1)S(1)} %collective-permute-done.9.refs_1_, bf16[512,128]{1,0:T(8,128)(2,1)S(1)} %collective-permute-done.10.refs_2_, ...), custom_call_target="tpu_custom_call" | custom-call | flops 1811939328 | bytes 884736 | tf_op jit(solution)/shard_map/pallas_call | solution.py:141
  33.3 2.5 %shard_map.41 = (f32[32,512]{1,0:T(8,128)S(1)}, f32[32,512]{1,0:T(8,128)S(1)}, f32[32,512]{1,0:T(8,128)S(1)}) custom-call(bf16[512,128]{1,0:T(8,128)(2,1)S(1)} %collective-permute-done.8.refs_0_, bf16[512,128]{1,0:T(8,128)(2,1)S(1)} %collective-permute-done.9.refs_1_, bf16[512,128]{1,0:T(8,128)(2,1)S(1)} %collective-permute-done.10.refs_2_, ...), custom_call_target="tpu_custom_call" | custom-call | flops 1207959552 | bytes 720896 | tf_op jit(solution)/shard_map/pallas_call | solution.py:141
  35.9 1.9 %shard_map.42 = (f32[32,512]{1,0:T(8,128)S(1)}, f32[32,512]{1,0:T(8,128)S(1)}, f32[32,512]{1,0:T(8,128)S(1)}) custom-call(bf16[512,128]{1,0:T(8,128)(2,1)S(1)} %collective-permute-done.8.refs_0_, bf16[512,128]{1,0:T(8,128)(2,1)S(1)} %collective-permute-done.9.refs_1_, bf16[512,128]{1,0:T(8,128)(2,1)S(1)} %collective-permute-done.10.refs_2_, ...), custom_call_target="tpu_custom_call" | custom-call | flops 905969664 | bytes 638976 | tf_op jit(solution)/shard_map/pallas_call | solution.py:141
  37.8 1.9 %shard_map.43 = (f32[32,512]{1,0:T(8,128)S(1)}, f32[32,512]{1,0:T(8,128)S(1)}, f32[32,512]{1,0:T(8,128)S(1)}) custom-call(bf16[512,128]{1,0:T(8,128)(2,1)S(1)} %collective-permute-done.8.refs_0_, bf16[512,128]{1,0:T(8,128)(2,1)S(1)} %collective-permute-done.9.refs_1_, bf16[512,128]{1,0:T(8,128)(2,1)S(1)} %collective-permute-done.10.refs_2_, ...), custom_call_target="tpu_custom_call" | custom-call | flops 905969664 | bytes 638976 | tf_op jit(solution)/shard_map/pallas_call | solution.py:141
  39.8 2.7 %collective-permute-start.11 = (f32[32,512]{1,0:T(8,128)S(1)}, f32[32,512]{1,0:T(8,128)S(1)}, u32[]{:S(2)}, u32[]{:S(2)}) collective-permute-start(f32[32,512]{1,0:T(8,128)S(1)} %get-tuple-element.32), channel_id=1, source_target_pairs={{0,16},{8,24},{16,0},{24,8},{1,17},{9,25},{17,1},{25,9},{2,18},{10... | collective-permute-start | bytes 196616 | tf_op jit(solution)/shard_map/ppermute | solution.py:284
  43.0 2.8 %collective-permute-start.13 = (f32[32,512]{1,0:T(8,128)S(1)}, f32[32,512]{1,0:T(8,128)S(1)}, u32[]{:S(2)}, u32[]{:S(2)}) collective-permute-start(f32[32,512]{1,0:T(8,128)S(1)} %get-tuple-element.34), channel_id=1, source_target_pairs={{0,24},{8,0},{16,8},{24,16},{1,25},{9,1},{17,9},{25,17},{2,26},{10... | collective-permute-start | bytes 196616 | tf_op jit(solution)/shard_map/ppermute | solution.py:284
  45.8 1.9 %shard_map.38.refs_3_ = f32[32,512]{1,0:T(8,128)S(1)} custom-call(bf16[512,128]{1,0:T(8,128)(2,1)S(1)} %constant_dynamic-update-slice_fusion.refs_0_, bf16[640,128]{1,0:T(8,128)(2,1)S(1)} %collective-permute-done.2.refs_1_.refs_4_, bf16[640,128]{1,0:T(8,128)(2,1)S(1)} %collective-permute-done.6.refs_2_.refs_5_, ...), custom_call_target="tpu_custom_call" | custom-call | flops 805306368 | bytes 786432 | tf_op jit(solution)/shard_map/pallas_call | solution.py:141
  47.6 1.4 %shard_map.39.refs_0_ = f32[32,512]{1,0:T(8,128)S(1)} custom-call(bf16[512,128]{1,0:T(8,128)(2,1)S(1)} %constant_dynamic-update-slice_fusion.refs_0_, bf16[960,128]{1,0:T(8,128)(2,1)S(1)} %collective-permute-done.4.refs_1_.refs_3_, bf16[960,128]{1,0:T(8,128)(2,1)S(1)} %collective-permute-done.5.refs_2_.refs_3_, f32[32,512]{1,0:T(8,128)S(1)} %shard_map.38.refs_3_), custom_call_target="tpu_custom_call" | custom-call | flops 603979776 | bytes 622592 | tf_op jit(solution)/shard_map/pallas_call | solution.py:141
  49.2 1.4 %collective-permute-start.15 = (f32[32,512]{1,0:T(8,128)S(1)}, f32[32,512]{1,0:T(8,128)S(1)}, u32[]{:S(2)}, u32[]{:S(2)}) collective-permute-start(f32[32,512]{1,0:T(8,128)S(1)} %add.1.mine), channel_id=1, source_target_pairs={{0,32},{32,0},{64,96},{96,64},{1,33},{33,1},{65,97},{97,65},{2,34}... | collective-permute-start | bytes 196616 | tf_op jit(solution)/shard_map/ppermute | solution.py:313
  51.4 2.1 %collective-permute-done.16.by_both = f32[32,512]{1,0:T(8,128)S(1)} collective-permute-done((f32[32,512]{1,0:T(8,128)S(1)}, f32[32,512]{1,0:T(8,128)S(1)}, u32[]{:S(2)}, u32[]{:S(2)}) %collective-permute-start.16) | collective-permute-done | bytes 65568 | tf_op jit(solution)/shard_map/ppermute | solution.py:313
  53.5 1.4 %collective-permute-done.14.by_y = f32[32,512]{1,0:T(8,128)S(1)} collective-permute-done((f32[32,512]{1,0:T(8,128)S(1)}, f32[32,512]{1,0:T(8,128)S(1)}, u32[]{:S(2)}, u32[]{:S(2)}) %collective-permute-start.14) | collective-permute-done | bytes 65568 | tf_op jit(solution)/shard_map/ppermute | solution.py:313
  55.2 17.5 %all_to_all.5.grams = f32[32,8,128]{2,1,0:T(8,128)S(1)} all-to-all(f32[32,8,128]{2,1,0:T(8,128)S(1)} %get-tuple-element.35), channel_id=1, replica_groups=mesh['freq'=2,'y'=2,'c'=2,'x'=4,'z'=8] {'x','z'}, dimensions={0} | all-to-all | bytes 262144 | tf_op jit(solution)/shard_map/all_to_all | solution.py:315
  72.8 2.1 %modes.1 = f32[32,256]{1,0:T(8,128)} custom-call(f32[32,8,128]{2,1,0:T(8,128)S(1)} %all_to_all.5.grams, f32[32,256]{1,0:T(8,128)S(1)} %get-tuple-element.36.image_ref), custom_call_target="tpu_custom_call" | custom-call | tf_op jit(solution)/shard_map/modes/pallas_call | solution.py:251
  (28 shorter events, 6.1 us)
Async XLA Ops:
  2.9 1.4 %collective-permute-start.1 = (bf16[320,128]{1,0:T(8,128)(2,1)S(1)}, bf16[320,128]{1,0:T(8,128)(2,1)S(1)}, u32[]{:S(2)}, u32[]{:S(2)}) collective-permute-start(bf16[320,128]{1,0:T(8,128)(2,1)S(1)} %get-tuple-element.22), channel_id=1, source_target_pairs={{0,32},{32,0},{1,33},{33,1},{2,34},{34,2},{3,35},{35,3},{4,36},{36... | collective-permute-start | bytes 245768 | tf_op jit(solution)/shard_map/ppermute | solution.py:287
  4.3 9.8 %collective-permute-start.3 = (bf16[640,128]{1,0:T(8,128)(2,1)S(1)}, bf16[640,128]{1,0:T(8,128)(2,1)S(1)}, u32[]{:S(2)}, u32[]{:S(2)}) collective-permute-start(bf16[640,128]{1,0:T(8,128)(2,1)S(1)} %constant_dynamic-update-slice_fusion.2.refs_1_.refs_3_), channel_id=1, source_target_pairs={{0,2},{1,3},{2,4},{3,5},{4,6},{5,7},{6,0},{7,1},{32,38},{33,39},{3... | collective-permute-start | bytes 491528 | tf_op jit(solution)/shard_map/ppermute | solution.py:291
  7.6 9.4 %collective-permute-start.2 = (bf16[640,128]{1,0:T(8,128)(2,1)S(1)}, bf16[640,128]{1,0:T(8,128)(2,1)S(1)}, u32[]{:S(2)}, u32[]{:S(2)}) collective-permute-start(bf16[640,128]{1,0:T(8,128)(2,1)S(1)} %constant_dynamic-update-slice_fusion.2.refs_1_.refs_3_), channel_id=1, source_target_pairs={{0,1},{1,2},{2,3},{3,4},{4,5},{5,6},{6,7},{7,0},{32,39},{33,32},{3... | collective-permute-start | bytes 491528 | tf_op jit(solution)/shard_map/ppermute | solution.py:291
  9.5 9.6 %collective-permute-start = (bf16[256,128]{1,0:T(8,128)(2,1)S(1)}, bf16[256,128]{1,0:T(8,128)(2,1)S(1)}, u32[]{:S(2)}, u32[]{:S(2)}) collective-permute-start(bf16[256,128]{1,0:T(8,128)(2,1)S(1)} %get-tuple-element.21), channel_id=1, source_target_pairs={{0,64},{64,0},{1,65},{65,1},{2,66},{66,2},{3,67},{67,3},{4,68},{68... | collective-permute-start | bytes 196616 | tf_op jit(solution)/shard_map/ppermute | solution.py:287
  17.0 10.4 %collective-permute-start.4 = (bf16[960,128]{1,0:T(8,128)(2,1)S(1)}, bf16[960,128]{1,0:T(8,128)(2,1)S(1)}, u32[]{:S(2)}, u32[]{:S(2)}) collective-permute-start(bf16[960,128]{1,0:T(8,128)(2,1)S(1)} %pad_maximum_fusion), channel_id=1, source_target_pairs={{0,2},{1,3},{2,4},{3,5},{4,6},{5,7},{6,0},{7,1},{32,38},{33,39},{3... | collective-permute-start | bytes 737288 | tf_op jit(solution)/shard_map/ppermute | solution.py:291
  18.2 11.4 %collective-permute-start.6 = (bf16[640,128]{1,0:T(8,128)(2,1)S(1)}, bf16[640,128]{1,0:T(8,128)(2,1)S(1)}, u32[]{:S(2)}, u32[]{:S(2)}) collective-permute-start(bf16[640,128]{1,0:T(8,128)(2,1)S(1)} %collective-permute-done.2.refs_1_.refs_4_), channel_id=1, source_target_pairs={{0,32},{32,0},{1,33},{33,1},{2,34},{34,2},{3,35},{35,3},{4,36},{36... | collective-permute-start | bytes 491528 | tf_op jit(solution)/shard_map/ppermute | solution.py:287
  19.1 6.7 %collective-permute-start.10 = (bf16[512,128]{1,0:T(8,128)(2,1)S(1)}, bf16[512,128]{1,0:T(8,128)(2,1)S(1)}, u32[]{:S(2)}, u32[]{:S(2)}) collective-permute-start(bf16[512,128]{1,0:T(8,128)(2,1)S(1)} %constant_dynamic-update-slice_fusion.refs_0_), channel_id=1, source_target_pairs={{24,0},{0,8},{8,16},{16,24},{25,1},{1,9},{9,17},{17,25},{26,2},{2,... | collective-permute-start | bytes 393224 | tf_op jit(solution)/shard_map/ppermute | solution.py:281
  20.7 8.9 %collective-permute-start.9 = (bf16[512,128]{1,0:T(8,128)(2,1)S(1)}, bf16[512,128]{1,0:T(8,128)(2,1)S(1)}, u32[]{:S(2)}, u32[]{:S(2)}) collective-permute-start(bf16[512,128]{1,0:T(8,128)(2,1)S(1)} %constant_dynamic-update-slice_fusion.refs_0_), channel_id=1, source_target_pairs={{16,0},{24,8},{0,16},{8,24},{17,1},{25,9},{1,17},{9,25},{18,2},{26... | collective-permute-start | bytes 393224 | tf_op jit(solution)/shard_map/ppermute | solution.py:281
  23.4 6.2 %collective-permute-start.8 = (bf16[512,128]{1,0:T(8,128)(2,1)S(1)}, bf16[512,128]{1,0:T(8,128)(2,1)S(1)}, u32[]{:S(2)}, u32[]{:S(2)}) collective-permute-start(bf16[512,128]{1,0:T(8,128)(2,1)S(1)} %constant_dynamic-update-slice_fusion.refs_0_), channel_id=1, source_target_pairs={{8,0},{16,8},{24,16},{0,24},{9,1},{17,9},{25,17},{1,25},{10,2},{18... | collective-permute-start | bytes 393224 | tf_op jit(solution)/shard_map/ppermute | solution.py:281
  25.8 7.5 %collective-permute-start.7 = (bf16[640,128]{1,0:T(8,128)(2,1)S(1)}, bf16[640,128]{1,0:T(8,128)(2,1)S(1)}, u32[]{:S(2)}, u32[]{:S(2)}) collective-permute-start(bf16[640,128]{1,0:T(8,128)(2,1)S(1)} %collective-permute-done.3.refs_3_), channel_id=1, source_target_pairs={{0,32},{32,0},{1,33},{33,1},{2,34},{34,2},{3,35},{35,3},{4,36},{36... | collective-permute-start | bytes 491528 | tf_op jit(solution)/shard_map/ppermute | solution.py:287
  27.4 10.4 %collective-permute-start.5 = (bf16[960,128]{1,0:T(8,128)(2,1)S(1)}, bf16[960,128]{1,0:T(8,128)(2,1)S(1)}, u32[]{:S(2)}, u32[]{:S(2)}) collective-permute-start(bf16[960,128]{1,0:T(8,128)(2,1)S(1)} %collective-permute-done.4.refs_1_.refs_3_), channel_id=1, source_target_pairs={{0,32},{32,0},{1,33},{33,1},{2,34},{34,2},{3,35},{35,3},{4,36},{36... | collective-permute-start | bytes 737288 | tf_op jit(solution)/shard_map/ppermute | solution.py:287
  39.8 9.3 %collective-permute-start.11 = (f32[32,512]{1,0:T(8,128)S(1)}, f32[32,512]{1,0:T(8,128)S(1)}, u32[]{:S(2)}, u32[]{:S(2)}) collective-permute-start(f32[32,512]{1,0:T(8,128)S(1)} %get-tuple-element.32), channel_id=1, source_target_pairs={{0,16},{8,24},{16,0},{24,8},{1,17},{9,25},{17,1},{25,9},{2,18},{10... | collective-permute-start | bytes 196616 | tf_op jit(solution)/shard_map/ppermute | solution.py:284
  42.5 6.6 %collective-permute-start.12 = (f32[32,512]{1,0:T(8,128)S(1)}, f32[32,512]{1,0:T(8,128)S(1)}, u32[]{:S(2)}, u32[]{:S(2)}) collective-permute-start(f32[32,512]{1,0:T(8,128)S(1)} %get-tuple-element.33), channel_id=1, source_target_pairs={{0,8},{8,16},{16,24},{24,0},{1,9},{9,17},{17,25},{25,1},{2,10},{10... | collective-permute-start | bytes 196616 | tf_op jit(solution)/shard_map/ppermute | solution.py:284
  43.0 6.1 %collective-permute-start.13 = (f32[32,512]{1,0:T(8,128)S(1)}, f32[32,512]{1,0:T(8,128)S(1)}, u32[]{:S(2)}, u32[]{:S(2)}) collective-permute-start(f32[32,512]{1,0:T(8,128)S(1)} %get-tuple-element.34), channel_id=1, source_target_pairs={{0,24},{8,0},{16,8},{24,16},{1,25},{9,1},{17,9},{25,17},{2,26},{10... | collective-permute-start | bytes 196616 | tf_op jit(solution)/shard_map/ppermute | solution.py:284
  49.1 4.3 %collective-permute-start.16 = (f32[32,512]{1,0:T(8,128)S(1)}, f32[32,512]{1,0:T(8,128)S(1)}, u32[]{:S(2)}, u32[]{:S(2)}) collective-permute-start(f32[32,512]{1,0:T(8,128)S(1)} %add.1.mine), channel_id=1, source_target_pairs={{0,96},{32,64},{64,32},{96,0},{1,97},{33,65},{65,33},{97,1},{2,98}... | collective-permute-start | bytes 196616 | tf_op jit(solution)/shard_map/ppermute | solution.py:313
  49.2 4.2 %collective-permute-start.15 = (f32[32,512]{1,0:T(8,128)S(1)}, f32[32,512]{1,0:T(8,128)S(1)}, u32[]{:S(2)}, u32[]{:S(2)}) collective-permute-start(f32[32,512]{1,0:T(8,128)S(1)} %add.1.mine), channel_id=1, source_target_pairs={{0,32},{32,0},{64,96},{96,64},{1,33},{33,1},{65,97},{97,65},{2,34}... | collective-permute-start | bytes 196616 | tf_op jit(solution)/shard_map/ppermute | solution.py:313
  50.6 4.3 %collective-permute-start.14 = (f32[32,512]{1,0:T(8,128)S(1)}, f32[32,512]{1,0:T(8,128)S(1)}, u32[]{:S(2)}, u32[]{:S(2)}) collective-permute-start(f32[32,512]{1,0:T(8,128)S(1)} %add.1.mine), channel_id=1, source_target_pairs={{0,64},{32,96},{64,0},{96,32},{1,65},{33,97},{65,1},{97,33},{2,66}... | collective-permute-start | bytes 196616 | tf_op jit(solution)/shard_map/ppermute | solution.py:313

commit v4 on v3

--- a/solution.py
+++ b/solution.py
@@ -47,44 +47,36 @@
     )
 
 
-CHUNKS = 2
-
-
 def spectra_kernel(counts_hbm, subspace_hbm, tables_hbm, u_ref, w_ref, counts, subspace, tables, sems):
-    rows = counts.shape[0]
-    part = rows // CHUNKS
-    copies = [pltpu.make_async_copy(tables_hbm, tables, sems.at[CHUNKS])]
-    for i in range(CHUNKS):
-        span = pl.ds(i * part, part)
-        copies.append(pltpu.make_async_copy(counts_hbm.at[span], counts.at[span], sems.at[i]))
-    copies.append(pltpu.make_async_copy(subspace_hbm, subspace, sems.at[CHUNKS + 1]))
-    for copy in copies:
+    rows = counts.shape[1]
+    first = pltpu.make_async_copy(tables_hbm, tables, sems.at[SEGS])
+    segments = [pltpu.make_async_copy(counts_hbm.at[:, s, :], counts.at[s], sems.at[s]) for s in range(SEGS)]
+    last = pltpu.make_async_copy(subspace_hbm, subspace, sems.at[SEGS + 1])
+    for copy in (first, *segments, last):
         copy.start()
     segment = lax.broadcasted_iota(jnp.int32, (EPOCH_STEPS, COLS), 1) % HALF // TAPERS
-    copies[0].wait()
+    first.wait()
     table = [
         [jnp.where(segment == s, tables[p].astype(jnp.float32), 0.0).astype(jnp.bfloat16) for p in range(3)]
         for s in range(SEGS)
     ]
-    for i in range(CHUNKS):
-        copies[1 + i].wait()
-        span = slice(i * part, (i + 1) * part)
-        upper = jnp.zeros((part, 2 * COLS), jnp.float32)
-        lower = jnp.zeros((part, COLS), jnp.float32)
-        for s in range(0, SEGS, 2):
-            x = [counts[span, s + j, :].astype(jnp.float32).astype(jnp.bfloat16) for j in range(2)]
-            x = jnp.concatenate(x, axis=1)
-            t = [jnp.concatenate([table[s][p], table[s + 1][p]], axis=0) for p in range(3)]
-            upper = upper + dot(x, jnp.concatenate(t[:2], axis=1), 1, 0)
-            lower = lower + dot(x, t[2], 1, 0)
-        total = upper[:, :COLS] + (upper[:, COLS:] + lower)
-        spectra = total.astype(jnp.bfloat16).astype(jnp.float32)
-        power = jnp.sum(spectra * spectra, axis=1, keepdims=True) + 1e-05
-        scale = jnp.sqrt(np.float32(np.sqrt(DEGREES / (DEGREES - 1.0))) / power)
-        u = (spectra * scale).astype(jnp.bfloat16)
-        u_ref[span, :] = u
-        w_ref[span, :] = u
-    copies[-1].wait()
+    upper = jnp.zeros((rows, 2 * COLS), jnp.float32)
+    lower = jnp.zeros((rows, COLS), jnp.float32)
+    for s in range(0, SEGS, 2):
+        segments[s].wait()
+        segments[s + 1].wait()
+        x = jnp.concatenate([counts[s + j].astype(jnp.float32).astype(jnp.bfloat16) for j in range(2)], axis=1)
+        t = [jnp.concatenate([table[s][p], table[s + 1][p]], axis=0) for p in range(3)]
+        upper = upper + dot(x, jnp.concatenate(t[:2], axis=1), 1, 0)
+        lower = lower + dot(x, t[2], 1, 0)
+    total = upper[:, :COLS] + (upper[:, COLS:] + lower)
+    spectra = total.astype(jnp.bfloat16).astype(jnp.float32)
+    power = jnp.sum(spectra * spectra, axis=1, keepdims=True) + 1e-05
+    scale = jnp.sqrt(np.float32(np.sqrt(DEGREES / (DEGREES - 1.0))) / power)
+    u = (spectra * scale).astype(jnp.bfloat16)
+    u_ref[...] = u
+    w_ref[0:rows, :] = u
+    last.wait()
     for j in range(rows // 128):
         w_ref[rows + MODES * j : rows + MODES * (j + 1), :] = subspace[:, 128 * j : 128 * (j + 1)]
 
@@ -268,10 +260,10 @@
         ],
         in_specs=[pl.BlockSpec(memory_space=pltpu.HBM)] * 3,
         scratch_shapes=[
-            pltpu.VMEM(counts.shape, jnp.int32),
+            pltpu.VMEM((SEGS, shard, EPOCH_STEPS), jnp.int32),
             pltpu.VMEM((MODES, shard), jnp.bfloat16),
             pltpu.VMEM((3, EPOCH_STEPS, COLS), jnp.bfloat16),
-            pltpu.SemaphoreType.DMA((CHUNKS + 2,)),
+            pltpu.SemaphoreType.DMA((SEGS + 2,)),
         ],
         compiler_params=LARGE,
         name="spectra",
@@ -295,19 +287,18 @@
     one = both_ways(pair, 1)
     two = both_ways(pair, 2)
     rows = [first] + [from_x(first, k) for k in range(1, nx)]
-    one_c = swap(one, "c")
-    two_c = swap(two, "c")
-    far = both_ways(jnp.concatenate([one, two[: w.shape[0]]], axis=0), 2)
+    ahead = jnp.concatenate([one, two], axis=0)
+    far = both_ways(ahead[: 3 * w.shape[0]], 2)
+    ahead_c = swap(ahead, "c")
     far_c = swap(far, "c")
     home, rest = rows[:1], rows[1:]
-    near = image(home, [pair], shard)
-    near = image(home, [one, one_c, two, two_c], shard, near)
-    away = image(rest, [pair, one, one_c], shard)
-    away = image(rest, [two, two_c], shard, away)
+    near = image(home, [pair, one], shard)
+    away = image(rest, [pair, ahead], shard)
+    away = image(rest, [ahead_c], shard, away)
     away = image(rest, [far], shard, away)
     away = image(rest, [far_c], shard, away)
     back = [to_x(away[k - 1], k) for k in (2, 1, 3)]
-    near = image(home, [far, far_c], shard, near)
+    near = image(home, [two, ahead_c, far, far_c], shard, near)
     mine = add([*near, *back])
     quad = ("y", "c")
     others = [lax.ppermute(mine, quad, [(i, i ^ k) for i in range(4)]) for k in (2, 1, 3)]

time: 75 us -> 73.9 us (0.985)
  starting transfers between devices: 22.6 us -> 19.3 us
  waiting for transfers between devices: 15.1 us -> 18.4 us
  Pallas kernels: 19.4 us -> 18.3 us
    ppermute x3, waiting for transfers between devices: 2.56 us -> 5.53 us  [from_x(): return lax.ppermute(v, 'x', [((i + k) % nx, i) for i in range(nx)])]
    ppermute x3, starting transfers between devices: 5.97 us -> 4.11 us  [to_x(): return lax.ppermute(v, 'x', [(i, (i + k) % nx) for i in range(nx)])]
    ppermute x3, starting transfers between devices: 5.73 us -> 4.52 us  [from_x(): return lax.ppermute(v, 'x', [((i + k) % nx, i) for i in range(nx)])]
    pallas_call x1, Pallas kernels: 2.89 us -> 2.04 us  [local(): pl.pallas_call(spectra_kernel, out_shape=[jax.ShapeDtypeStruct((shard, CO...]
    ppermute x5 -> x4, starting transfers between devices: 2.24 us -> 2.69 us  [swap(): return lax.ppermute(v, axis, [(0, 1), (1, 0)])]
    pallas_call x7 -> x6, Pallas kernels: 14.1 us -> 13.8 us  [image(): pl.pallas_call(functools.partial(image_kernel, shard, len(rows), len(pane...]
  transfers between devices with their start and end apart: 17 -> 16, of which waited for: 8 -> 9; matrix products, arithmetic and copies ran while one was open for 0% -> 0% of each run, Pallas kernels for 16% -> 16%
where the time goes in v4:
time: 73.9 us; the launch traced here: 73.8 us
  starting transfers between devices  19.3 us (26%)
  waiting for transfers between devices  18.4 us (25%)
  Pallas kernels  18.3 us (25%)
  blocking collectives  17.6 us (24%)
    all_to_all x1, blocking collectives, local(): grams = lax.all_to_all(grams, ('x', 'z'), 0, 0)  17.6 us
    pallas_call x6, Pallas kernels, image(): pl.pallas_call(functools.partial(image_kernel, shard, len(rows), len(pane...  13.8 us
    ppermute x3, waiting for transfers between devices, both_ways(): return lax.ppermute(v, ('c', 'z'), pairs)  8.51 us
    ppermute x3, starting transfers between devices, both_ways(): return lax.ppermute(v, ('c', 'z'), pairs)  5.79 us
    ppermute x3, waiting for transfers between devices, from_x(): return lax.ppermute(v, 'x', [((i + k) % nx, i) for i in range(nx)])  5.53 us
    ppermute x3, starting transfers between devices, from_x(): return lax.ppermute(v, 'x', [((i + k) % nx, i) for i in range(nx)])  4.52 us
    ppermute x3, starting transfers between devices, to_x(): return lax.ppermute(v, 'x', [(i, (i + k) % nx) for i in range(nx)])  4.11 us
    ppermute x3, waiting for transfers between devices, local(): lax.ppermute(mine, quad, [(i, i ^ k) for i in range(4)])  2.85 us
  transfers between devices with their start and end apart: 16, of which 9 were waited for; matrix products, arithmetic and copies ran while one was open for 0% of the time, Pallas kernels for 16%

profile of v4, /device:TPU:16, one launch (start us, length us, event | category | flops | bytes accessed | tf_op | source)
XLA Modules:
  0.0 73.8 jit_solution(4145896751444838770)
XLA Ops:
  0.0 2.0 %spectra.1 = (bf16[256,128]{1,0:T(8,128)(2,1)S(1)}, bf16[320,128]{1,0:T(8,128)(2,1)S(1)}) custom-call(s32[256,8,128]{2,1,0:T(8,128)} %counts_hbm.1, bf16[32,256]{1,0:T(8,128)(2,1)} %bitcast.2, bf16[3,128,128]{2,1,0:T(8,128)(2,1)} %constant.2.clone.tables_hbm), custom_call_target="tpu_custom_call" | custom-call | tf_op jit(solution)/shard_map/spectra/pallas_call | solution.py:255
  2.2 1.2 %collective-permute-done.1 = bf16[320,128]{1,0:T(8,128)(2,1)S(1)} collective-permute-done((bf16[320,128]{1,0:T(8,128)(2,1)S(1)}, bf16[320,128]{1,0:T(8,128)(2,1)S(1)}, u32[]{:S(2)}, u32[]{:S(2)}) %collective-permute-start.1) | collective-permute-done | bytes 81952 | tf_op jit(solution)/shard_map/ppermute | solution.py:279
  3.4 2.0 %collective-permute-start.3 = (bf16[640,128]{1,0:T(8,128)(2,1)S(1)}, bf16[640,128]{1,0:T(8,128)(2,1)S(1)}, u32[]{:S(2)}, u32[]{:S(2)}) collective-permute-start(bf16[640,128]{1,0:T(8,128)(2,1)S(1)} %constant_dynamic-update-slice_fusion.2.refs_1_.refs_3_), channel_id=1, source_target_pairs={{0,1},{1,2},{2,3},{3,4},{4,5},{5,6},{6,7},{7,0},{32,39},{33,32},{3... | collective-permute-start | bytes 491528 | tf_op jit(solution)/shard_map/ppermute | solution.py:283
  5.4 3.3 %collective-permute-start.2 = (bf16[640,128]{1,0:T(8,128)(2,1)S(1)}, bf16[640,128]{1,0:T(8,128)(2,1)S(1)}, u32[]{:S(2)}, u32[]{:S(2)}) collective-permute-start(bf16[640,128]{1,0:T(8,128)(2,1)S(1)} %constant_dynamic-update-slice_fusion.2.refs_1_.refs_3_), channel_id=1, source_target_pairs={{0,2},{1,3},{2,4},{3,5},{4,6},{5,7},{6,0},{7,1},{32,38},{33,39},{3... | collective-permute-start | bytes 491528 | tf_op jit(solution)/shard_map/ppermute | solution.py:283
  8.7 1.3 %collective-permute-start = (bf16[256,128]{1,0:T(8,128)(2,1)S(1)}, bf16[256,128]{1,0:T(8,128)(2,1)S(1)}, u32[]{:S(2)}, u32[]{:S(2)}) collective-permute-start(bf16[256,128]{1,0:T(8,128)(2,1)S(1)} %get-tuple-element.21), channel_id=1, source_target_pairs={{0,64},{64,0},{1,65},{65,1},{2,66},{66,2},{3,67},{67,3},{4,68},{68... | collective-permute-start | bytes 196616 | tf_op jit(solution)/shard_map/ppermute | solution.py:279
  10.0 2.7 %collective-permute-done.3.refs_2_ = bf16[640,128]{1,0:T(8,128)(2,1)S(1)} collective-permute-done((bf16[640,128]{1,0:T(8,128)(2,1)S(1)}, bf16[640,128]{1,0:T(8,128)(2,1)S(1)}, u32[]{:S(2)}, u32[]{:S(2)}) %collective-permute-start.3) | collective-permute-done | bytes 163872 | tf_op jit(solution)/shard_map/ppermute | solution.py:283
  12.7 3.7 %collective-permute-done.2.refs_1_ = bf16[640,128]{1,0:T(8,128)(2,1)S(1)} collective-permute-done((bf16[640,128]{1,0:T(8,128)(2,1)S(1)}, bf16[640,128]{1,0:T(8,128)(2,1)S(1)}, u32[]{:S(2)}, u32[]{:S(2)}) %collective-permute-start.2) | collective-permute-done | bytes 163872 | tf_op jit(solution)/shard_map/ppermute | solution.py:283
  17.0 2.8 %collective-permute-start.7 = (bf16[512,128]{1,0:T(8,128)(2,1)S(1)}, bf16[512,128]{1,0:T(8,128)(2,1)S(1)}, u32[]{:S(2)}, u32[]{:S(2)}) collective-permute-start(bf16[512,128]{1,0:T(8,128)(2,1)S(1)} %constant_dynamic-update-slice_fusion.refs_0_), channel_id=1, source_target_pairs={{8,0},{16,8},{24,16},{0,24},{9,1},{17,9},{25,17},{1,25},{10,2},{18... | collective-permute-start | bytes 393224 | tf_op jit(solution)/shard_map/ppermute | solution.py:273
  20.7 0.9 %collective-permute-start.9 = (bf16[512,128]{1,0:T(8,128)(2,1)S(1)}, bf16[512,128]{1,0:T(8,128)(2,1)S(1)}, u32[]{:S(2)}, u32[]{:S(2)}) collective-permute-start(bf16[512,128]{1,0:T(8,128)(2,1)S(1)} %constant_dynamic-update-slice_fusion.refs_0_), channel_id=1, source_target_pairs={{24,0},{0,8},{8,16},{16,24},{25,1},{1,9},{9,17},{17,25},{26,2},{2,... | collective-permute-start | bytes 393224 | tf_op jit(solution)/shard_map/ppermute | solution.py:273
  21.6 1.3 %collective-permute-start.4 = (bf16[1280,128]{1,0:T(8,128)(2,1)S(1)}, bf16[1280,128]{1,0:T(8,128)(2,1)S(1)}, u32[]{:S(2)}, u32[]{:S(2)}) collective-permute-start(bf16[1280,128]{1,0:T(8,128)(2,1)S(1)} %constant_dynamic-update-slice_fusion.4.refs_4_), channel_id=1, source_target_pairs={{0,32},{32,0},{1,33},{33,1},{2,34},{34,2},{3,35},{35,3},{4,36},{36... | collective-permute-start | bytes 983048 | tf_op jit(solution)/shard_map/ppermute | solution.py:279
  22.9 2.1 %collective-permute-done.5.refs_3_ = bf16[960,128]{1,0:T(8,128)(2,1)S(1)} collective-permute-done((bf16[960,128]{1,0:T(8,128)(2,1)S(1)}, bf16[960,128]{1,0:T(8,128)(2,1)S(1)}, u32[]{:S(2)}, u32[]{:S(2)}) %collective-permute-start.5) | collective-permute-done | bytes 245792 | tf_op jit(solution)/shard_map/ppermute | solution.py:283
  25.0 2.0 %collective-permute-done.8.refs_1_ = bf16[512,128]{1,0:T(8,128)(2,1)S(1)} collective-permute-done((bf16[512,128]{1,0:T(8,128)(2,1)S(1)}, bf16[512,128]{1,0:T(8,128)(2,1)S(1)}, u32[]{:S(2)}, u32[]{:S(2)}) %collective-permute-start.8) | collective-permute-done | bytes 131104 | tf_op jit(solution)/shard_map/ppermute | solution.py:273
  26.9 3.6 %collective-permute-done.9.refs_2_ = bf16[512,128]{1,0:T(8,128)(2,1)S(1)} collective-permute-done((bf16[512,128]{1,0:T(8,128)(2,1)S(1)}, bf16[512,128]{1,0:T(8,128)(2,1)S(1)}, u32[]{:S(2)}, u32[]{:S(2)}) %collective-permute-start.9) | collective-permute-done | bytes 131104 | tf_op jit(solution)/shard_map/ppermute | solution.py:273
  30.5 3.7 %shard_map.39 = (f32[32,512]{1,0:T(8,128)S(1)}, f32[32,512]{1,0:T(8,128)S(1)}, f32[32,512]{1,0:T(8,128)S(1)}) custom-call(bf16[512,128]{1,0:T(8,128)(2,1)S(1)} %collective-permute-done.7.refs_0_, bf16[512,128]{1,0:T(8,128)(2,1)S(1)} %collective-permute-done.8.refs_1_, bf16[512,128]{1,0:T(8,128)(2,1)S(1)} %collective-permute-done.9.refs_2_, ...), custom_call_target="tpu_custom_call" | custom-call | flops 1811939328 | bytes 884736 | tf_op jit(solution)/shard_map/pallas_call | solution.py:133
  34.2 1.0 %shard_map.37.refs_5_ = f32[32,512]{1,0:T(8,128)S(1)} custom-call(bf16[512,128]{1,0:T(8,128)(2,1)S(1)} %constant_dynamic-update-slice_fusion.refs_0_, bf16[640,128]{1,0:T(8,128)(2,1)S(1)} %constant_dynamic-update-slice_fusion.2.refs_1_.refs_3_, bf16[640,128]{1,0:T(8,128)(2,1)S(1)} %collective-permute-done.3.refs_2_), custom_call_target="tpu_custom_call" | custom-call | flops 402653184 | bytes 458752 | tf_op jit(solution)/shard_map/pallas_call | solution.py:133
  35.2 2.5 %shard_map.40 = (f32[32,512]{1,0:T(8,128)S(1)}, f32[32,512]{1,0:T(8,128)S(1)}, f32[32,512]{1,0:T(8,128)S(1)}) custom-call(bf16[512,128]{1,0:T(8,128)(2,1)S(1)} %collective-permute-done.7.refs_0_, bf16[512,128]{1,0:T(8,128)(2,1)S(1)} %collective-permute-done.8.refs_1_, bf16[512,128]{1,0:T(8,128)(2,1)S(1)} %collective-permute-done.9.refs_2_, ...), custom_call_target="tpu_custom_call" | custom-call | flops 1207959552 | bytes 720896 | tf_op jit(solution)/shard_map/pallas_call | solution.py:133
  37.7 1.9 %shard_map.41 = (f32[32,512]{1,0:T(8,128)S(1)}, f32[32,512]{1,0:T(8,128)S(1)}, f32[32,512]{1,0:T(8,128)S(1)}) custom-call(bf16[512,128]{1,0:T(8,128)(2,1)S(1)} %collective-permute-done.7.refs_0_, bf16[512,128]{1,0:T(8,128)(2,1)S(1)} %collective-permute-done.8.refs_1_, bf16[512,128]{1,0:T(8,128)(2,1)S(1)} %collective-permute-done.9.refs_2_, ...), custom_call_target="tpu_custom_call" | custom-call | flops 905969664 | bytes 638976 | tf_op jit(solution)/shard_map/pallas_call | solution.py:133
  39.7 1.9 %shard_map.42 = (f32[32,512]{1,0:T(8,128)S(1)}, f32[32,512]{1,0:T(8,128)S(1)}, f32[32,512]{1,0:T(8,128)S(1)}) custom-call(bf16[512,128]{1,0:T(8,128)(2,1)S(1)} %collective-permute-done.7.refs_0_, bf16[512,128]{1,0:T(8,128)(2,1)S(1)} %collective-permute-done.8.refs_1_, bf16[512,128]{1,0:T(8,128)(2,1)S(1)} %collective-permute-done.9.refs_2_, ...), custom_call_target="tpu_custom_call" | custom-call | flops 905969664 | bytes 638976 | tf_op jit(solution)/shard_map/pallas_call | solution.py:133
  42.5 3.2 %collective-permute-start.12 = (f32[32,512]{1,0:T(8,128)S(1)}, f32[32,512]{1,0:T(8,128)S(1)}, u32[]{:S(2)}, u32[]{:S(2)}) collective-permute-start(f32[32,512]{1,0:T(8,128)S(1)} %get-tuple-element.34), channel_id=1, source_target_pairs={{0,24},{8,0},{16,8},{24,16},{1,25},{9,1},{17,9},{25,17},{2,26},{10... | collective-permute-start | bytes 196616 | tf_op jit(solution)/shard_map/ppermute | solution.py:276
  45.7 2.7 %shard_map.38.refs_0_ = f32[32,512]{1,0:T(8,128)S(1)} custom-call(bf16[512,128]{1,0:T(8,128)(2,1)S(1)} %constant_dynamic-update-slice_fusion.refs_0_, bf16[640,128]{1,0:T(8,128)(2,1)S(1)} %collective-permute-done.2.refs_1_, bf16[1280,128]{1,0:T(8,128)(2,1)S(1)} %collective-permute-done.4.refs_2_.refs_3_, ...), custom_call_target="tpu_custom_call" | custom-call | flops 1207959552 | bytes 1114112 | tf_op jit(solution)/shard_map/pallas_call | solution.py:133
  48.7 1.4 %collective-permute-start.13 = (f32[32,512]{1,0:T(8,128)S(1)}, f32[32,512]{1,0:T(8,128)S(1)}, u32[]{:S(2)}, u32[]{:S(2)}) collective-permute-start(f32[32,512]{1,0:T(8,128)S(1)} %add.1.mine), channel_id=1, source_target_pairs={{0,64},{32,96},{64,0},{96,32},{1,65},{33,97},{65,1},{97,33},{2,66}... | collective-permute-start | bytes 196616 | tf_op jit(solution)/shard_map/ppermute | solution.py:304
  51.0 2.1 %collective-permute-done.13.by_y = f32[32,512]{1,0:T(8,128)S(1)} collective-permute-done((f32[32,512]{1,0:T(8,128)S(1)}, f32[32,512]{1,0:T(8,128)S(1)}, u32[]{:S(2)}, u32[]{:S(2)}) %collective-permute-start.13) | collective-permute-done | bytes 65568 | tf_op jit(solution)/shard_map/ppermute | solution.py:304
  54.1 17.6 %all_to_all.5.grams = f32[32,8,128]{2,1,0:T(8,128)S(1)} all-to-all(f32[32,8,128]{2,1,0:T(8,128)S(1)} %get-tuple-element.35), channel_id=1, replica_groups=mesh['freq'=2,'y'=2,'c'=2,'x'=4,'z'=8] {'x','z'}, dimensions={0} | all-to-all | bytes 262144 | tf_op jit(solution)/shard_map/all_to_all | solution.py:306
  71.7 2.1 %modes.1 = f32[32,256]{1,0:T(8,128)} custom-call(f32[32,8,128]{2,1,0:T(8,128)S(1)} %all_to_all.5.grams, f32[32,256]{1,0:T(8,128)S(1)} %get-tuple-element.36.image_ref), custom_call_target="tpu_custom_call" | custom-call | tf_op jit(solution)/shard_map/modes/pallas_call | solution.py:243
  (26 shorter events, 4.6 us)
Async XLA Ops:
  2.1 1.4 %collective-permute-start.1 = (bf16[320,128]{1,0:T(8,128)(2,1)S(1)}, bf16[320,128]{1,0:T(8,128)(2,1)S(1)}, u32[]{:S(2)}, u32[]{:S(2)}) collective-permute-start(bf16[320,128]{1,0:T(8,128)(2,1)S(1)} %get-tuple-element.22), channel_id=1, source_target_pairs={{0,32},{32,0},{1,33},{33,1},{2,34},{34,2},{3,35},{35,3},{4,36},{36... | collective-permute-start | bytes 245768 | tf_op jit(solution)/shard_map/ppermute | solution.py:279
  3.4 9.2 %collective-permute-start.3 = (bf16[640,128]{1,0:T(8,128)(2,1)S(1)}, bf16[640,128]{1,0:T(8,128)(2,1)S(1)}, u32[]{:S(2)}, u32[]{:S(2)}) collective-permute-start(bf16[640,128]{1,0:T(8,128)(2,1)S(1)} %constant_dynamic-update-slice_fusion.2.refs_1_.refs_3_), channel_id=1, source_target_pairs={{0,1},{1,2},{2,3},{3,4},{4,5},{5,6},{6,7},{7,0},{32,39},{33,32},{3... | collective-permute-start | bytes 491528 | tf_op jit(solution)/shard_map/ppermute | solution.py:283
  5.4 11.0 %collective-permute-start.2 = (bf16[640,128]{1,0:T(8,128)(2,1)S(1)}, bf16[640,128]{1,0:T(8,128)(2,1)S(1)}, u32[]{:S(2)}, u32[]{:S(2)}) collective-permute-start(bf16[640,128]{1,0:T(8,128)(2,1)S(1)} %constant_dynamic-update-slice_fusion.2.refs_1_.refs_3_), channel_id=1, source_target_pairs={{0,2},{1,3},{2,4},{3,5},{4,6},{5,7},{6,0},{7,1},{32,38},{33,39},{3... | collective-permute-start | bytes 491528 | tf_op jit(solution)/shard_map/ppermute | solution.py:283
  8.7 8.3 %collective-permute-start = (bf16[256,128]{1,0:T(8,128)(2,1)S(1)}, bf16[256,128]{1,0:T(8,128)(2,1)S(1)}, u32[]{:S(2)}, u32[]{:S(2)}) collective-permute-start(bf16[256,128]{1,0:T(8,128)(2,1)S(1)} %get-tuple-element.21), channel_id=1, source_target_pairs={{0,64},{64,0},{1,65},{65,1},{2,66},{66,2},{3,67},{67,3},{4,68},{68... | collective-permute-start | bytes 196616 | tf_op jit(solution)/shard_map/ppermute | solution.py:279
  16.5 8.5 %collective-permute-start.5 = (bf16[960,128]{1,0:T(8,128)(2,1)S(1)}, bf16[960,128]{1,0:T(8,128)(2,1)S(1)}, u32[]{:S(2)}, u32[]{:S(2)}) collective-permute-start(bf16[960,128]{1,0:T(8,128)(2,1)S(1)} %slice.4), channel_id=1, source_target_pairs={{0,2},{1,3},{2,4},{3,5},{4,6},{5,7},{6,0},{7,1},{32,38},{33,39},{3... | collective-permute-start | bytes 737288 | tf_op jit(solution)/shard_map/ppermute | solution.py:283
  17.0 7.9 %collective-permute-start.7 = (bf16[512,128]{1,0:T(8,128)(2,1)S(1)}, bf16[512,128]{1,0:T(8,128)(2,1)S(1)}, u32[]{:S(2)}, u32[]{:S(2)}) collective-permute-start(bf16[512,128]{1,0:T(8,128)(2,1)S(1)} %constant_dynamic-update-slice_fusion.refs_0_), channel_id=1, source_target_pairs={{8,0},{16,8},{24,16},{0,24},{9,1},{17,9},{25,17},{1,25},{10,2},{18... | collective-permute-start | bytes 393224 | tf_op jit(solution)/shard_map/ppermute | solution.py:273
  19.9 7.1 %collective-permute-start.8 = (bf16[512,128]{1,0:T(8,128)(2,1)S(1)}, bf16[512,128]{1,0:T(8,128)(2,1)S(1)}, u32[]{:S(2)}, u32[]{:S(2)}) collective-permute-start(bf16[512,128]{1,0:T(8,128)(2,1)S(1)} %constant_dynamic-update-slice_fusion.refs_0_), channel_id=1, source_target_pairs={{16,0},{24,8},{0,16},{8,24},{17,1},{25,9},{1,17},{9,25},{18,2},{26... | collective-permute-start | bytes 393224 | tf_op jit(solution)/shard_map/ppermute | solution.py:273
  20.7 9.8 %collective-permute-start.9 = (bf16[512,128]{1,0:T(8,128)(2,1)S(1)}, bf16[512,128]{1,0:T(8,128)(2,1)S(1)}, u32[]{:S(2)}, u32[]{:S(2)}) collective-permute-start(bf16[512,128]{1,0:T(8,128)(2,1)S(1)} %constant_dynamic-update-slice_fusion.refs_0_), channel_id=1, source_target_pairs={{24,0},{0,8},{8,16},{16,24},{25,1},{1,9},{9,17},{17,25},{26,2},{2,... | collective-permute-start | bytes 393224 | tf_op jit(solution)/shard_map/ppermute | solution.py:273
  21.6 13.7 %collective-permute-start.4 = (bf16[1280,128]{1,0:T(8,128)(2,1)S(1)}, bf16[1280,128]{1,0:T(8,128)(2,1)S(1)}, u32[]{:S(2)}, u32[]{:S(2)}) collective-permute-start(bf16[1280,128]{1,0:T(8,128)(2,1)S(1)} %constant_dynamic-update-slice_fusion.4.refs_4_), channel_id=1, source_target_pairs={{0,32},{32,0},{1,33},{33,1},{2,34},{34,2},{3,35},{35,3},{4,36},{36... | collective-permute-start | bytes 983048 | tf_op jit(solution)/shard_map/ppermute | solution.py:279
  25.0 14.7 %collective-permute-start.6 = (bf16[960,128]{1,0:T(8,128)(2,1)S(1)}, bf16[960,128]{1,0:T(8,128)(2,1)S(1)}, u32[]{:S(2)}, u32[]{:S(2)}) collective-permute-start(bf16[960,128]{1,0:T(8,128)(2,1)S(1)} %collective-permute-done.5.refs_3_), channel_id=1, source_target_pairs={{0,32},{32,0},{1,33},{33,1},{2,34},{34,2},{3,35},{35,3},{4,36},{36... | collective-permute-start | bytes 737288 | tf_op jit(solution)/shard_map/ppermute | solution.py:279
  41.6 6.8 %collective-permute-start.10 = (f32[32,512]{1,0:T(8,128)S(1)}, f32[32,512]{1,0:T(8,128)S(1)}, u32[]{:S(2)}, u32[]{:S(2)}) collective-permute-start(f32[32,512]{1,0:T(8,128)S(1)} %get-tuple-element.32), channel_id=1, source_target_pairs={{0,16},{8,24},{16,0},{24,8},{1,17},{9,25},{17,1},{25,9},{2,18},{10... | collective-permute-start | bytes 196616 | tf_op jit(solution)/shard_map/ppermute | solution.py:276
  42.5 6.2 %collective-permute-start.11 = (f32[32,512]{1,0:T(8,128)S(1)}, f32[32,512]{1,0:T(8,128)S(1)}, u32[]{:S(2)}, u32[]{:S(2)}) collective-permute-start(f32[32,512]{1,0:T(8,128)S(1)} %get-tuple-element.33), channel_id=1, source_target_pairs={{0,8},{8,16},{16,24},{24,0},{1,9},{9,17},{17,25},{25,1},{2,10},{10... | collective-permute-start | bytes 196616 | tf_op jit(solution)/shard_map/ppermute | solution.py:276
  42.5 6.2 %collective-permute-start.12 = (f32[32,512]{1,0:T(8,128)S(1)}, f32[32,512]{1,0:T(8,128)S(1)}, u32[]{:S(2)}, u32[]{:S(2)}) collective-permute-start(f32[32,512]{1,0:T(8,128)S(1)} %get-tuple-element.34), channel_id=1, source_target_pairs={{0,24},{8,0},{16,8},{24,16},{1,25},{9,1},{17,9},{25,17},{2,26},{10... | collective-permute-start | bytes 196616 | tf_op jit(solution)/shard_map/ppermute | solution.py:276
  48.7 4.4 %collective-permute-start.13 = (f32[32,512]{1,0:T(8,128)S(1)}, f32[32,512]{1,0:T(8,128)S(1)}, u32[]{:S(2)}, u32[]{:S(2)}) collective-permute-start(f32[32,512]{1,0:T(8,128)S(1)} %add.1.mine), channel_id=1, source_target_pairs={{0,64},{32,96},{64,0},{96,32},{1,65},{33,97},{65,1},{97,33},{2,66}... | collective-permute-start | bytes 196616 | tf_op jit(solution)/shard_map/ppermute | solution.py:304
  50.1 3.0 %collective-permute-start.14 = (f32[32,512]{1,0:T(8,128)S(1)}, f32[32,512]{1,0:T(8,128)S(1)}, u32[]{:S(2)}, u32[]{:S(2)}) collective-permute-start(f32[32,512]{1,0:T(8,128)S(1)} %add.1.mine), channel_id=1, source_target_pairs={{0,32},{32,0},{64,96},{96,64},{1,33},{33,1},{65,97},{97,65},{2,34}... | collective-permute-start | bytes 196616 | tf_op jit(solution)/shard_map/ppermute | solution.py:304
  50.1 3.7 %collective-permute-start.15 = (f32[32,512]{1,0:T(8,128)S(1)}, f32[32,512]{1,0:T(8,128)S(1)}, u32[]{:S(2)}, u32[]{:S(2)}) collective-permute-start(f32[32,512]{1,0:T(8,128)S(1)} %add.1.mine), channel_id=1, source_target_pairs={{0,96},{32,64},{64,32},{96,0},{1,97},{33,65},{65,33},{97,1},{2,98}... | collective-permute-start | bytes 196616 | tf_op jit(solution)/shard_map/ppermute | solution.py:304

commit v5 on v4

--- a/solution.py
+++ b/solution.py
@@ -296,8 +296,9 @@
     away = image(rest, [pair, ahead], shard)
     away = image(rest, [ahead_c], shard, away)
     away = image(rest, [far], shard, away)
-    away = image(rest, [far_c], shard, away)
-    back = [to_x(away[k - 1], k) for k in (2, 1, 3)]
+    (two_away,) = image(rest[1:2], [far_c], shard, away[1:2])
+    one_away, three_away = image(rest[0::2], [far_c], shard, away[0::2])
+    back = [to_x(two_away, 2), to_x(one_away, 1), to_x(three_away, 3)]
     near = image(home, [two, ahead_c, far, far_c], shard, near)
     mine = add([*near, *back])
     quad = ("y", "c")

time: 73.9 us -> 74.1 us (level)
  waiting for transfers between devices: 18.4 us -> 15.3 us
  starting transfers between devices: 19.3 us -> 21.6 us
    ppermute x3, waiting for transfers between devices: 5.53 us -> 3.27 us  [from_x(): return lax.ppermute(v, 'x', [((i + k) % nx, i) for i in range(nx)])]
    ppermute x3, starting transfers between devices: 4.11 us -> 5.8 us  [to_x(): return lax.ppermute(v, 'x', [(i, (i + k) % nx) for i in range(nx)])]
    pallas_call x6 -> x7, Pallas kernels: 13.8 us -> 14.1 us  [image(): pl.pallas_call(functools.partial(image_kernel, shard, len(rows), len(pane...]
  transfers between devices with their start and end apart: 16 -> 16, of which waited for: 9 -> 8; matrix products, arithmetic and copies ran while one was open for 0% -> 0% of each run, Pallas kernels for 16% -> 18%
where the time goes in v5:
time: 74.1 us; the launch traced here: 74 us
  starting transfers between devices  21.6 us (29%)
  Pallas kernels  18.6 us (25%)
  blocking collectives  18.2 us (25%)
  waiting for transfers between devices  15.3 us (21%)
    all_to_all x1, blocking collectives, local(): grams = lax.all_to_all(grams, ('x', 'z'), 0, 0)  18.2 us
    pallas_call x7, Pallas kernels, image(): pl.pallas_call(functools.partial(image_kernel, shard, len(rows), len(pane...  14.1 us
    ppermute x3, waiting for transfers between devices, both_ways(): return lax.ppermute(v, ('c', 'z'), pairs)  7.9 us
    ppermute x3, starting transfers between devices, to_x(): return lax.ppermute(v, 'x', [(i, (i + k) % nx) for i in range(nx)])  5.8 us
    ppermute x3, starting transfers between devices, both_ways(): return lax.ppermute(v, ('c', 'z'), pairs)  5.79 us
    ppermute x3, starting transfers between devices, from_x(): return lax.ppermute(v, 'x', [((i + k) % nx, i) for i in range(nx)])  5.13 us
    ppermute x3, waiting for transfers between devices, from_x(): return lax.ppermute(v, 'x', [((i + k) % nx, i) for i in range(nx)])  3.27 us
    ppermute x3, waiting for transfers between devices, local(): lax.ppermute(mine, quad, [(i, i ^ k) for i in range(4)])  2.85 us
  transfers between devices with their start and end apart: 16, of which 8 were waited for; matrix products, arithmetic and copies ran while one was open for 0% of the time, Pallas kernels for 18%

profile of v5, /device:TPU:16, one launch (start us, length us, event | category | flops | bytes accessed | tf_op | source)
XLA Modules:
  0.0 74.0 jit_solution(10276668405148362027)
XLA Ops:
  0.0 2.0 %spectra.1 = (bf16[256,128]{1,0:T(8,128)(2,1)S(1)}, bf16[320,128]{1,0:T(8,128)(2,1)S(1)}) custom-call(s32[256,8,128]{2,1,0:T(8,128)} %counts_hbm.1, bf16[32,256]{1,0:T(8,128)(2,1)} %bitcast.2, bf16[3,128,128]{2,1,0:T(8,128)(2,1)} %constant.2.clone.tables_hbm), custom_call_target="tpu_custom_call" | custom-call | tf_op jit(solution)/shard_map/spectra/pallas_call | solution.py:255
  2.2 1.2 %collective-permute-done.1 = bf16[320,128]{1,0:T(8,128)(2,1)S(1)} collective-permute-done((bf16[320,128]{1,0:T(8,128)(2,1)S(1)}, bf16[320,128]{1,0:T(8,128)(2,1)S(1)}, u32[]{:S(2)}, u32[]{:S(2)}) %collective-permute-start.1) | collective-permute-done | bytes 81952 | tf_op jit(solution)/shard_map/ppermute | solution.py:279
  3.4 2.0 %collective-permute-start.3 = (bf16[640,128]{1,0:T(8,128)(2,1)S(1)}, bf16[640,128]{1,0:T(8,128)(2,1)S(1)}, u32[]{:S(2)}, u32[]{:S(2)}) collective-permute-start(bf16[640,128]{1,0:T(8,128)(2,1)S(1)} %constant_dynamic-update-slice_fusion.2.refs_1_.refs_3_), channel_id=1, source_target_pairs={{0,1},{1,2},{2,3},{3,4},{4,5},{5,6},{6,7},{7,0},{32,39},{33,32},{3... | collective-permute-start | bytes 491528 | tf_op jit(solution)/shard_map/ppermute | solution.py:283
  5.4 3.3 %collective-permute-start.2 = (bf16[640,128]{1,0:T(8,128)(2,1)S(1)}, bf16[640,128]{1,0:T(8,128)(2,1)S(1)}, u32[]{:S(2)}, u32[]{:S(2)}) collective-permute-start(bf16[640,128]{1,0:T(8,128)(2,1)S(1)} %constant_dynamic-update-slice_fusion.2.refs_1_.refs_3_), channel_id=1, source_target_pairs={{0,2},{1,3},{2,4},{3,5},{4,6},{5,7},{6,0},{7,1},{32,38},{33,39},{3... | collective-permute-start | bytes 491528 | tf_op jit(solution)/shard_map/ppermute | solution.py:283
  8.7 1.3 %collective-permute-start = (bf16[256,128]{1,0:T(8,128)(2,1)S(1)}, bf16[256,128]{1,0:T(8,128)(2,1)S(1)}, u32[]{:S(2)}, u32[]{:S(2)}) collective-permute-start(bf16[256,128]{1,0:T(8,128)(2,1)S(1)} %get-tuple-element.20), channel_id=1, source_target_pairs={{0,64},{64,0},{1,65},{65,1},{2,66},{66,2},{3,67},{67,3},{4,68},{68... | collective-permute-start | bytes 196616 | tf_op jit(solution)/shard_map/ppermute | solution.py:279
  10.0 2.7 %collective-permute-done.3.refs_2_ = bf16[640,128]{1,0:T(8,128)(2,1)S(1)} collective-permute-done((bf16[640,128]{1,0:T(8,128)(2,1)S(1)}, bf16[640,128]{1,0:T(8,128)(2,1)S(1)}, u32[]{:S(2)}, u32[]{:S(2)}) %collective-permute-start.3) | collective-permute-done | bytes 163872 | tf_op jit(solution)/shard_map/ppermute | solution.py:283
  12.7 3.7 %collective-permute-done.2.refs_1_ = bf16[640,128]{1,0:T(8,128)(2,1)S(1)} collective-permute-done((bf16[640,128]{1,0:T(8,128)(2,1)S(1)}, bf16[640,128]{1,0:T(8,128)(2,1)S(1)}, u32[]{:S(2)}, u32[]{:S(2)}) %collective-permute-start.2) | collective-permute-done | bytes 163872 | tf_op jit(solution)/shard_map/ppermute | solution.py:283
  17.0 3.1 %collective-permute-start.7 = (bf16[512,128]{1,0:T(8,128)(2,1)S(1)}, bf16[512,128]{1,0:T(8,128)(2,1)S(1)}, u32[]{:S(2)}, u32[]{:S(2)}) collective-permute-start(bf16[512,128]{1,0:T(8,128)(2,1)S(1)} %constant_dynamic-update-slice_fusion.refs_0_), channel_id=1, source_target_pairs={{16,0},{24,8},{0,16},{8,24},{17,1},{25,9},{1,17},{9,25},{18,2},{26... | collective-permute-start | bytes 393224 | tf_op jit(solution)/shard_map/ppermute | solution.py:273
  20.1 1.1 %collective-permute-start.8 = (bf16[512,128]{1,0:T(8,128)(2,1)S(1)}, bf16[512,128]{1,0:T(8,128)(2,1)S(1)}, u32[]{:S(2)}, u32[]{:S(2)}) collective-permute-start(bf16[512,128]{1,0:T(8,128)(2,1)S(1)} %constant_dynamic-update-slice_fusion.refs_0_), channel_id=1, source_target_pairs={{8,0},{16,8},{24,16},{0,24},{9,1},{17,9},{25,17},{1,25},{10,2},{18... | collective-permute-start | bytes 393224 | tf_op jit(solution)/shard_map/ppermute | solution.py:273
  22.2 1.3 %collective-permute-start.4 = (bf16[1280,128]{1,0:T(8,128)(2,1)S(1)}, bf16[1280,128]{1,0:T(8,128)(2,1)S(1)}, u32[]{:S(2)}, u32[]{:S(2)}) collective-permute-start(bf16[1280,128]{1,0:T(8,128)(2,1)S(1)} %constant_dynamic-update-slice_fusion.4.refs_4_), channel_id=1, source_target_pairs={{0,32},{32,0},{1,33},{33,1},{2,34},{34,2},{3,35},{35,3},{4,36},{36... | collective-permute-start | bytes 983048 | tf_op jit(solution)/shard_map/ppermute | solution.py:279
  23.5 1.5 %collective-permute-done.5.refs_3_ = bf16[960,128]{1,0:T(8,128)(2,1)S(1)} collective-permute-done((bf16[960,128]{1,0:T(8,128)(2,1)S(1)}, bf16[960,128]{1,0:T(8,128)(2,1)S(1)}, u32[]{:S(2)}, u32[]{:S(2)}) %collective-permute-start.5) | collective-permute-done | bytes 245792 | tf_op jit(solution)/shard_map/ppermute | solution.py:283
  25.0 1.7 %collective-permute-done.8.refs_0_ = bf16[512,128]{1,0:T(8,128)(2,1)S(1)} collective-permute-done((bf16[512,128]{1,0:T(8,128)(2,1)S(1)}, bf16[512,128]{1,0:T(8,128)(2,1)S(1)}, u32[]{:S(2)}, u32[]{:S(2)}) %collective-permute-start.8) | collective-permute-done | bytes 131104 | tf_op jit(solution)/shard_map/ppermute | solution.py:273
  26.7 1.5 %collective-permute-done.9.refs_2_.refs_1_ = bf16[512,128]{1,0:T(8,128)(2,1)S(1)} collective-permute-done((bf16[512,128]{1,0:T(8,128)(2,1)S(1)}, bf16[512,128]{1,0:T(8,128)(2,1)S(1)}, u32[]{:S(2)}, u32[]{:S(2)}) %collective-permute-start.9) | collective-permute-done | bytes 131104 | tf_op jit(solution)/shard_map/ppermute | solution.py:273
  28.2 3.7 %shard_map.39 = (f32[32,512]{1,0:T(8,128)S(1)}, f32[32,512]{1,0:T(8,128)S(1)}, f32[32,512]{1,0:T(8,128)S(1)}) custom-call(bf16[512,128]{1,0:T(8,128)(2,1)S(1)} %collective-permute-done.8.refs_0_, bf16[512,128]{1,0:T(8,128)(2,1)S(1)} %collective-permute-done.7.refs_1_.refs_0_, bf16[512,128]{1,0:T(8,128)(2,1)S(1)} %collective-permute-done.9.refs_2_.refs_1_, ...), custom_call_target="tpu_custom_call" | custom-call | flops 1811939328 | bytes 884736 | tf_op jit(solution)/shard_map/pallas_call | solution.py:133
  33.0 2.5 %shard_map.40 = (f32[32,512]{1,0:T(8,128)S(1)}, f32[32,512]{1,0:T(8,128)S(1)}, f32[32,512]{1,0:T(8,128)S(1)}) custom-call(bf16[512,128]{1,0:T(8,128)(2,1)S(1)} %collective-permute-done.8.refs_0_, bf16[512,128]{1,0:T(8,128)(2,1)S(1)} %collective-permute-done.7.refs_1_.refs_0_, bf16[512,128]{1,0:T(8,128)(2,1)S(1)} %collective-permute-done.9.refs_2_.refs_1_, ...), custom_call_target="tpu_custom_call" | custom-call | flops 1207959552 | bytes 720896 | tf_op jit(solution)/shard_map/pallas_call | solution.py:133
  35.5 1.9 %shard_map.41 = (f32[32,512]{1,0:T(8,128)S(1)}, f32[32,512]{1,0:T(8,128)S(1)}, f32[32,512]{1,0:T(8,128)S(1)}) custom-call(bf16[512,128]{1,0:T(8,128)(2,1)S(1)} %collective-permute-done.8.refs_0_, bf16[512,128]{1,0:T(8,128)(2,1)S(1)} %collective-permute-done.7.refs_1_.refs_0_, bf16[512,128]{1,0:T(8,128)(2,1)S(1)} %collective-permute-done.9.refs_2_.refs_1_, ...), custom_call_target="tpu_custom_call" | custom-call | flops 905969664 | bytes 638976 | tf_op jit(solution)/shard_map/pallas_call | solution.py:133
  38.2 2.5 %collective-permute-start.10 = (f32[32,512]{1,0:T(8,128)S(1)}, f32[32,512]{1,0:T(8,128)S(1)}, u32[]{:S(2)}, u32[]{:S(2)}) collective-permute-start(f32[32,512]{1,0:T(8,128)S(1)} %shard_map.42), channel_id=1, source_target_pairs={{0,16},{8,24},{16,0},{24,8},{1,17},{9,25},{17,1},{25,9},{2,18},{10... | collective-permute-start | bytes 196616 | tf_op jit(solution)/shard_map/ppermute | solution.py:276
  40.8 1.4 %shard_map.43 = (f32[32,512]{1,0:T(8,128)S(1)}, f32[32,512]{1,0:T(8,128)S(1)}) custom-call(bf16[512,128]{1,0:T(8,128)(2,1)S(1)} %collective-permute-done.8.refs_0_, bf16[512,128]{1,0:T(8,128)(2,1)S(1)} %collective-permute-done.9.refs_2_.refs_1_, bf16[960,128]{1,0:T(8,128)(2,1)S(1)} %collective-permute-done.6.refs_4_.refs_1_.refs_2_, ...), custom_call_target="tpu_custom_call" | custom-call | flops 603979776 | bytes 507904 | tf_op jit(solution)/shard_map/pallas_call | solution.py:133
  42.7 2.8 %collective-permute-start.12 = (f32[32,512]{1,0:T(8,128)S(1)}, f32[32,512]{1,0:T(8,128)S(1)}, u32[]{:S(2)}, u32[]{:S(2)}) collective-permute-start(f32[32,512]{1,0:T(8,128)S(1)} %get-tuple-element.32), channel_id=1, source_target_pairs={{0,24},{8,0},{16,8},{24,16},{1,25},{9,1},{17,9},{25,17},{2,26},{10... | collective-permute-start | bytes 196616 | tf_op jit(solution)/shard_map/ppermute | solution.py:276
  45.5 2.7 %shard_map.38.refs_0_ = f32[32,512]{1,0:T(8,128)S(1)} custom-call(bf16[512,128]{1,0:T(8,128)(2,1)S(1)} %constant_dynamic-update-slice_fusion.refs_0_, bf16[640,128]{1,0:T(8,128)(2,1)S(1)} %collective-permute-done.2.refs_1_, bf16[1280,128]{1,0:T(8,128)(2,1)S(1)} %collective-permute-done.4.refs_2_.refs_3_, ...), custom_call_target="tpu_custom_call" | custom-call | flops 1207959552 | bytes 1114112 | tf_op jit(solution)/shard_map/pallas_call | solution.py:133
  48.3 1.4 %collective-permute-start.13 = (f32[32,512]{1,0:T(8,128)S(1)}, f32[32,512]{1,0:T(8,128)S(1)}, u32[]{:S(2)}, u32[]{:S(2)}) collective-permute-start(f32[32,512]{1,0:T(8,128)S(1)} %add.1.mine), channel_id=1, source_target_pairs={{0,64},{32,96},{64,0},{96,32},{1,65},{33,97},{65,1},{97,33},{2,66}... | collective-permute-start | bytes 196616 | tf_op jit(solution)/shard_map/ppermute | solution.py:305
  50.5 2.1 %collective-permute-done.13.by_y = f32[32,512]{1,0:T(8,128)S(1)} collective-permute-done((f32[32,512]{1,0:T(8,128)S(1)}, f32[32,512]{1,0:T(8,128)S(1)}, u32[]{:S(2)}, u32[]{:S(2)}) %collective-permute-start.13) | collective-permute-done | bytes 65568 | tf_op jit(solution)/shard_map/ppermute | solution.py:305
  53.7 18.2 %all_to_all.5.grams = f32[32,8,128]{2,1,0:T(8,128)S(1)} all-to-all(f32[32,8,128]{2,1,0:T(8,128)S(1)} %get-tuple-element.33), channel_id=1, replica_groups=mesh['freq'=2,'y'=2,'c'=2,'x'=4,'z'=8] {'x','z'}, dimensions={0} | all-to-all | bytes 262144 | tf_op jit(solution)/shard_map/all_to_all | solution.py:307
  71.9 2.1 %modes.1 = f32[32,256]{1,0:T(8,128)} custom-call(f32[32,8,128]{2,1,0:T(8,128)S(1)} %all_to_all.5.grams, f32[32,256]{1,0:T(8,128)S(1)} %get-tuple-element.34.image_ref), custom_call_target="tpu_custom_call" | custom-call | tf_op jit(solution)/shard_map/modes/pallas_call | solution.py:243
  (27 shorter events, 5.8 us)
Async XLA Ops:
  2.1 1.4 %collective-permute-start.1 = (bf16[320,128]{1,0:T(8,128)(2,1)S(1)}, bf16[320,128]{1,0:T(8,128)(2,1)S(1)}, u32[]{:S(2)}, u32[]{:S(2)}) collective-permute-start(bf16[320,128]{1,0:T(8,128)(2,1)S(1)} %get-tuple-element.21), channel_id=1, source_target_pairs={{0,32},{32,0},{1,33},{33,1},{2,34},{34,2},{3,35},{35,3},{4,36},{36... | collective-permute-start | bytes 245768 | tf_op jit(solution)/shard_map/ppermute | solution.py:279
  3.4 9.2 %collective-permute-start.3 = (bf16[640,128]{1,0:T(8,128)(2,1)S(1)}, bf16[640,128]{1,0:T(8,128)(2,1)S(1)}, u32[]{:S(2)}, u32[]{:S(2)}) collective-permute-start(bf16[640,128]{1,0:T(8,128)(2,1)S(1)} %constant_dynamic-update-slice_fusion.2.refs_1_.refs_3_), channel_id=1, source_target_pairs={{0,1},{1,2},{2,3},{3,4},{4,5},{5,6},{6,7},{7,0},{32,39},{33,32},{3... | collective-permute-start | bytes 491528 | tf_op jit(solution)/shard_map/ppermute | solution.py:283
  5.4 11.0 %collective-permute-start.2 = (bf16[640,128]{1,0:T(8,128)(2,1)S(1)}, bf16[640,128]{1,0:T(8,128)(2,1)S(1)}, u32[]{:S(2)}, u32[]{:S(2)}) collective-permute-start(bf16[640,128]{1,0:T(8,128)(2,1)S(1)} %constant_dynamic-update-slice_fusion.2.refs_1_.refs_3_), channel_id=1, source_target_pairs={{0,2},{1,3},{2,4},{3,5},{4,6},{5,7},{6,0},{7,1},{32,38},{33,39},{3... | collective-permute-start | bytes 491528 | tf_op jit(solution)/shard_map/ppermute | solution.py:283
  8.7 8.3 %collective-permute-start = (bf16[256,128]{1,0:T(8,128)(2,1)S(1)}, bf16[256,128]{1,0:T(8,128)(2,1)S(1)}, u32[]{:S(2)}, u32[]{:S(2)}) collective-permute-start(bf16[256,128]{1,0:T(8,128)(2,1)S(1)} %get-tuple-element.20), channel_id=1, source_target_pairs={{0,64},{64,0},{1,65},{65,1},{2,66},{66,2},{3,67},{67,3},{4,68},{68... | collective-permute-start | bytes 196616 | tf_op jit(solution)/shard_map/ppermute | solution.py:279
  16.5 8.5 %collective-permute-start.5 = (bf16[960,128]{1,0:T(8,128)(2,1)S(1)}, bf16[960,128]{1,0:T(8,128)(2,1)S(1)}, u32[]{:S(2)}, u32[]{:S(2)}) collective-permute-start(bf16[960,128]{1,0:T(8,128)(2,1)S(1)} %slice.4), channel_id=1, source_target_pairs={{0,2},{1,3},{2,4},{3,5},{4,6},{5,7},{6,0},{7,1},{32,38},{33,39},{3... | collective-permute-start | bytes 737288 | tf_op jit(solution)/shard_map/ppermute | solution.py:283
  17.0 7.9 %collective-permute-start.7 = (bf16[512,128]{1,0:T(8,128)(2,1)S(1)}, bf16[512,128]{1,0:T(8,128)(2,1)S(1)}, u32[]{:S(2)}, u32[]{:S(2)}) collective-permute-start(bf16[512,128]{1,0:T(8,128)(2,1)S(1)} %constant_dynamic-update-slice_fusion.refs_0_), channel_id=1, source_target_pairs={{16,0},{24,8},{0,16},{8,24},{17,1},{25,9},{1,17},{9,25},{18,2},{26... | collective-permute-start | bytes 393224 | tf_op jit(solution)/shard_map/ppermute | solution.py:273
  20.1 6.6 %collective-permute-start.8 = (bf16[512,128]{1,0:T(8,128)(2,1)S(1)}, bf16[512,128]{1,0:T(8,128)(2,1)S(1)}, u32[]{:S(2)}, u32[]{:S(2)}) collective-permute-start(bf16[512,128]{1,0:T(8,128)(2,1)S(1)} %constant_dynamic-update-slice_fusion.refs_0_), channel_id=1, source_target_pairs={{8,0},{16,8},{24,16},{0,24},{9,1},{17,9},{25,17},{1,25},{10,2},{18... | collective-permute-start | bytes 393224 | tf_op jit(solution)/shard_map/ppermute | solution.py:273
  21.3 7.0 %collective-permute-start.9 = (bf16[512,128]{1,0:T(8,128)(2,1)S(1)}, bf16[512,128]{1,0:T(8,128)(2,1)S(1)}, u32[]{:S(2)}, u32[]{:S(2)}) collective-permute-start(bf16[512,128]{1,0:T(8,128)(2,1)S(1)} %constant_dynamic-update-slice_fusion.refs_0_), channel_id=1, source_target_pairs={{24,0},{0,8},{8,16},{16,24},{25,1},{1,9},{9,17},{17,25},{26,2},{2,... | collective-permute-start | bytes 393224 | tf_op jit(solution)/shard_map/ppermute | solution.py:273
  22.2 10.8 %collective-permute-start.4 = (bf16[1280,128]{1,0:T(8,128)(2,1)S(1)}, bf16[1280,128]{1,0:T(8,128)(2,1)S(1)}, u32[]{:S(2)}, u32[]{:S(2)}) collective-permute-start(bf16[1280,128]{1,0:T(8,128)(2,1)S(1)} %constant_dynamic-update-slice_fusion.4.refs_4_), channel_id=1, source_target_pairs={{0,32},{32,0},{1,33},{33,1},{2,34},{34,2},{3,35},{35,3},{4,36},{36... | collective-permute-start | bytes 983048 | tf_op jit(solution)/shard_map/ppermute | solution.py:279
  25.0 12.5 %collective-permute-start.6 = (bf16[960,128]{1,0:T(8,128)(2,1)S(1)}, bf16[960,128]{1,0:T(8,128)(2,1)S(1)}, u32[]{:S(2)}, u32[]{:S(2)}) collective-permute-start(bf16[960,128]{1,0:T(8,128)(2,1)S(1)} %collective-permute-done.5.refs_3_), channel_id=1, source_target_pairs={{0,32},{32,0},{1,33},{33,1},{2,34},{34,2},{3,35},{35,3},{4,36},{36... | collective-permute-start | bytes 737288 | tf_op jit(solution)/shard_map/ppermute | solution.py:279
  38.2 10.0 %collective-permute-start.10 = (f32[32,512]{1,0:T(8,128)S(1)}, f32[32,512]{1,0:T(8,128)S(1)}, u32[]{:S(2)}, u32[]{:S(2)}) collective-permute-start(f32[32,512]{1,0:T(8,128)S(1)} %shard_map.42), channel_id=1, source_target_pairs={{0,16},{8,24},{16,0},{24,8},{1,17},{9,25},{17,1},{25,9},{2,18},{10... | collective-permute-start | bytes 196616 | tf_op jit(solution)/shard_map/ppermute | solution.py:276
  42.2 6.0 %collective-permute-start.11 = (f32[32,512]{1,0:T(8,128)S(1)}, f32[32,512]{1,0:T(8,128)S(1)}, u32[]{:S(2)}, u32[]{:S(2)}) collective-permute-start(f32[32,512]{1,0:T(8,128)S(1)} %get-tuple-element.31), channel_id=1, source_target_pairs={{0,8},{8,16},{16,24},{24,0},{1,9},{9,17},{17,25},{25,1},{2,10},{10... | collective-permute-start | bytes 196616 | tf_op jit(solution)/shard_map/ppermute | solution.py:276
  42.7 5.5 %collective-permute-start.12 = (f32[32,512]{1,0:T(8,128)S(1)}, f32[32,512]{1,0:T(8,128)S(1)}, u32[]{:S(2)}, u32[]{:S(2)}) collective-permute-start(f32[32,512]{1,0:T(8,128)S(1)} %get-tuple-element.32), channel_id=1, source_target_pairs={{0,24},{8,0},{16,8},{24,16},{1,25},{9,1},{17,9},{25,17},{2,26},{10... | collective-permute-start | bytes 196616 | tf_op jit(solution)/shard_map/ppermute | solution.py:276
  48.3 4.4 %collective-permute-start.13 = (f32[32,512]{1,0:T(8,128)S(1)}, f32[32,512]{1,0:T(8,128)S(1)}, u32[]{:S(2)}, u32[]{:S(2)}) collective-permute-start(f32[32,512]{1,0:T(8,128)S(1)} %add.1.mine), channel_id=1, source_target_pairs={{0,64},{32,96},{64,0},{96,32},{1,65},{33,97},{65,1},{97,33},{2,66}... | collective-permute-start | bytes 196616 | tf_op jit(solution)/shard_map/ppermute | solution.py:305
  49.6 3.0 %collective-permute-start.14 = (f32[32,512]{1,0:T(8,128)S(1)}, f32[32,512]{1,0:T(8,128)S(1)}, u32[]{:S(2)}, u32[]{:S(2)}) collective-permute-start(f32[32,512]{1,0:T(8,128)S(1)} %add.1.mine), channel_id=1, source_target_pairs={{0,32},{32,0},{64,96},{96,64},{1,33},{33,1},{65,97},{97,65},{2,34}... | collective-permute-start | bytes 196616 | tf_op jit(solution)/shard_map/ppermute | solution.py:305
  49.6 3.7 %collective-permute-start.15 = (f32[32,512]{1,0:T(8,128)S(1)}, f32[32,512]{1,0:T(8,128)S(1)}, u32[]{:S(2)}, u32[]{:S(2)}) collective-permute-start(f32[32,512]{1,0:T(8,128)S(1)} %add.1.mine), channel_id=1, source_target_pairs={{0,96},{32,64},{64,32},{96,0},{1,97},{33,65},{65,33},{97,1},{2,98}... | collective-permute-start | bytes 196616 | tf_op jit(solution)/shard_map/ppermute | solution.py:305

commit v6 on v4

--- a/solution.py
+++ b/solution.py
@@ -287,18 +287,19 @@
     one = both_ways(pair, 1)
     two = both_ways(pair, 2)
     rows = [first] + [from_x(first, k) for k in range(1, nx)]
-    ahead = jnp.concatenate([one, two], axis=0)
-    far = both_ways(ahead[: 3 * w.shape[0]], 2)
-    ahead_c = swap(ahead, "c")
-    far_c = swap(far, "c")
+    three = both_ways(one, 2)
+    four = both_ways(two[: w.shape[0]], 2)
+    ahead_c = swap(jnp.concatenate([one, two], axis=0), "c")
+    three_c = swap(three, "c")
+    four_c = swap(four, "c")
     home, rest = rows[:1], rows[1:]
     near = image(home, [pair, one], shard)
-    away = image(rest, [pair, ahead], shard)
+    away = image(rest, [pair, one, two], shard)
     away = image(rest, [ahead_c], shard, away)
-    away = image(rest, [far], shard, away)
-    away = image(rest, [far_c], shard, away)
+    away = image(rest, [three, three_c], shard, away)
+    away = image(rest, [four, four_c], shard, away)
     back = [to_x(away[k - 1], k) for k in (2, 1, 3)]
-    near = image(home, [two, ahead_c, far, far_c], shard, near)
+    near = image(home, [two, ahead_c, three, three_c, four, four_c], shard, near)
     mine = add([*near, *back])
     quad = ("y", "c")
     others = [lax.ppermute(mine, quad, [(i, i ^ k) for i in range(4)]) for k in (2, 1, 3)]

time: 73.9 us -> 74.1 us (level)
  waiting for transfers between devices: 18.4 us -> 9.95 us
  starting transfers between devices: 19.3 us -> 26.1 us
  blocking collectives: 17.6 us -> 19.5 us
    ppermute x3, waiting for transfers between devices: 5.53 us -> 0.01 us  [from_x(): return lax.ppermute(v, 'x', [((i + k) % nx, i) for i in range(nx)])]
    ppermute x3 -> x4, starting transfers between devices: 5.79 us -> 10.1 us  [both_ways(): return lax.ppermute(v, ('c', 'z'), pairs)]
    ppermute x3 -> x4, waiting for transfers between devices: 8.51 us -> 5.64 us  [both_ways(): return lax.ppermute(v, ('c', 'z'), pairs)]
    ppermute x3, starting transfers between devices: 4.11 us -> 6.37 us  [to_x(): return lax.ppermute(v, 'x', [(i, (i + k) % nx) for i in range(nx)])]
    all_to_all x1, blocking collectives: 17.6 us -> 19.5 us  [local(): grams = lax.all_to_all(grams, ('x', 'z'), 0, 0)]
    ppermute x4 -> x5, starting transfers between devices: 2.69 us -> 2.87 us  [swap(): return lax.ppermute(v, axis, [(0, 1), (1, 0)])]
  transfers between devices with their start and end apart: 16 -> 18, of which waited for: 9 -> 5; matrix products, arithmetic and copies ran while one was open for 0% -> 0% of each run, Pallas kernels for 16% -> 17%
where the time goes in v6:
time: 74.1 us; the launch traced here: 74 us
  starting transfers between devices  26.1 us (35%)
  blocking collectives  19.5 us (26%)
  Pallas kernels  18.3 us (25%)
  waiting for transfers between devices  9.95 us (13%)
    all_to_all x1, blocking collectives, local(): grams = lax.all_to_all(grams, ('x', 'z'), 0, 0)  19.5 us
    pallas_call x6, Pallas kernels, image(): pl.pallas_call(functools.partial(image_kernel, shard, len(rows), len(pane...  13.8 us
    ppermute x4, starting transfers between devices, both_ways(): return lax.ppermute(v, ('c', 'z'), pairs)  10.1 us
    ppermute x3, starting transfers between devices, to_x(): return lax.ppermute(v, 'x', [(i, (i + k) % nx) for i in range(nx)])  6.37 us
    ppermute x4, waiting for transfers between devices, both_ways(): return lax.ppermute(v, ('c', 'z'), pairs)  5.64 us
    ppermute x3, starting transfers between devices, from_x(): return lax.ppermute(v, 'x', [((i + k) % nx, i) for i in range(nx)])  4.52 us
    ppermute x3, waiting for transfers between devices, local(): lax.ppermute(mine, quad, [(i, i ^ k) for i in range(4)])  2.99 us
    ppermute x5, starting transfers between devices, swap(): return lax.ppermute(v, axis, [(0, 1), (1, 0)])  2.87 us
  transfers between devices with their start and end apart: 18, of which 5 were waited for; matrix products, arithmetic and copies ran while one was open for 0% of the time, Pallas kernels for 17%

profile of v6, /device:TPU:16, one launch (start us, length us, event | category | flops | bytes accessed | tf_op | source)
XLA Modules:
  0.0 74.0 jit_solution(17920269365028665298)
XLA Ops:
  0.0 2.0 %spectra.1 = (bf16[256,128]{1,0:T(8,128)(2,1)S(1)}, bf16[320,128]{1,0:T(8,128)(2,1)S(1)}) custom-call(s32[256,8,128]{2,1,0:T(8,128)} %counts_hbm.1, bf16[32,256]{1,0:T(8,128)(2,1)} %bitcast.2, bf16[3,128,128]{2,1,0:T(8,128)(2,1)} %constant.2.clone.tables_hbm), custom_call_target="tpu_custom_call" | custom-call | tf_op jit(solution)/shard_map/spectra/pallas_call | solution.py:255
  2.1 1.4 %collective-permute-start = (bf16[256,128]{1,0:T(8,128)(2,1)S(1)}, bf16[256,128]{1,0:T(8,128)(2,1)S(1)}, u32[]{:S(2)}, u32[]{:S(2)}) collective-permute-start(bf16[256,128]{1,0:T(8,128)(2,1)S(1)} %get-tuple-element.21), channel_id=1, source_target_pairs={{0,64},{64,0},{1,65},{65,1},{2,66},{66,2},{3,67},{67,3},{4,68},{68... | collective-permute-start | bytes 196616 | tf_op jit(solution)/shard_map/ppermute | solution.py:279
  3.4 1.3 %collective-permute-done.1 = bf16[320,128]{1,0:T(8,128)(2,1)S(1)} collective-permute-done((bf16[320,128]{1,0:T(8,128)(2,1)S(1)}, bf16[320,128]{1,0:T(8,128)(2,1)S(1)}, u32[]{:S(2)}, u32[]{:S(2)}) %collective-permute-start.1) | collective-permute-done | bytes 81952 | tf_op jit(solution)/shard_map/ppermute | solution.py:279
  4.7 3.3 %collective-permute-start.2 = (bf16[640,128]{1,0:T(8,128)(2,1)S(1)}, bf16[640,128]{1,0:T(8,128)(2,1)S(1)}, u32[]{:S(2)}, u32[]{:S(2)}) collective-permute-start(bf16[640,128]{1,0:T(8,128)(2,1)S(1)} %constant_dynamic-update-slice_fusion.2.refs_1_.refs_3_), channel_id=1, source_target_pairs={{0,2},{1,3},{2,4},{3,5},{4,6},{5,7},{6,0},{7,1},{32,38},{33,39},{3... | collective-permute-start | bytes 491528 | tf_op jit(solution)/shard_map/ppermute | solution.py:283
  8.1 1.9 %collective-permute-start.3 = (bf16[640,128]{1,0:T(8,128)(2,1)S(1)}, bf16[640,128]{1,0:T(8,128)(2,1)S(1)}, u32[]{:S(2)}, u32[]{:S(2)}) collective-permute-start(bf16[640,128]{1,0:T(8,128)(2,1)S(1)} %constant_dynamic-update-slice_fusion.2.refs_1_.refs_3_), channel_id=1, source_target_pairs={{0,1},{1,2},{2,3},{3,4},{4,5},{5,6},{6,7},{7,0},{32,39},{33,32},{3... | collective-permute-start | bytes 491528 | tf_op jit(solution)/shard_map/ppermute | solution.py:283
  10.0 2.8 %collective-permute-start.9 = (bf16[512,128]{1,0:T(8,128)(2,1)S(1)}, bf16[512,128]{1,0:T(8,128)(2,1)S(1)}, u32[]{:S(2)}, u32[]{:S(2)}) collective-permute-start(bf16[512,128]{1,0:T(8,128)(2,1)S(1)} %constant_dynamic-update-slice_fusion.refs_0_), channel_id=1, source_target_pairs={{8,0},{16,8},{24,16},{0,24},{9,1},{17,9},{25,17},{1,25},{10,2},{18... | collective-permute-start | bytes 393224 | tf_op jit(solution)/shard_map/ppermute | solution.py:273
  13.6 0.9 %collective-permute-start.11 = (bf16[512,128]{1,0:T(8,128)(2,1)S(1)}, bf16[512,128]{1,0:T(8,128)(2,1)S(1)}, u32[]{:S(2)}, u32[]{:S(2)}) collective-permute-start(bf16[512,128]{1,0:T(8,128)(2,1)S(1)} %constant_dynamic-update-slice_fusion.refs_0_), channel_id=1, source_target_pairs={{24,0},{0,8},{8,16},{16,24},{25,1},{1,9},{9,17},{17,25},{26,2},{2,... | collective-permute-start | bytes 393224 | tf_op jit(solution)/shard_map/ppermute | solution.py:273
  14.5 2.9 %collective-permute-done.3.refs_2_.refs_4_ = bf16[640,128]{1,0:T(8,128)(2,1)S(1)} collective-permute-done((bf16[640,128]{1,0:T(8,128)(2,1)S(1)}, bf16[640,128]{1,0:T(8,128)(2,1)S(1)}, u32[]{:S(2)}, u32[]{:S(2)}) %collective-permute-start.3) | collective-permute-done | bytes 163872 | tf_op jit(solution)/shard_map/ppermute | solution.py:283
  17.5 1.1 %collective-permute-start.5 = (bf16[640,128]{1,0:T(8,128)(2,1)S(1)}, bf16[640,128]{1,0:T(8,128)(2,1)S(1)}, u32[]{:S(2)}, u32[]{:S(2)}) collective-permute-start(bf16[640,128]{1,0:T(8,128)(2,1)S(1)} %collective-permute-done.3.refs_2_.refs_4_), channel_id=1, source_target_pairs={{0,2},{1,3},{2,4},{3,5},{4,6},{5,7},{6,0},{7,1},{32,38},{33,39},{3... | collective-permute-start | bytes 491528 | tf_op jit(solution)/shard_map/ppermute | solution.py:283
  18.6 0.9 %collective-permute-start.4 = (bf16[1280,128]{1,0:T(8,128)(2,1)S(1)}, bf16[1280,128]{1,0:T(8,128)(2,1)S(1)}, u32[]{:S(2)}, u32[]{:S(2)}) collective-permute-start(bf16[1280,128]{1,0:T(8,128)(2,1)S(1)} %pad_maximum_fusion), channel_id=1, source_target_pairs={{0,32},{32,0},{1,33},{33,1},{2,34},{34,2},{3,35},{35,3},{4,36},{36... | collective-permute-start | bytes 983048 | tf_op jit(solution)/shard_map/ppermute | solution.py:279
  19.6 3.7 %collective-permute-start.7 = (bf16[320,128]{1,0:T(8,128)(2,1)S(1)}, bf16[320,128]{1,0:T(8,128)(2,1)S(1)}, u32[]{:S(2)}, u32[]{:S(2)}) collective-permute-start(bf16[320,128]{1,0:T(8,128)(2,1)S(1)} %slice.4), channel_id=1, source_target_pairs={{0,2},{1,3},{2,4},{3,5},{4,6},{5,7},{6,0},{7,1},{32,38},{33,39},{3... | collective-permute-start | bytes 245768 | tf_op jit(solution)/shard_map/ppermute | solution.py:283
  23.3 2.7 %collective-permute-done.5.refs_3_ = bf16[640,128]{1,0:T(8,128)(2,1)S(1)} collective-permute-done((bf16[640,128]{1,0:T(8,128)(2,1)S(1)}, bf16[640,128]{1,0:T(8,128)(2,1)S(1)}, u32[]{:S(2)}, u32[]{:S(2)}) %collective-permute-start.5) | collective-permute-done | bytes 163872 | tf_op jit(solution)/shard_map/ppermute | solution.py:283
  26.0 3.7 %shard_map.39 = (f32[32,512]{1,0:T(8,128)S(1)}, f32[32,512]{1,0:T(8,128)S(1)}, f32[32,512]{1,0:T(8,128)S(1)}) custom-call(bf16[512,128]{1,0:T(8,128)(2,1)S(1)} %collective-permute-done.9.refs_0_, bf16[512,128]{1,0:T(8,128)(2,1)S(1)} %collective-permute-done.10.refs_1_, bf16[512,128]{1,0:T(8,128)(2,1)S(1)} %collective-permute-done.11.refs_2_, ...), custom_call_target="tpu_custom_call" | custom-call | flops 1811939328 | bytes 884736 | tf_op jit(solution)/shard_map/pallas_call | solution.py:133
  29.7 1.0 %shard_map.37.refs_7_ = f32[32,512]{1,0:T(8,128)S(1)} custom-call(bf16[512,128]{1,0:T(8,128)(2,1)S(1)} %constant_dynamic-update-slice_fusion.refs_0_, bf16[640,128]{1,0:T(8,128)(2,1)S(1)} %constant_dynamic-update-slice_fusion.2.refs_1_.refs_3_, bf16[640,128]{1,0:T(8,128)(2,1)S(1)} %collective-permute-done.3.refs_2_.refs_4_), custom_call_target="tpu_custom_call" | custom-call | flops 402653184 | bytes 458752 | tf_op jit(solution)/shard_map/pallas_call | solution.py:133
  31.3 2.5 %shard_map.40 = (f32[32,512]{1,0:T(8,128)S(1)}, f32[32,512]{1,0:T(8,128)S(1)}, f32[32,512]{1,0:T(8,128)S(1)}) custom-call(bf16[512,128]{1,0:T(8,128)(2,1)S(1)} %collective-permute-done.9.refs_0_, bf16[512,128]{1,0:T(8,128)(2,1)S(1)} %collective-permute-done.10.refs_1_, bf16[512,128]{1,0:T(8,128)(2,1)S(1)} %collective-permute-done.11.refs_2_, ...), custom_call_target="tpu_custom_call" | custom-call | flops 1207959552 | bytes 720896 | tf_op jit(solution)/shard_map/pallas_call | solution.py:133
  33.8 2.5 %shard_map.41 = (f32[32,512]{1,0:T(8,128)S(1)}, f32[32,512]{1,0:T(8,128)S(1)}, f32[32,512]{1,0:T(8,128)S(1)}) custom-call(bf16[512,128]{1,0:T(8,128)(2,1)S(1)} %collective-permute-done.9.refs_0_, bf16[512,128]{1,0:T(8,128)(2,1)S(1)} %collective-permute-done.10.refs_1_, bf16[512,128]{1,0:T(8,128)(2,1)S(1)} %collective-permute-done.11.refs_2_, ...), custom_call_target="tpu_custom_call" | custom-call | flops 1207959552 | bytes 720896 | tf_op jit(solution)/shard_map/pallas_call | solution.py:133
  36.4 1.3 %shard_map.42 = (f32[32,512]{1,0:T(8,128)S(1)}, f32[32,512]{1,0:T(8,128)S(1)}, f32[32,512]{1,0:T(8,128)S(1)}) custom-call(bf16[512,128]{1,0:T(8,128)(2,1)S(1)} %collective-permute-done.9.refs_0_, bf16[512,128]{1,0:T(8,128)(2,1)S(1)} %collective-permute-done.10.refs_1_, bf16[512,128]{1,0:T(8,128)(2,1)S(1)} %collective-permute-done.11.refs_2_, ...), custom_call_target="tpu_custom_call" | custom-call | flops 603979776 | bytes 557056 | tf_op jit(solution)/shard_map/pallas_call | solution.py:133
  37.7 3.1 %collective-permute-start.12 = (f32[32,512]{1,0:T(8,128)S(1)}, f32[32,512]{1,0:T(8,128)S(1)}, u32[]{:S(2)}, u32[]{:S(2)}) collective-permute-start(f32[32,512]{1,0:T(8,128)S(1)} %get-tuple-element.32), channel_id=1, source_target_pairs={{0,16},{8,24},{16,0},{24,8},{1,17},{9,25},{17,1},{25,9},{2,18},{10... | collective-permute-start | bytes 196616 | tf_op jit(solution)/shard_map/ppermute | solution.py:276
  41.3 2.8 %collective-permute-start.14 = (f32[32,512]{1,0:T(8,128)S(1)}, f32[32,512]{1,0:T(8,128)S(1)}, u32[]{:S(2)}, u32[]{:S(2)}) collective-permute-start(f32[32,512]{1,0:T(8,128)S(1)} %get-tuple-element.34), channel_id=1, source_target_pairs={{0,24},{8,0},{16,8},{24,16},{1,25},{9,1},{17,9},{25,17},{2,26},{10... | collective-permute-start | bytes 196616 | tf_op jit(solution)/shard_map/ppermute | solution.py:276
  44.1 2.7 %shard_map.38.refs_0_ = f32[32,512]{1,0:T(8,128)S(1)} custom-call(bf16[512,128]{1,0:T(8,128)(2,1)S(1)} %constant_dynamic-update-slice_fusion.refs_0_, bf16[640,128]{1,0:T(8,128)(2,1)S(1)} %collective-permute-done.2.refs_1_.refs_5_, bf16[1280,128]{1,0:T(8,128)(2,1)S(1)} %collective-permute-done.4.refs_2_.refs_3_, ...), custom_call_target="tpu_custom_call" | custom-call | flops 1207959552 | bytes 1114112 | tf_op jit(solution)/shard_map/pallas_call | solution.py:133
  47.7 1.4 %collective-permute-start.17 = (f32[32,512]{1,0:T(8,128)S(1)}, f32[32,512]{1,0:T(8,128)S(1)}, u32[]{:S(2)}, u32[]{:S(2)}) collective-permute-start(f32[32,512]{1,0:T(8,128)S(1)} %add.1.mine), channel_id=1, source_target_pairs={{0,96},{32,64},{64,32},{96,0},{1,97},{33,65},{65,33},{97,1},{2,98}... | collective-permute-start | bytes 196616 | tf_op jit(solution)/shard_map/ppermute | solution.py:305
  49.1 2.6 %collective-permute-done.15.by_y = f32[32,512]{1,0:T(8,128)S(1)} collective-permute-done((f32[32,512]{1,0:T(8,128)S(1)}, f32[32,512]{1,0:T(8,128)S(1)}, u32[]{:S(2)}, u32[]{:S(2)}) %collective-permute-start.15) | collective-permute-done | bytes 65568 | tf_op jit(solution)/shard_map/ppermute | solution.py:305
  52.4 19.5 %all_to_all.5.grams = f32[32,8,128]{2,1,0:T(8,128)S(1)} all-to-all(f32[32,8,128]{2,1,0:T(8,128)S(1)} %get-tuple-element.35), channel_id=1, replica_groups=mesh['freq'=2,'y'=2,'c'=2,'x'=4,'z'=8] {'x','z'}, dimensions={0} | all-to-all | bytes 262144 | tf_op jit(solution)/shard_map/all_to_all | solution.py:307
  71.9 2.1 %modes.1 = f32[32,256]{1,0:T(8,128)} custom-call(f32[32,8,128]{2,1,0:T(8,128)S(1)} %all_to_all.5.grams, f32[32,256]{1,0:T(8,128)S(1)} %get-tuple-element.36.image_ref), custom_call_target="tpu_custom_call" | custom-call | tf_op jit(solution)/shard_map/modes/pallas_call | solution.py:243
  (29 shorter events, 3.5 us)
Async XLA Ops:
  2.1 7.9 %collective-permute-start = (bf16[256,128]{1,0:T(8,128)(2,1)S(1)}, bf16[256,128]{1,0:T(8,128)(2,1)S(1)}, u32[]{:S(2)}, u32[]{:S(2)}) collective-permute-start(bf16[256,128]{1,0:T(8,128)(2,1)S(1)} %get-tuple-element.21), channel_id=1, source_target_pairs={{0,64},{64,0},{1,65},{65,1},{2,66},{66,2},{3,67},{67,3},{4,68},{68... | collective-permute-start | bytes 196616 | tf_op jit(solution)/shard_map/ppermute | solution.py:279
  3.4 1.3 %collective-permute-start.1 = (bf16[320,128]{1,0:T(8,128)(2,1)S(1)}, bf16[320,128]{1,0:T(8,128)(2,1)S(1)}, u32[]{:S(2)}, u32[]{:S(2)}) collective-permute-start(bf16[320,128]{1,0:T(8,128)(2,1)S(1)} %get-tuple-element.22), channel_id=1, source_target_pairs={{0,32},{32,0},{1,33},{33,1},{2,34},{34,2},{3,35},{35,3},{4,36},{36... | collective-permute-start | bytes 245768 | tf_op jit(solution)/shard_map/ppermute | solution.py:279
  4.7 13.9 %collective-permute-start.2 = (bf16[640,128]{1,0:T(8,128)(2,1)S(1)}, bf16[640,128]{1,0:T(8,128)(2,1)S(1)}, u32[]{:S(2)}, u32[]{:S(2)}) collective-permute-start(bf16[640,128]{1,0:T(8,128)(2,1)S(1)} %constant_dynamic-update-slice_fusion.2.refs_1_.refs_3_), channel_id=1, source_target_pairs={{0,2},{1,3},{2,4},{3,5},{4,6},{5,7},{6,0},{7,1},{32,38},{33,39},{3... | collective-permute-start | bytes 491528 | tf_op jit(solution)/shard_map/ppermute | solution.py:283
  8.1 9.4 %collective-permute-start.3 = (bf16[640,128]{1,0:T(8,128)(2,1)S(1)}, bf16[640,128]{1,0:T(8,128)(2,1)S(1)}, u32[]{:S(2)}, u32[]{:S(2)}) collective-permute-start(bf16[640,128]{1,0:T(8,128)(2,1)S(1)} %constant_dynamic-update-slice_fusion.2.refs_1_.refs_3_), channel_id=1, source_target_pairs={{0,1},{1,2},{2,3},{3,4},{4,5},{5,6},{6,7},{7,0},{32,39},{33,32},{3... | collective-permute-start | bytes 491528 | tf_op jit(solution)/shard_map/ppermute | solution.py:283
  10.0 9.6 %collective-permute-start.9 = (bf16[512,128]{1,0:T(8,128)(2,1)S(1)}, bf16[512,128]{1,0:T(8,128)(2,1)S(1)}, u32[]{:S(2)}, u32[]{:S(2)}) collective-permute-start(bf16[512,128]{1,0:T(8,128)(2,1)S(1)} %constant_dynamic-update-slice_fusion.refs_0_), channel_id=1, source_target_pairs={{8,0},{16,8},{24,16},{0,24},{9,1},{17,9},{25,17},{1,25},{10,2},{18... | collective-permute-start | bytes 393224 | tf_op jit(solution)/shard_map/ppermute | solution.py:273
  12.8 13.1 %collective-permute-start.10 = (bf16[512,128]{1,0:T(8,128)(2,1)S(1)}, bf16[512,128]{1,0:T(8,128)(2,1)S(1)}, u32[]{:S(2)}, u32[]{:S(2)}) collective-permute-start(bf16[512,128]{1,0:T(8,128)(2,1)S(1)} %constant_dynamic-update-slice_fusion.refs_0_), channel_id=1, source_target_pairs={{16,0},{24,8},{0,16},{8,24},{17,1},{25,9},{1,17},{9,25},{18,2},{26... | collective-permute-start | bytes 393224 | tf_op jit(solution)/shard_map/ppermute | solution.py:273
  13.6 12.4 %collective-permute-start.11 = (bf16[512,128]{1,0:T(8,128)(2,1)S(1)}, bf16[512,128]{1,0:T(8,128)(2,1)S(1)}, u32[]{:S(2)}, u32[]{:S(2)}) collective-permute-start(bf16[512,128]{1,0:T(8,128)(2,1)S(1)} %constant_dynamic-update-slice_fusion.refs_0_), channel_id=1, source_target_pairs={{24,0},{0,8},{8,16},{16,24},{25,1},{1,9},{9,17},{17,25},{26,2},{2,... | collective-permute-start | bytes 393224 | tf_op jit(solution)/shard_map/ppermute | solution.py:273
  17.5 8.5 %collective-permute-start.5 = (bf16[640,128]{1,0:T(8,128)(2,1)S(1)}, bf16[640,128]{1,0:T(8,128)(2,1)S(1)}, u32[]{:S(2)}, u32[]{:S(2)}) collective-permute-start(bf16[640,128]{1,0:T(8,128)(2,1)S(1)} %collective-permute-done.3.refs_2_.refs_4_), channel_id=1, source_target_pairs={{0,2},{1,3},{2,4},{3,5},{4,6},{5,7},{6,0},{7,1},{32,38},{33,39},{3... | collective-permute-start | bytes 491528 | tf_op jit(solution)/shard_map/ppermute | solution.py:283
  18.6 12.7 %collective-permute-start.4 = (bf16[1280,128]{1,0:T(8,128)(2,1)S(1)}, bf16[1280,128]{1,0:T(8,128)(2,1)S(1)}, u32[]{:S(2)}, u32[]{:S(2)}) collective-permute-start(bf16[1280,128]{1,0:T(8,128)(2,1)S(1)} %pad_maximum_fusion), channel_id=1, source_target_pairs={{0,32},{32,0},{1,33},{33,1},{2,34},{34,2},{3,35},{35,3},{4,36},{36... | collective-permute-start | bytes 983048 | tf_op jit(solution)/shard_map/ppermute | solution.py:279
  19.6 11.2 %collective-permute-start.7 = (bf16[320,128]{1,0:T(8,128)(2,1)S(1)}, bf16[320,128]{1,0:T(8,128)(2,1)S(1)}, u32[]{:S(2)}, u32[]{:S(2)}) collective-permute-start(bf16[320,128]{1,0:T(8,128)(2,1)S(1)} %slice.4), channel_id=1, source_target_pairs={{0,2},{1,3},{2,4},{3,5},{4,6},{5,7},{6,0},{7,1},{32,38},{33,39},{3... | collective-permute-start | bytes 245768 | tf_op jit(solution)/shard_map/ppermute | solution.py:283
  26.0 7.8 %collective-permute-start.6 = (bf16[640,128]{1,0:T(8,128)(2,1)S(1)}, bf16[640,128]{1,0:T(8,128)(2,1)S(1)}, u32[]{:S(2)}, u32[]{:S(2)}) collective-permute-start(bf16[640,128]{1,0:T(8,128)(2,1)S(1)} %collective-permute-done.5.refs_3_), channel_id=1, source_target_pairs={{0,32},{32,0},{1,33},{33,1},{2,34},{34,2},{3,35},{35,3},{4,36},{36... | collective-permute-start | bytes 491528 | tf_op jit(solution)/shard_map/ppermute | solution.py:279
  30.7 5.6 %collective-permute-start.8 = (bf16[320,128]{1,0:T(8,128)(2,1)S(1)}, bf16[320,128]{1,0:T(8,128)(2,1)S(1)}, u32[]{:S(2)}, u32[]{:S(2)}) collective-permute-start(bf16[320,128]{1,0:T(8,128)(2,1)S(1)} %collective-permute-done.7.refs_5_.refs_3_), channel_id=1, source_target_pairs={{0,32},{32,0},{1,33},{33,1},{2,34},{34,2},{3,35},{35,3},{4,36},{36... | collective-permute-start | bytes 245768 | tf_op jit(solution)/shard_map/ppermute | solution.py:279
  37.7 9.1 %collective-permute-start.12 = (f32[32,512]{1,0:T(8,128)S(1)}, f32[32,512]{1,0:T(8,128)S(1)}, u32[]{:S(2)}, u32[]{:S(2)}) collective-permute-start(f32[32,512]{1,0:T(8,128)S(1)} %get-tuple-element.32), channel_id=1, source_target_pairs={{0,16},{8,24},{16,0},{24,8},{1,17},{9,25},{17,1},{25,9},{2,18},{10... | collective-permute-start | bytes 196616 | tf_op jit(solution)/shard_map/ppermute | solution.py:276
  40.8 6.0 %collective-permute-start.13 = (f32[32,512]{1,0:T(8,128)S(1)}, f32[32,512]{1,0:T(8,128)S(1)}, u32[]{:S(2)}, u32[]{:S(2)}) collective-permute-start(f32[32,512]{1,0:T(8,128)S(1)} %get-tuple-element.33), channel_id=1, source_target_pairs={{0,8},{8,16},{16,24},{24,0},{1,9},{9,17},{17,25},{25,1},{2,10},{10... | collective-permute-start | bytes 196616 | tf_op jit(solution)/shard_map/ppermute | solution.py:276
  41.3 5.5 %collective-permute-start.14 = (f32[32,512]{1,0:T(8,128)S(1)}, f32[32,512]{1,0:T(8,128)S(1)}, u32[]{:S(2)}, u32[]{:S(2)}) collective-permute-start(f32[32,512]{1,0:T(8,128)S(1)} %get-tuple-element.34), channel_id=1, source_target_pairs={{0,24},{8,0},{16,8},{24,16},{1,25},{9,1},{17,9},{25,17},{2,26},{10... | collective-permute-start | bytes 196616 | tf_op jit(solution)/shard_map/ppermute | solution.py:276
  46.8 4.9 %collective-permute-start.15 = (f32[32,512]{1,0:T(8,128)S(1)}, f32[32,512]{1,0:T(8,128)S(1)}, u32[]{:S(2)}, u32[]{:S(2)}) collective-permute-start(f32[32,512]{1,0:T(8,128)S(1)} %add.1.mine), channel_id=1, source_target_pairs={{0,64},{32,96},{64,0},{96,32},{1,65},{33,97},{65,1},{97,33},{2,66}... | collective-permute-start | bytes 196616 | tf_op jit(solution)/shard_map/ppermute | solution.py:305
  47.7 4.1 %collective-permute-start.16 = (f32[32,512]{1,0:T(8,128)S(1)}, f32[32,512]{1,0:T(8,128)S(1)}, u32[]{:S(2)}, u32[]{:S(2)}) collective-permute-start(f32[32,512]{1,0:T(8,128)S(1)} %add.1.mine), channel_id=1, source_target_pairs={{0,32},{32,0},{64,96},{96,64},{1,33},{33,1},{65,97},{97,65},{2,34}... | collective-permute-start | bytes 196616 | tf_op jit(solution)/shard_map/ppermute | solution.py:305
  47.7 4.4 %collective-permute-start.17 = (f32[32,512]{1,0:T(8,128)S(1)}, f32[32,512]{1,0:T(8,128)S(1)}, u32[]{:S(2)}, u32[]{:S(2)}) collective-permute-start(f32[32,512]{1,0:T(8,128)S(1)} %add.1.mine), channel_id=1, source_target_pairs={{0,96},{32,64},{64,32},{96,0},{1,97},{33,65},{65,33},{97,1},{2,98}... | collective-permute-start | bytes 196616 | tf_op jit(solution)/shard_map/ppermute | solution.py:305
